TPU v7x, 32 devices: a whole 2x2x4 slice. The times are simulated.
32 devices in a mesh: space: 8 (over y, x, core), frame: 4 (over z).
Axes of the slice: x: 2, y: 2, z: 4, core: 2. Of those that a mesh axis runs over, the one named last changes fastest.
Arguments:
- features: bfloat16 [4, 32, 8, 8, 512], P('frame', 'space'), may hold values from -6 to 6
- occupancy: int32 [4, 32, 512], P('frame', 'space'), may hold values 0 or 1
- w_spatial: bfloat16 [2, 27, 64, 64], replicated, may hold values from -0.21875 to 0.21875
- b_spatial: float32 [2, 64], replicated, may hold values from -3 to 3
- w_temporal: bfloat16 [3, 64, 64], replicated, may hold values from -0.75 to 0.75
- face_send: int32 [4, 16], P('frame', 'space'), may hold values from -1 to 19, as said below
- face_source: int32 [4, 32, 6], P('frame', 'space'), may hold values from -1 to 25, as said below
- send_ahead: int32 [4, 24], P('frame', 'space'), may hold values from 0 to 3, as said below
- from_prior: int32 [4, 32], P('frame', 'space'), may hold values from -1 to 2, as said below
- send_back: int32 [4, 24], P('frame', 'space'), may hold values from 0 to 3, as said below
- from_later: int32 [4, 32], P('frame', 'space'), may hold values from -1 to 2, as said below
Outputs:
- section_out: bfloat16 [4, 32, 8, 8, 512], P('frame', 'space')
Inputs may be any that keep to these rules, and one draw needn't show every extreme that they name: `face_send`: entries 0 to 0 of a device's row are the faces it sends to the device one lower in space, as brick * 6 + 0 of 1 distinct own bricks; entries 1 to 1 those it sends to the device one higher, as brick * 6 + 1 of 1 distinct own bricks; all -1 toward a side where the axis ends. `face_source`: entry (b, f) names an entry of the device's table: k < 1 a face from the device below (only for f = 0), 1 + k one from the device above (only for f = 1), 2 + 6 j + g face g of brick j of the same device, the opposite of f; or -1. Every received face is named exactly once; local pairs are mutual. `send_ahead`: each device's 3 entries are distinct bricks of that device. `from_prior`: -1 for every brick of frame 0; in other frames exactly 3 bricks of each device name a slot, each slot once. `send_back`: each device's 3 entries are distinct bricks of that device. `from_later`: -1 for every brick of the last frame; in other frames exactly 3 bricks of each device name a slot, each slot once.
All inputs are finite; a program needn't handle non-finite values. No bound on the sum of `occupancy` on one device may be relied on, other than what follows from the above.
Results may differ from a plain program's by a relative error of at most 0.0049.
Values may be sent and summed in bfloat16 or wider, within the bound.
No kernel may reach another device: no remote copies, remote signals or barrier semaphores. Data moves between devices by JAX's collectives and lax.ppermute only.
A program may use at most 64 MiB of HBM per device.

v0:
```python
import jax
import jax.numpy as jnp
from jax import lax
from jax.sharding import PartitionSpec as P


def passed_along(x, axis, by):
    length = lax.axis_size(axis)
    pairs = [(i, i + by) for i in range(length) if 0 <= i + by < length]
    return lax.ppermute(x, axis, pairs)


def voxel_mask(occupied, edge_len, channels):
    bricks = occupied.shape[0]
    shaped = occupied.astype(jnp.float32).reshape(bricks, edge_len, edge_len, edge_len, 1)
    return jnp.broadcast_to(shaped, (bricks, edge_len, edge_len, edge_len, channels)).reshape(
        bricks, edge_len, edge_len, edge_len * channels
    )


def face_layers(field_data, edge_len, channels):
    bricks = field_data.shape[0]
    volume = field_data.reshape(bricks, edge_len, edge_len, edge_len, channels)
    planes = [
        volume[:, :, :, 0],
        volume[:, :, :, edge_len - 1],
        volume[:, :, 0],
        volume[:, :, edge_len - 1],
        volume[:, 0],
        volume[:, edge_len - 1],
    ]
    stacked = jnp.stack(
        [single.reshape(bricks, edge_len, edge_len * channels) for single in planes], axis=1
    )
    return stacked.reshape(bricks * 6, edge_len, edge_len * channels)


def padded_block(field_data, rim_faces, edge_len, channels):
    bricks = field_data.shape[0]
    wide_cols = (edge_len + 2) * channels
    inner = slice(1, edge_len + 1)
    middle = slice(channels, (edge_len + 1) * channels)
    padded = jnp.zeros((bricks, edge_len + 2, edge_len + 2, wide_cols), jnp.bfloat16)
    padded = padded.at[:, inner, inner, middle].set(field_data)
    padded = padded.at[:, inner, inner, 0:channels].set(
        rim_faces[:, 0].reshape(bricks, edge_len, edge_len, channels)
    )
    padded = padded.at[:, inner, inner, (edge_len + 1) * channels : wide_cols].set(
        rim_faces[:, 1].reshape(bricks, edge_len, edge_len, channels)
    )
    padded = padded.at[:, inner, 0, middle].set(rim_faces[:, 2])
    padded = padded.at[:, inner, edge_len + 1, middle].set(rim_faces[:, 3])
    padded = padded.at[:, 0, inner, middle].set(rim_faces[:, 4])
    padded = padded.at[:, edge_len + 1, inner, middle].set(rim_faces[:, 5])
    return padded


def conv_layer(padded, weights, bias_row, keep_mask, edge_len, channels, group_size):
    bricks = padded.shape[0]

    def one_group(pieces):
        piece_block, piece_mask = pieces
        shifted = []
        for depth_off in range(3):
            for row_off in range(3):
                for col_off in range(3):
                    shifted.append(
                        piece_block[
                            :,
                            depth_off : depth_off + edge_len,
                            row_off : row_off + edge_len,
                            col_off * channels : col_off * channels + edge_len * channels,
                        ]
                    )
        columns = jnp.stack(shifted, axis=1).reshape(
            group_size, 27, edge_len, edge_len, edge_len, channels
        )
        summed = jnp.einsum(
            "btzyxc,tcd->bzyxd", columns, weights, preferred_element_type=jnp.float32
        )
        summed = summed.reshape(group_size, edge_len, edge_len, edge_len * channels) + jnp.tile(
            bias_row, edge_len
        )
        return (jnp.maximum(summed, 0.0) * piece_mask).astype(jnp.bfloat16)

    grouped = lax.map(
        one_group,
        (
            padded.reshape((bricks // group_size, group_size) + padded.shape[1:]),
            keep_mask.reshape((bricks // group_size, group_size) + keep_mask.shape[1:]),
        ),
    )
    return grouped.reshape(bricks, edge_len, edge_len, edge_len * channels)


def per_device(
    features,
    occupancy,
    w_spatial,
    b_spatial,
    w_temporal,
    face_send,
    face_source,
    send_ahead,
    from_prior,
    send_back,
    from_later,
):
    channels = w_spatial.shape[-1]
    edge_len = features.shape[2]
    bricks = features.shape[1]
    layers = w_spatial.shape[0]
    slab_count = face_send.shape[1] // 2
    keep_mask = voxel_mask(occupancy[0], edge_len, channels)
    inputs = (features[0].astype(jnp.float32) * keep_mask).astype(jnp.bfloat16)
    sources = face_source[0]
    outgoing = face_send[0]
    hidden = inputs
    for layer_index in range(layers):
        face_table = face_layers(hidden, edge_len, channels)
        outbound = jnp.where((outgoing >= 0)[:, None, None], face_table[jnp.clip(outgoing, 0)], 0)
        parcels = outbound.reshape(2, slab_count, edge_len, edge_len * channels)
        below_faces = passed_along(parcels[1], "space", 1)
        above_faces = passed_along(parcels[0], "space", -1)
        arrived = jnp.concatenate([below_faces, above_faces], axis=0)
        table = jnp.concatenate([arrived, face_table], axis=0)
        rim_faces = jnp.where((sources >= 0)[:, :, None, None], table[jnp.clip(sources, 0)], 0)
        padded = padded_block(hidden, rim_faces, edge_len, channels)
        hidden = conv_layer(
            padded, w_spatial[layer_index], b_spatial[layer_index], keep_mask, edge_len, channels, 2
        )
    ahead_rows = hidden[send_ahead[0]]
    prior_rows = passed_along(ahead_rows, "frame", 1)
    back_rows = hidden[send_back[0]]
    later_rows = passed_along(back_rows, "frame", -1)
    prior_slots = from_prior[0]
    later_slots = from_later[0]
    from_before = jnp.where(
        (prior_slots >= 0)[:, None, None, None], prior_rows[jnp.clip(prior_slots, 0)], 0
    )
    from_after = jnp.where(
        (later_slots >= 0)[:, None, None, None], later_rows[jnp.clip(later_slots, 0)], 0
    )
    temporal_sum = jnp.dot(
        from_before.reshape(-1, channels), w_temporal[0], preferred_element_type=jnp.float32
    )
    temporal_sum = temporal_sum + jnp.dot(
        hidden.reshape(-1, channels), w_temporal[1], preferred_element_type=jnp.float32
    )
    temporal_sum = temporal_sum + jnp.dot(
        from_after.reshape(-1, channels), w_temporal[2], preferred_element_type=jnp.float32
    )
    total_sum = inputs.astype(jnp.float32) + temporal_sum.reshape(
        bricks, edge_len, edge_len, edge_len * channels
    )
    return (keep_mask * total_sum).astype(jnp.bfloat16)[None]


def solution(mesh):
    in_specs = (
        P("frame", "space", None, None, None),
        P("frame", "space", None),
        P(),
        P(),
        P(),
        P("frame", "space"),
        P("frame", "space", None),
        P("frame", "space"),
        P("frame", "space"),
        P("frame", "space"),
        P("frame", "space"),
    )
    out_specs = P("frame", "space", None, None, None)
    return jax.shard_map(
        per_device, mesh=mesh, in_specs=in_specs, out_specs=out_specs, check_vma=False
    )
```

profile of v0, /device:TPU:0, one launch (start us, length us, event | category | flops | bytes accessed | tf_op | source)
XLA Modules:
  0.0 295.6 jit_solution(11369679095738194732)
XLA Ops:
  0.9 1.2 reshape.908
  5.8 1.3 collective-permute-start.1
  7.1 3.0 %collective-permute-start = (bf16[1,8,512]{2,1,0:T(8,128)(2,1)S(1)}, bf16[1,8,512]{2,1,0:T(8,128)(2,1)S(1)}, u32[]{:S(2)}, u32[]{:S(2)}) collective-permute-start(bf16[1,8,512]{2,1,0:T(8,128)(2,1)S(1)} %get-tuple-element.345), channel_id=1, source_target_pairs={{0,4},{4,8},{8,12},{12,16},{16,20},{20,24},{24,28},{1,5},{5,9},{9,... | collective-permute-start | bytes 24584 | tf_op jit(solution)/shard_map/ppermute | solution.py:10
  12.2 1.2 compare_bitcast_fusion
  13.4 1.2 maximum_bitcast_fusion.1
  14.6 1.2 compare_bitcast_fusion.3
  16.6 1.2 slice_bitcast_fusion
  18.2 1.4 scatter.46
  20.6 3.5 %scatter.49 = bf16[4,10,10,640]{3,2,1,0:T(8,128)(2,1)} dynamic-update-slice(bf16[4,10,10,640]{3,2,1,0:T(8,128)(2,1)} %scatter.46, bf16[4,8,8,64]{3,2,1,0:T(8,128)(2,1)S(1)} %reshape.893, s32[]{:T(128)} %copy.143, s32[]{:T(128)} %constant.417.clone.1, s32[]{:T(128)} %constant.417.clone.1, s32[]{:T(128)} %copy.143) | dynamic-update-slice | bytes 65540 | tf_op jit(solution)/shard_map/scatter | solution.py:45
  24.2 10.5 %scatter.50 = bf16[4,10,10,640]{3,2,1,0:T(8,128)(2,1)} dynamic-update-slice(bf16[4,10,10,640]{3,2,1,0:T(8,128)(2,1)} %scatter.49, bf16[4,8,8,64]{3,2,1,0:T(8,128)(2,1)S(1)} %reshape.894, s32[]{:T(128)} %copy.143, s32[]{:T(128)} %constant.417.clone.1, s32[]{:T(128)} %constant.417.clone.1, s32[]{:T(128)} %constant.418.clone.1) | dynamic-update-slice | bytes 65540 | tf_op jit(solution)/shard_map/scatter | solution.py:48
  34.7 7.9 %scatter.51 = bf16[4,10,10,640]{3,2,1,0:T(8,128)(2,1)} dynamic-update-slice(bf16[4,10,10,640]{3,2,1,0:T(8,128)(2,1)} %scatter.50, bf16[4,8,1,512]{3,2,1,0:T(2,128)(2,1)S(1)} %copy.25, s32[]{:T(128)} %copy.143, s32[]{:T(128)} %constant.417.clone.1, s32[]{:T(128)} %copy.143, s32[]{:T(128)} %constant.419.clone.1) | dynamic-update-slice | bytes 65540 | tf_op jit(solution)/shard_map/scatter | solution.py:51
  42.5 7.8 %scatter.54 = bf16[4,10,10,640]{3,2,1,0:T(8,128)(2,1)} dynamic-update-slice(bf16[4,10,10,640]{3,2,1,0:T(8,128)(2,1)} %scatter.51, bf16[4,8,1,512]{3,2,1,0:T(2,128)(2,1)S(1)} %copy.26, s32[]{:T(128)} %copy.143, s32[]{:T(128)} %constant.417.clone.1, s32[]{:T(128)} %constant.420.clone.1, s32[]{:T(128)} %constant.419.clone.1) | dynamic-update-slice | bytes 65540 | tf_op jit(solution)/shard_map/scatter | solution.py:52
  50.3 3.4 %scatter.55 = bf16[4,10,10,640]{3,2,1,0:T(8,128)(2,1)} dynamic-update-slice(bf16[4,10,10,640]{3,2,1,0:T(8,128)(2,1)} %scatter.54, bf16[4,1,8,512]{3,2,1,0:T(8,128)(2,1)S(1)} %get-tuple-element.338, s32[]{:T(128)} %copy.143, s32[]{:T(128)} %copy.143, s32[]{:T(128)} %constant.417.clone.1, s32[]{:T(128)} %constant.419.clone.1) | dynamic-update-slice | bytes 65540 | tf_op jit(solution)/shard_map/scatter | solution.py:53
  53.7 3.4 %scatter.56 = bf16[4,10,10,640]{3,2,1,0:T(8,128)(2,1)} dynamic-update-slice(bf16[4,10,10,640]{3,2,1,0:T(8,128)(2,1)} %scatter.55, bf16[4,1,8,512]{3,2,1,0:T(8,128)(2,1)S(1)} %get-tuple-element.337, s32[]{:T(128)} %copy.143, s32[]{:T(128)} %constant.420.clone.1, s32[]{:T(128)} %constant.417.clone.1, s32[]{:T(128)} %constant.419.clone.1) | dynamic-update-slice | bytes 65540 | tf_op jit(solution)/shard_map/scatter | solution.py:54
  57.8 103.2 %while.34 = (s32[]{:T(128)}, bf16[2,2,8,8,512]{4,3,2,1,0:T(8,128)(2,1)}, bf16[2,2,10,10,640]{4,3,2,1,0:T(8,128)(2,1)}, bf16[27,64,64]{2,1,0:T(8,128)(2,1)S(1)}, ...) while((s32[]{:T(128)}, bf16[2,2,8,8,512]{4,3,2,1,0:T(8,128)(2,1)}, ...), condition=%wide.region_1.2_spmd, body=%wide.region_0.1_spmd.sunk | while | flops 226754560 | bytes 33116592 | solution.py:86
  59.9 1.1 stack.230
  61.8 1.1 stack.231
  63.7 1.1 stack.232
  65.5 1.1 stack.233
  72.1 1.6 fusion.47
  73.7 1.1 stack.238
  103.6 4.8 %convolution_bitcast_fusion.4 = f32[2,8,8,8,64]{4,3,2,1,0:T(8,128)S(1)} fusion(bf16[2,27,8,8,8,64]{5,4,1,3,2,0:T(8,128)(2,1)} %constant_dynamic-update-slice_fusion.146, bf16[27,64,64]{2,1,0:T(8,128)(2,1)S(1)} %get-tuple-element.550), kind=kOutput, calls=%fused_computation.8.clone.1 | convolution fusion | flops 226492416 | bytes 4022272 | tf_op jit(solution)/shard_map/while/body/eval_jaxpr/btzyxc,tcd->bzyxd/dot_general | solution.py:78
  123.7 1.6 fusion.47
  125.3 1.1 stack.238
  155.2 4.8 %convolution_bitcast_fusion.4 = f32[2,8,8,8,64]{4,3,2,1,0:T(8,128)S(1)} fusion(bf16[2,27,8,8,8,64]{5,4,1,3,2,0:T(8,128)(2,1)} %constant_dynamic-update-slice_fusion.146, bf16[27,64,64]{2,1,0:T(8,128)(2,1)S(1)} %get-tuple-element.550), kind=kOutput, calls=%fused_computation.8.clone.1 | convolution fusion | flops 226492416 | bytes 4022272 | tf_op jit(solution)/shard_map/while/body/eval_jaxpr/btzyxc,tcd->bzyxd/dot_general | solution.py:78
  161.0 1.3 reshape_reshape.11
  165.2 1.3 collective-permute-start.3
  166.5 5.1 %collective-permute-start.2 = (bf16[1,8,512]{2,1,0:T(8,128)(2,1)S(1)}, bf16[1,8,512]{2,1,0:T(8,128)(2,1)S(1)}, u32[]{:S(2)}, u32[]{:S(2)}) collective-permute-start(bf16[1,8,512]{2,1,0:T(8,128)(2,1)S(1)} %get-tuple-element.343), channel_id=1, source_target_pairs={{0,4},{4,8},{8,12},{12,16},{16,20},{20,24},{24,28},{1,5},{5,9},{9,... | collective-permute-start | bytes 24584 | tf_op jit(solution)/shard_map/ppermute | solution.py:10
  172.3 1.1 reshape.890
  173.4 1.4 scatter.59
  175.8 1.4 scatter.60
  177.2 9.8 %scatter.61 = bf16[4,10,10,640]{3,2,1,0:T(8,128)(2,1)S(1)} dynamic-update-slice(bf16[4,10,10,640]{3,2,1,0:T(8,128)(2,1)S(1)} %scatter.60, bf16[4,8,8,64]{3,2,1,0:T(8,128)(2,1)S(1)} %reshape.901, s32[]{:T(128)} %copy.143, s32[]{:T(128)} %constant.417.clone.1, s32[]{:T(128)} %constant.417.clone.1, s32[]{:T(128)} %constant.418.clone.1) | dynamic-update-slice | bytes 65540 | tf_op jit(solution)/shard_map/scatter | solution.py:48
  187.0 6.5 %scatter.64 = bf16[4,10,10,640]{3,2,1,0:T(8,128)(2,1)S(1)} dynamic-update-slice(bf16[4,10,10,640]{3,2,1,0:T(8,128)(2,1)S(1)} %scatter.61, bf16[4,8,1,512]{3,2,1,0:T(2,128)(2,1)S(1)} %copy.35, s32[]{:T(128)} %copy.143, s32[]{:T(128)} %constant.417.clone.1, s32[]{:T(128)} %copy.143, s32[]{:T(128)} %constant.419.clone.1) | dynamic-update-slice | bytes 65540 | tf_op jit(solution)/shard_map/scatter | solution.py:51
  193.6 6.5 %scatter.65 = bf16[4,10,10,640]{3,2,1,0:T(8,128)(2,1)S(1)} dynamic-update-slice(bf16[4,10,10,640]{3,2,1,0:T(8,128)(2,1)S(1)} %scatter.64, bf16[4,8,1,512]{3,2,1,0:T(2,128)(2,1)S(1)} %copy.36, s32[]{:T(128)} %copy.143, s32[]{:T(128)} %constant.417.clone.1, s32[]{:T(128)} %constant.420.clone.1, s32[]{:T(128)} %constant.419.clone.1) | dynamic-update-slice | bytes 65540 | tf_op jit(solution)/shard_map/scatter | solution.py:52
  200.1 1.8 scatter.66
  201.9 1.8 scatter.69
  204.5 73.4 %while.35 = (s32[]{:T(128)}, bf16[2,2,8,8,512]{4,3,2,1,0:T(8,128)(2,1)}, bf16[2,2,10,10,640]{4,3,2,1,0:T(8,128)(2,1)S(1)}, bf16[27,64,64]{2,1,0:T(8,128)(2,1)S(1...) while((s32[]{:T(128)}, bf16[2,2,8,8,512]{4,3,2,1,0:T(8,128)(2,1)}, ...), condition=%wide.region_3.4_spmd, body=%wide.region_2.3_spmd.sunk | while | flops 226754560 | bytes 36688332 | solution.py:86
  213.4 1.2 fusion.52
  235.3 4.8 %convolution_bitcast_fusion.5 = f32[2,8,8,8,64]{4,3,2,1,0:T(8,128)S(1)} fusion(bf16[2,27,8,8,8,64]{5,4,1,3,2,0:T(8,128)(2,1)} %constant_dynamic-update-slice_fusion.173, bf16[27,64,64]{2,1,0:T(8,128)(2,1)S(1)} %get-tuple-element.571), kind=kOutput, calls=%fused_computation.40.clone.1 | convolution fusion | flops 226492416 | bytes 4022272 | tf_op jit(solution)/shard_map/while/body/eval_jaxpr/btzyxc,tcd->bzyxd/dot_general | solution.py:78
  250.1 1.2 fusion.52
  272.0 4.8 %convolution_bitcast_fusion.5 = f32[2,8,8,8,64]{4,3,2,1,0:T(8,128)S(1)} fusion(bf16[2,27,8,8,8,64]{5,4,1,3,2,0:T(8,128)(2,1)} %constant_dynamic-update-slice_fusion.173, bf16[27,64,64]{2,1,0:T(8,128)(2,1)S(1)} %get-tuple-element.571), kind=kOutput, calls=%fused_computation.40.clone.1 | convolution fusion | flops 226492416 | bytes 4022272 | tf_op jit(solution)/shard_map/while/body/eval_jaxpr/btzyxc,tcd->bzyxd/dot_general | solution.py:78
  277.8 1.3 reshape_reshape.12
  279.2 1.5 gather_fusion.6
  280.7 1.3 collective-permute-start.5
  282.0 1.5 gather_fusion.4
  283.5 4.6 %collective-permute-start.4 = (bf16[3,8,8,512]{3,2,1,0:T(8,128)(2,1)S(1)}, bf16[3,8,8,512]{3,2,1,0:T(8,128)(2,1)S(1)}, u32[]{:S(2)}, u32[]{:S(2)}) collective-permute-start(bf16[3,8,8,512]{3,2,1,0:T(8,128)(2,1)S(1)} %gather_fusion.4), channel_id=1, source_target_pairs={{0,1},{1,2},{2,3},{4,5},{5,6},{6,7},{8,9},{9,10},{10,11},{12,13},{... | collective-permute-start | bytes 589832 | tf_op jit(solution)/shard_map/ppermute | solution.py:10
  288.4 1.2 collective-permute-done.5
  290.9 2.0 collective-permute-done.4
  (380 shorter events, 163.1 us)
Async XLA Ops:
  0.0 16.4 %copy-start.7 = (bf16[1,4,8,8,512]{4,3,2,1,0:T(8,128)(2,1)S(1)}, bf16[1,4,8,8,512]{4,3,2,1,0:T(8,128)(2,1)}, u32[]{:S(2)}) copy-start(bf16[1,4,8,8,512]{4,3,2,1,0:T(8,128)(2,1)} %param.43) | copy-start | bytes 786436
  0.0 17.8 %copy-start.12 = (f32[2,64]{1,0:T(2,128)S(1)}, f32[2,64]{1,0:T(2,128)}, u32[]{:S(2)}) copy-start(f32[2,64]{1,0:T(2,128)} %param.46) | copy-start | bytes 1540
  0.0 17.9 %copy-start.15 = (s32[1,3]{1,0:T(1,128)S(1)}, s32[1,3]{1,0:T(1,128)}, u32[]{:S(2)}) copy-start(s32[1,3]{1,0:T(1,128)} %param.52) | copy-start | bytes 40
  0.0 17.9 %copy-start.16 = (s32[1,3]{1,0:T(1,128)S(1)}, s32[1,3]{1,0:T(1,128)}, u32[]{:S(2)}) copy-start(s32[1,3]{1,0:T(1,128)} %param.50) | copy-start | bytes 40
  4.2 13.8 %copy-start.11 = (pred[2]{0:T(512)(128)(4,1)}, pred[2]{0:T(512)(128)(4,1)S(1)}, u32[]{:S(2)}) copy-start(pred[2]{0:T(512)(128)(4,1)S(1)} %compare_bitcast_fusion.1) | copy-start | bytes 10
  5.8 13.7 %collective-permute-start.1 = (bf16[1,8,512]{2,1,0:T(8,128)(2,1)S(1)}, bf16[1,8,512]{2,1,0:T(8,128)(2,1)S(1)}, u32[]{:S(2)}, u32[]{:S(2)}) collective-permute-start(bf16[1,8,512]{2,1,0:T(8,128)(2,1)S(1)} %get-tuple-element.346), channel_id=1, source_target_pairs={{4,0},{8,4},{12,8},{16,12},{20,16},{24,20},{28,24},{5,1},{9,5},{13... | collective-permute-start | bytes 24584 | tf_op jit(solution)/shard_map/ppermute | solution.py:10
  7.1 12.4 %collective-permute-start = (bf16[1,8,512]{2,1,0:T(8,128)(2,1)S(1)}, bf16[1,8,512]{2,1,0:T(8,128)(2,1)S(1)}, u32[]{:S(2)}, u32[]{:S(2)}) collective-permute-start(bf16[1,8,512]{2,1,0:T(8,128)(2,1)S(1)} %get-tuple-element.345), channel_id=1, source_target_pairs={{0,4},{4,8},{8,12},{12,16},{16,20},{20,24},{24,28},{1,5},{5,9},{9,... | collective-permute-start | bytes 24584 | tf_op jit(solution)/shard_map/ppermute | solution.py:10
  73.7 25.1 %copy-start = (bf16[2,8,8,512]{3,2,1,0:T(8,128)(2,1)S(1)}, bf16[2,8,8,512]{3,2,1,0:T(8,128)(2,1)}, u32[]{:S(2)}) copy-start(bf16[2,8,8,512]{3,2,1,0:T(8,128)(2,1)} %get-tuple-element.495) | copy-start | bytes 393220 | tf_op jit(solution)/shard_map/while
  99.8 8.9 %copy-start.5 = (bf16[2,2,8,8,512]{4,3,2,1,0:T(8,128)(2,1)S(1)}, bf16[2,2,8,8,512]{4,3,2,1,0:T(8,128)(2,1)}, u32[]{:S(2)}) copy-start(bf16[2,2,8,8,512]{4,3,2,1,0:T(8,128)(2,1)} %get-tuple-element.541) | copy-start | bytes 786436 | tf_op jit(solution)/shard_map/while
  108.7 0.7 copy-start.6
  125.3 25.1 %copy-start = (bf16[2,8,8,512]{3,2,1,0:T(8,128)(2,1)S(1)}, bf16[2,8,8,512]{3,2,1,0:T(8,128)(2,1)}, u32[]{:S(2)}) copy-start(bf16[2,8,8,512]{3,2,1,0:T(8,128)(2,1)} %get-tuple-element.495) | copy-start | bytes 393220 | tf_op jit(solution)/shard_map/while
  151.4 8.9 %copy-start.5 = (bf16[2,2,8,8,512]{4,3,2,1,0:T(8,128)(2,1)S(1)}, bf16[2,2,8,8,512]{4,3,2,1,0:T(8,128)(2,1)}, u32[]{:S(2)}) copy-start(bf16[2,2,8,8,512]{4,3,2,1,0:T(8,128)(2,1)} %get-tuple-element.541) | copy-start | bytes 786436 | tf_op jit(solution)/shard_map/while
  160.3 0.7 copy-start.6
  165.2 9.5 %collective-permute-start.3 = (bf16[1,8,512]{2,1,0:T(8,128)(2,1)S(1)}, bf16[1,8,512]{2,1,0:T(8,128)(2,1)S(1)}, u32[]{:S(2)}, u32[]{:S(2)}) collective-permute-start(bf16[1,8,512]{2,1,0:T(8,128)(2,1)S(1)} %get-tuple-element.344), channel_id=1, source_target_pairs={{4,0},{8,4},{12,8},{16,12},{20,16},{24,20},{28,24},{5,1},{9,5},{13... | collective-permute-start | bytes 24584 | tf_op jit(solution)/shard_map/ppermute | solution.py:10
  166.5 8.2 %collective-permute-start.2 = (bf16[1,8,512]{2,1,0:T(8,128)(2,1)S(1)}, bf16[1,8,512]{2,1,0:T(8,128)(2,1)S(1)}, u32[]{:S(2)}, u32[]{:S(2)}) collective-permute-start(bf16[1,8,512]{2,1,0:T(8,128)(2,1)S(1)} %get-tuple-element.343), channel_id=1, source_target_pairs={{0,4},{4,8},{8,12},{12,16},{16,20},{20,24},{24,28},{1,5},{5,9},{9,... | collective-permute-start | bytes 24584 | tf_op jit(solution)/shard_map/ppermute | solution.py:10
  204.5 83.6 %copy-start.10 = (bf16[3,64,64]{2,1,0:T(8,128)(2,1)S(1)}, bf16[3,64,64]{2,1,0:T(8,128)(2,1)}, u32[]{:S(2)}) copy-start(bf16[3,64,64]{2,1,0:T(8,128)(2,1)} %param.47) | copy-start | bytes 73732
  204.5 85.7 %copy-start.14 = (pred[4]{0:T(512)(128)(4,1)S(1)}, pred[4]{0:T(512)(128)(4,1)}, u32[]{:S(2)}) copy-start(pred[4]{0:T(512)(128)(4,1)} %compare_bitcast_fusion) | copy-start | bytes 16
  204.5 89.0 %copy-start.13 = (pred[4]{0:T(512)(128)(4,1)S(1)}, pred[4]{0:T(512)(128)(4,1)}, u32[]{:S(2)}) copy-start(pred[4]{0:T(512)(128)(4,1)} %compare_bitcast_fusion.3) | copy-start | bytes 16
  204.5 0.9 copy-start.1
  229.8 10.6 %copy-start.3 = (bf16[2,2,8,8,512]{4,3,2,1,0:T(8,128)(2,1)S(1)}, bf16[2,2,8,8,512]{4,3,2,1,0:T(8,128)(2,1)}, u32[]{:S(2)}) copy-start(bf16[2,2,8,8,512]{4,3,2,1,0:T(8,128)(2,1)} %get-tuple-element.562) | copy-start | bytes 786436 | tf_op jit(solution)/shard_map/while
  230.5 10.6 %copy-start.2 = (bf16[2,2,10,10,640]{4,3,2,1,0:T(8,128)(2,1)S(1)}, bf16[2,2,10,10,640]{4,3,2,1,0:T(8,128)(2,1)}, u32[]{:S(2)}) copy-start(bf16[2,2,10,10,640]{4,3,2,1,0:T(8,128)(2,1)} %copy-done.1) | copy-start | bytes 1536004 | tf_op jit(solution)/shard_map/while
  240.4 0.7 copy-start.4
  241.1 0.9 copy-start.1
  266.5 10.6 %copy-start.3 = (bf16[2,2,8,8,512]{4,3,2,1,0:T(8,128)(2,1)S(1)}, bf16[2,2,8,8,512]{4,3,2,1,0:T(8,128)(2,1)}, u32[]{:S(2)}) copy-start(bf16[2,2,8,8,512]{4,3,2,1,0:T(8,128)(2,1)} %get-tuple-element.562) | copy-start | bytes 786436 | tf_op jit(solution)/shard_map/while
  267.2 10.6 %copy-start.2 = (bf16[2,2,10,10,640]{4,3,2,1,0:T(8,128)(2,1)S(1)}, bf16[2,2,10,10,640]{4,3,2,1,0:T(8,128)(2,1)}, u32[]{:S(2)}) copy-start(bf16[2,2,10,10,640]{4,3,2,1,0:T(8,128)(2,1)} %copy-done.1) | copy-start | bytes 1536004 | tf_op jit(solution)/shard_map/while
  277.1 0.7 copy-start.4
  277.8 16.9 %copy-start.8 = (bf16[1,4,8,8,512]{4,3,2,1,0:T(8,128)(2,1)S(1)}, bf16[1,4,8,8,512]{4,3,2,1,0:T(8,128)(2,1)}, u32[]{:S(2)}) copy-start(bf16[1,4,8,8,512]{4,3,2,1,0:T(8,128)(2,1)} %param.43) | copy-start | bytes 786436
  277.8 16.9 %copy-start.9 = (f32[1,4,8,8,512]{4,3,2,1,0:T(8,128)S(1)}, f32[1,4,8,8,512]{4,3,2,1,0:T(8,128)}, u32[]{:S(2)}) copy-start(f32[1,4,8,8,512]{4,3,2,1,0:T(8,128)} %reshape.890) | copy-start | bytes 1572868
  280.7 8.9 %collective-permute-start.5 = (bf16[3,8,8,512]{3,2,1,0:T(8,128)(2,1)S(1)}, bf16[3,8,8,512]{3,2,1,0:T(8,128)(2,1)S(1)}, u32[]{:S(2)}, u32[]{:S(2)}) collective-permute-start(bf16[3,8,8,512]{3,2,1,0:T(8,128)(2,1)S(1)} %gather_fusion.6), channel_id=1, source_target_pairs={{1,0},{2,1},{3,2},{5,4},{6,5},{7,6},{9,8},{10,9},{11,10},{13,12},{... | collective-permute-start | bytes 589832 | tf_op jit(solution)/shard_map/ppermute | solution.py:10
  283.5 9.3 %collective-permute-start.4 = (bf16[3,8,8,512]{3,2,1,0:T(8,128)(2,1)S(1)}, bf16[3,8,8,512]{3,2,1,0:T(8,128)(2,1)S(1)}, u32[]{:S(2)}, u32[]{:S(2)}) collective-permute-start(bf16[3,8,8,512]{3,2,1,0:T(8,128)(2,1)S(1)} %gather_fusion.4), channel_id=1, source_target_pairs={{0,1},{1,2},{2,3},{4,5},{5,6},{6,7},{8,9},{9,10},{10,11},{12,13},{... | collective-permute-start | bytes 589832 | tf_op jit(solution)/shard_map/ppermute | solution.py:10
where the time goes:
time: 299 us; the launch traced here: 296 us
  local copies, waits for them, and re-layouts  243 us (81%)
  matrix products  20.3 us (7%)
  starting transfers between devices  16.6 us (6%)
  other arithmetic  11 us (4%)
  waiting for transfers between devices  3.15 us (1%)
    while x132, local copies, waits for them, and re-layouts  83.6 us
    another operation x112, local copies, waits for them, and re-layouts, one_group(): jnp.stack(shifted, axis=1)  61.4 us
    scatter x2, local copies, waits for them, and re-layouts, padded_block(): padded.at[:, inner, inner, (edge_len + 1) * channels:wide_cols]  20.2 us
    dot_general x4, matrix products, one_group(): jnp.einsum('btzyxc,tcd->bzyxd', columns, weights, preferred_element_type=...  19.3 us
    ppermute x6, starting transfers between devices, passed_along(): return lax.ppermute(x, axis, pairs)  16.6 us
    scatter x2, local copies, waits for them, and re-layouts, padded_block(): padded = padded.at[:, inner, 0, middle].set(rim_faces[:, 2])  14.4 us
    scatter x2, local copies, waits for them, and re-layouts, padded_block(): padded = padded.at[:, inner, edge_len + 1, middle].set(rim_faces[:, 3])  14.4 us
    slice x8, local copies, waits for them, and re-layouts, one_group(): piece_block[:, depth_off:depth_off + edge_len, row_off:row_off + edge_len...  8.27 us
  transfers between devices with their start and end apart: 6, of which 2 were waited for; matrix products, arithmetic and copies ran while one was open for 5% of the time, Pallas kernels for 0%

commit v1 on v0

v1 whole, which is shorter than its diff:
```python
import functools

import jax
import jax.numpy as jnp
from jax import lax
from jax.experimental import pallas as pl
from jax.experimental.pallas import tpu as pltpu
from jax.sharding import PartitionSpec as P

F32 = jnp.float32
BF16 = jnp.bfloat16
LANES = 128
AXES = ("space", "frame")


def swap_pairs(peers, frames):
    def at(s, t):
        return s * frames + t

    def second(i, n):
        return ((i + 1) ^ 1) - 1 if 0 < i < n - 1 else -1

    space_first, space_second, frame_first, frame_second = [], [], [], []
    for s in range(peers):
        for t in range(frames):
            space_first.append((at(s, t), at(s ^ 1, t)))
            other = second(s, peers)
            space_second.append((at(s, t), at(other, t) if other >= 0 else at(s, t ^ 1)))
            frame_first.append((at(s, t), at(s, t ^ 1)))
            other = second(t, frames)
            frame_second.append((at(s, t), at(s, other) if other >= 0 else at(s ^ 1, t)))
    return space_first, space_second, frame_first, frame_second


def iota(shape, dim):
    return lax.broadcasted_iota(jnp.int32, shape, dim)


def half(tile):
    return pltpu.roll(tile, LANES // 2, 1)


class Tables:
    def __init__(self, send_ref, source_ref, bricks, slabs):
        self.send_ref, self.source_ref = send_ref, source_ref
        self.bricks, self.slabs = bricks, slabs

    def sent(self, side, k):
        entry = self.send_ref[0, side * self.slabs + k]
        return jnp.where(entry < 0, self.bricks, entry // 6)

    def raw(self, brick, face):
        inside = jnp.minimum(brick, self.bricks - 1)
        return jnp.where(brick < self.bricks, self.source_ref[0, inside, face], -1)

    def local(self, brick, face):
        entry = self.raw(brick, face)
        base = 2 * self.slabs
        return jnp.where(entry >= base, (entry - base) // 6, self.bricks)

    def remote(self, brick, face):
        entry = self.raw(brick, face)
        low = face * self.slabs
        return (entry >= low) & (entry < low + self.slabs)

    def rim(self, brick, face):
        entry = self.raw(brick, face)
        low = face * self.slabs
        has = self.send_ref[0, face * self.slabs] >= 0
        arrived = jnp.where(has, self.bricks + 1 + entry - low, self.bricks)
        return jnp.where(self.remote(brick, face), arrived, self.local(brick, face))


def pack_kernel(send_ref, source_ref, feat_ref, occ_ref, rt_ref, mask_ref, pa_ref, pb_ref):
    _, bricks, edge, _, wide = feat_ref.shape
    channels = wide // edge
    slabs = send_ref.shape[1] // 2
    per_tile = LANES // (edge * edge)
    rows8, lanes8 = iota((8, LANES), 0), iota((8, LANES), 1)
    low = lanes8 < channels
    occ = occ_ref[0].astype(F32)
    picked = []
    for z in range(edge):
        keep = (lanes8 // edge) == (z % per_tile) * edge + rows8
        first = (z // per_tile) * LANES
        for b in range(bricks):
            row = jnp.broadcast_to(occ[b : b + 1, first : first + LANES], (8, LANES))
            picked.append(jnp.where(keep, row, 0.0))
    spread = (iota((LANES, wide), 0) % edge == iota((LANES, wide), 1) // channels).astype(F32)
    mask = jnp.dot(
        jnp.concatenate(picked, axis=0).astype(BF16),
        spread.astype(BF16),
        preferred_element_type=F32,
    )
    mask_ref[...] = mask
    tiles = wide // LANES
    for z in range(edge):
        for b in range(bricks):
            at = (z * bricks + b) * edge
            block = feat_ref[0, b, z].astype(F32) * mask[at : at + edge]
            for k in range(tiles):
                cols = slice(k * LANES, (k + 1) * LANES)
                rt_ref[b, z, :, cols] = half(block[:, cols])
    rt_ref[bricks] = jnp.zeros_like(rt_ref[bricks])

    tables = Tables(send_ref, source_ref, bricks, slabs)
    first = slice(0, LANES)
    last = slice(wide - LANES, wide)
    zero = jnp.zeros((8, LANES), F32)

    def window(side, k):
        brick = tables.sent(side, k)
        inside = jnp.minimum(brick, bricks - 1)
        own = last if side else first
        flag = jnp.where(tables.remote(brick, side), 1.0, 0.0)
        near = tables.local(brick, side)
        y_low, y_high = tables.local(brick, 2), tables.local(brick, 3)
        z_low, z_high = tables.local(brick, 4), tables.local(brick, 5)

        def pair(tile, outer, spare):
            if side:
                return [jnp.where(low, spare, tile), jnp.where(low, tile, outer)]
            return [jnp.where(low, outer, tile), jnp.where(low, tile, spare)]

        planes = [pair(rt_ref[z_low, edge - 1, :, own], flag + zero, zero)]
        for z in range(edge):
            at = pl.multiple_of((z * bricks + inside) * edge, edge)
            keep = half(mask_ref[pl.ds(at, edge), own])
            outer = rt_ref[near, z, :, first if side else last]
            planes.append(pair(rt_ref[brick, z, :, own], outer, keep))
        planes.append(pair(rt_ref[z_high, 0, :, own], zero, zero))
        for brick_y, row in ((y_low, edge - 1), (y_high, 0)):
            gathered = zero
            for z in range(edge):
                tile = rt_ref[brick_y, z, :, own]
                if (z - row) % 8:
                    tile = pltpu.roll(tile, (z - row) % 8, 0)
                gathered = jnp.where(rows8 == z, tile, gathered)
            planes.append(pair(gathered, zero, zero))
        return [jnp.concatenate([p[c] for p in planes], axis=0) for c in range(2)]

    odd = lax.rem(lax.axis_index("space"), 2) == 1
    size = (edge + 4) * 8
    for k in range(slabs):
        down, up = window(0, k), window(1, k)
        for c in range(2):
            cols = slice(c * LANES, (c + 1) * LANES)
            at = slice(k * size, (k + 1) * size)
            pa_ref[at, cols] = jnp.where(odd, down[c], up[c]).astype(BF16)
            pb_ref[at, cols] = jnp.where(odd, up[c], down[c]).astype(BF16)


def banded(w_ref, layer, band_ref):
    blank = jnp.zeros(w_ref.shape[2:], BF16)
    depth = w_ref.shape[2]
    for tap in range(9):
        before, here, after = (w_ref[layer, 3 * tap + i] for i in range(3))
        for row, (left, right) in enumerate(
            ((before, blank), (here, before), (after, here), (blank, after))
        ):
            at = (tap * 4 + row) * depth
            band_ref[at : at + depth, :] = jnp.concatenate([left, right], axis=1)


def shifted(tile, rim, down):
    rows8 = iota(tile.shape, 0)
    if down:
        return pltpu.roll(jnp.where(rows8 == 7, rim, tile), 1, 0)
    return pltpu.roll(jnp.where(rows8 == 0, rim, tile), 7, 0)


def fill_padded(tables, rt_ref, high_ref, low_ref, pad_ref, bricks, edge):
    tiles = rt_ref.shape[-1] // LANES
    low = iota((8, LANES), 1) < LANES // 2
    zero = jnp.zeros((8, LANES), F32)

    def joined(parts, left, right):
        line = [left] + parts + [right]
        return [jnp.where(low, line[i], line[i + 1]) for i in range(tiles + 1)]

    def load(brick, z):
        return [rt_ref[brick, z, :, k * LANES : (k + 1) * LANES] for k in range(tiles)]

    index = [[tables.local(b, f) for f in range(2, 6)] for b in range(bricks)]
    outer = [(tables.rim(b, 0), tables.rim(b, 1)) for b in range(bricks)]
    for z in range(-1, edge + 1):
        for pair in range(0, bricks, 2):
            built = []
            for b in (pair, pair + 1):
                y_low, y_high, z_low, z_high = index[b]
                if z < 0 or z == edge:
                    own = load(z_low, edge - 1) if z < 0 else load(z_high, 0)
                    above = below = [zero] * tiles
                    left = right = zero
                else:
                    own, below, above = load(b, z), load(y_low, z), load(y_high, z)
                    left, right = high_ref[outer[b][0], z], low_ref[outer[b][1], z]
                built.append(
                    (
                        joined(
                            [shifted(t, r, True) for t, r in zip(own, below)],
                            shifted(left, zero, True),
                            shifted(right, zero, True),
                        ),
                        joined(own, left, right),
                        joined(
                            [shifted(t, r, False) for t, r in zip(own, above)],
                            shifted(left, zero, False),
                            shifted(right, zero, False),
                        ),
                    )
                )
            at = ((z + 1) * bricks + pair) * edge
            for dy in range(3):
                for k in range(tiles + 1):
                    block = jnp.concatenate([built[0][dy][k], built[1][dy][k]], axis=0)
                    pad_ref[dy, at : at + 2 * edge, k * LANES : (k + 1) * LANES] = block.astype(BF16)


def tap_rows(pad_ref, rows, step, first_lane):
    return jnp.concatenate(
        [
            pad_ref[dy, dz * step : dz * step + rows, first_lane : first_lane + 2 * LANES]
            for dz in range(3)
            for dy in range(3)
        ],
        axis=1,
    )


def spatial_kernel(
    send_ref,
    source_ref,
    ahead_ref,
    back_ref,
    rt_ref,
    mask_ref,
    ra_ref,
    rb_ref,
    w_ref,
    bias_ref,
    out_ref,
    fa_ref,
    fb_ref,
    rt2_ref,
    high_ref,
    low_ref,
    pad_ref,
    side_ref,
    band_ref,
):
    bricks, edge = rt_ref.shape[0] - 1, rt_ref.shape[1]
    slabs = send_ref.shape[1] // 2
    wide = rt_ref.shape[-1]
    tiles = wide // LANES
    rows = bricks * edge * edge
    tables = Tables(send_ref, source_ref, bricks, slabs)
    low = iota((8, LANES), 1) < LANES // 2
    zero = jnp.zeros((8, LANES), F32)
    odd = lax.rem(lax.axis_index("space"), 2) == 1
    size = (edge + 4) * 8

    arrived_a, arrived_b = ra_ref[...].astype(F32), rb_ref[...].astype(F32)
    from_below = jnp.where(odd, arrived_a, arrived_b)
    from_above = jnp.where(odd, arrived_b, arrived_a)

    def x_faces(field_ref):
        for b in range(bricks + 1):
            for z in range(edge):
                high_ref[b, z] = field_ref[b, z, :, wide - LANES : wide]
                low_ref[b, z] = field_ref[b, z, :, 0:LANES]

    x_faces(rt_ref)
    for k in range(slabs):
        for z in range(edge):
            at = k * size + (z + 1) * 8
            high_ref[bricks + 1 + k, z] = from_below[at : at + 8, LANES : 2 * LANES]
            low_ref[bricks + 1 + k, z] = from_above[at : at + 8, 0:LANES]
    fill_padded(tables, rt_ref, high_ref, low_ref, pad_ref, bricks, edge)

    for k in range(slabs):
        base = k * size

        def plane(source, index):
            at = base + index * 8
            return [source[at : at + 8, c * LANES : (c + 1) * LANES] for c in range(2)]

        below, above = [plane(from_below, i) for i in range(edge + 4)], [
            plane(from_above, i) for i in range(edge + 4)
        ]
        flag_below, flag_above = below[0][1], above[0][0]
        below[0][1] = jnp.where(low, below[0][1], zero)
        above[0][0] = jnp.where(low, zero, above[0][0])
        own_low, own_high = tables.sent(0, k), tables.sent(1, k)
        for z in range(edge):
            mine = low_ref[own_low, z] * flag_below
            below[z + 1][1] = below[z + 1][1] + jnp.where(low, zero, mine)
            mine = high_ref[own_high, z] * flag_above
            above[z + 1][0] = above[z + 1][0] + jnp.where(low, mine, zero)
        for c in range(2):
            for i in range(edge + 2):
                inner = 0 < i <= edge
                per_side = []
                for planes in (below, above):
                    tile = planes[i][c]
                    if inner:
                        first = jnp.broadcast_to(planes[edge + 2][c][i - 1 : i], (8, LANES))
                        after = jnp.broadcast_to(planes[edge + 3][c][i - 1 : i], (8, LANES))
                    else:
                        first = after = zero
                    per_side.append((shifted(tile, first, True), tile, shifted(tile, after, False)))
                at = (i * slabs + k) * 16
                for dy in range(3):
                    block = jnp.concatenate([per_side[0][dy], per_side[1][dy]], axis=0)
                    side_ref[dy, at : at + 16, c * LANES : (c + 1) * LANES] = block.astype(BF16)

    def bias_of(layer):
        row = bias_ref[layer : layer + 1, :]
        return jnp.concatenate([row, row], axis=1)

    banded(w_ref, 0, band_ref)
    bias = bias_of(0)
    step = bricks * edge
    for i in range(tiles):
        total = jnp.dot(
            tap_rows(pad_ref, rows, step, i * LANES), band_ref[...], preferred_element_type=F32
        )
        cols = slice(i * LANES, (i + 1) * LANES)
        value = half(jnp.maximum(total + bias, 0.0) * mask_ref[:, cols])
        for z in range(edge):
            for b in range(bricks):
                at = (z * bricks + b) * edge
                rt2_ref[b, z, :, cols] = value[at : at + edge]
    rt2_ref[bricks] = jnp.zeros_like(rt2_ref[bricks])
    step = 16 * slabs
    total = jnp.dot(
        tap_rows(side_ref, edge * step, step, 0), band_ref[...], preferred_element_type=F32
    )
    value = half(jnp.maximum(total + bias, 0.0))
    x_faces(rt2_ref)
    for k in range(slabs):
        for z in range(edge):
            at = (z * slabs + k) * 16
            from_row = k * size + (z + 1) * 8
            high_ref[bricks + 1 + k, z] = value[at : at + 8] * from_below[from_row : from_row + 8, 0:LANES]
            low_ref[bricks + 1 + k, z] = (
                value[at + 8 : at + 16] * from_above[from_row : from_row + 8, LANES : 2 * LANES]
            )
    fill_padded(tables, rt2_ref, high_ref, low_ref, pad_ref, bricks, edge)

    banded(w_ref, 1, band_ref)
    bias = bias_of(1)
    step = bricks * edge
    for i in range(tiles):
        total = jnp.dot(
            tap_rows(pad_ref, rows, step, i * LANES), band_ref[...], preferred_element_type=F32
        )
        cols = slice(i * LANES, (i + 1) * LANES)
        value = (jnp.maximum(total + bias, 0.0) * mask_ref[:, cols]).astype(BF16)
        for z in range(edge):
            for b in range(bricks):
                at = (z * bricks + b) * edge
                out_ref[b, z, :, cols] = value[at : at + edge]

    odd_frame = lax.rem(lax.axis_index("frame"), 2) == 1
    for slot in range(ahead_ref.shape[1]):
        ahead, back = ahead_ref[0, slot], back_ref[0, slot]
        fa_ref[slot] = out_ref[jnp.where(odd_frame, back, ahead)]
        fb_ref[slot] = out_ref[jnp.where(odd_frame, ahead, back)]


def temporal_kernel(
    prior_ref, later_ref, feat_ref, mask_ref, hid_ref, ga_ref, gb_ref, w_ref, out_ref
):
    _, bricks, edge, _, wide = feat_ref.shape
    depth = w_ref.shape[1]
    blank = jnp.zeros((depth, depth), BF16)
    bands = []
    for i in range(3):
        w = w_ref[i]
        bands.append(jnp.concatenate([w, blank], axis=1))
        bands.append(jnp.concatenate([blank, w], axis=1))
    band = jnp.concatenate(bands, axis=0)
    odd_frame = lax.rem(lax.axis_index("frame"), 2) == 1
    slots = ga_ref.shape[0]
    for b in range(bricks):
        prior, later = prior_ref[0, b], later_ref[0, b]
        at_prior, at_later = jnp.clip(prior, 0, slots - 1), jnp.clip(later, 0, slots - 1)

        def flat(block):
            return block.astype(F32).reshape(edge * edge, wide)

        before = flat(jnp.where(odd_frame, ga_ref[at_prior], gb_ref[at_prior]))
        after = flat(jnp.where(odd_frame, gb_ref[at_later], ga_ref[at_later]))
        before = jnp.where(prior >= 0, before, 0.0).astype(BF16)
        after = jnp.where(later >= 0, after, 0.0).astype(BF16)
        here = flat(hid_ref[b]).astype(BF16)
        for k in range(wide // LANES):
            cols = slice(k * LANES, (k + 1) * LANES)
            total = jnp.dot(
                jnp.concatenate([before[:, cols], here[:, cols], after[:, cols]], axis=1),
                band,
                preferred_element_type=F32,
            )
            for z in range(edge):
                at = (z * bricks + b) * edge
                keep = mask_ref[at : at + edge, cols]
                x = feat_ref[0, b, z, :, cols].astype(F32) * keep
                out_ref[0, b, z, :, cols] = (
                    keep * (x + total[z * edge : (z + 1) * edge])
                ).astype(BF16)


VMEM = pl.BlockSpec(memory_space=pltpu.VMEM)
SMEM = pl.BlockSpec(memory_space=pltpu.SMEM)


def cost(flops, moved):
    return pl.CostEstimate(flops=flops, bytes_accessed=moved, transcendentals=0)


def per_device(
    swaps,
    features,
    occupancy,
    w_spatial,
    b_spatial,
    w_temporal,
    face_send,
    face_source,
    send_ahead,
    from_prior,
    send_back,
    from_later,
):
    _, bricks, edge, _, wide = features.shape
    slabs = face_send.shape[1] // 2
    slots = send_ahead.shape[1]
    rows = bricks * edge * edge
    space_first, space_second, frame_first, frame_second = swaps
    parcel = jax.ShapeDtypeStruct((slabs * (edge + 4) * 8, 2 * LANES), BF16)
    rolled, mask, parcel_a, parcel_b = pl.pallas_call(
        pack_kernel,
        name="pack",
        out_shape=(
            jax.ShapeDtypeStruct((bricks + 1, edge, edge, wide), F32),
            jax.ShapeDtypeStruct((rows, wide), F32),
            parcel,
            parcel,
        ),
        in_specs=[SMEM, SMEM, VMEM, VMEM],
        out_specs=(VMEM, VMEM, VMEM, VMEM),
        compiler_params=pltpu.CompilerParams(vmem_limit_bytes=8 << 20),
        cost_estimate=cost(10**8, 10**6),
    )(face_send, face_source, features, occupancy)
    arrived_a = lax.ppermute(parcel_a, AXES, space_first)
    arrived_b = lax.ppermute(parcel_b, AXES, space_second)
    sent_block = jax.ShapeDtypeStruct((slots, edge, edge, wide), BF16)
    hidden, parcel_a, parcel_b = pl.pallas_call(
        spatial_kernel,
        name="spatial",
        out_shape=(
            jax.ShapeDtypeStruct((bricks, edge, edge, wide), BF16),
            sent_block,
            sent_block,
        ),
        in_specs=[SMEM] * 4 + [VMEM] * 6,
        out_specs=(VMEM, VMEM, VMEM),
        scratch_shapes=[
            pltpu.VMEM((bricks + 1, edge, edge, wide), F32),
            pltpu.VMEM((bricks + 1 + slabs, edge, edge, LANES), F32),
            pltpu.VMEM((bricks + 1 + slabs, edge, edge, LANES), F32),
            pltpu.VMEM((3, (edge + 2) * bricks * edge, wide + LANES), BF16),
            pltpu.VMEM((3, (edge + 2) * 16 * slabs, 2 * LANES), BF16),
            pltpu.VMEM((36 * w_spatial.shape[2], LANES), BF16),
        ],
        compiler_params=pltpu.CompilerParams(vmem_limit_bytes=24 << 20),
        cost_estimate=cost(10**9, 4 * 10**6),
    )(
        face_send,
        face_source,
        send_ahead,
        send_back,
        rolled,
        mask,
        arrived_a,
        arrived_b,
        w_spatial,
        b_spatial,
    )
    arrived_a = lax.ppermute(parcel_a, AXES, frame_first)
    arrived_b = lax.ppermute(parcel_b, AXES, frame_second)
    return pl.pallas_call(
        temporal_kernel,
        name="temporal",
        out_shape=jax.ShapeDtypeStruct(features.shape, BF16),
        in_specs=[SMEM] * 2 + [VMEM] * 6,
        out_specs=VMEM,
        compiler_params=pltpu.CompilerParams(vmem_limit_bytes=8 << 20),
        cost_estimate=cost(10**8, 2 * 10**6),
    )(from_prior, from_later, features, mask, hidden, arrived_a, arrived_b, w_temporal)


def solution(mesh):
    swaps = swap_pairs(mesh.shape["space"], mesh.shape["frame"])
    in_specs = (
        P("frame", "space", None, None, None),
        P("frame", "space", None),
        P(),
        P(),
        P(),
        P("frame", "space"),
        P("frame", "space", None),
        P("frame", "space"),
        P("frame", "space"),
        P("frame", "space"),
        P("frame", "space"),
    )
    out_specs = P("frame", "space", None, None, None)
    return jax.shard_map(
        functools.partial(per_device, swaps),
        mesh=mesh,
        in_specs=in_specs,
        out_specs=out_specs,
        check_vma=False,
    )
```

time: 299 us -> 25.5 us (0.09)
  the two profiles are of different devices: /device:TPU:0 before, /device:TPU:19 now
where the time goes in v1:
time: 25.5 us; the launch traced here: 25.2 us
  waiting for transfers between devices  10 us (39%)
  Pallas kernels  6.98 us (27%)
  local copies, waits for them, and re-layouts  4.84 us (19%)
  starting transfers between devices  3.31 us (13%)
    ppermute x1, waiting for transfers between devices, per_device(): arrived_a = lax.ppermute(parcel_a, AXES, frame_first)  5.29 us
    unnamed x28, local copies, waits for them, and re-layouts  4.84 us
    pallas_call x1, Pallas kernels, per_device(): pl.pallas_call(spatial_kernel, name='spatial', out_shape=(jax.ShapeDtypeS...  4.28 us
    ppermute x1, waiting for transfers between devices, per_device(): arrived_b = lax.ppermute(parcel_b, AXES, space_second)  3.21 us
    pallas_call x1, Pallas kernels, per_device(): pl.pallas_call(temporal_kernel, name='temporal', out_shape=jax.ShapeDtype...  1.75 us
    ppermute x1, waiting for transfers between devices, per_device(): arrived_b = lax.ppermute(parcel_b, AXES, frame_second)  1.53 us
    ppermute x1, starting transfers between devices, per_device(): arrived_a = lax.ppermute(parcel_a, AXES, frame_first)  1.36 us
    ppermute x1, starting transfers between devices, per_device(): arrived_b = lax.ppermute(parcel_b, AXES, space_second)  1.21 us
  transfers between devices with their start and end apart: 4, of which 3 were waited for; matrix products, arithmetic and copies ran while one was open for 0% of the time, Pallas kernels for 0%

profile of v1, /device:TPU:19, one launch (start us, length us, event | category | flops | bytes accessed | tf_op | source)
XLA Modules:
  0.0 25.2 jit_solution(419088978222373208)
XLA Ops:
  0.0 0.0 copy-start
  0.0 0.9 %copy-done = bf16[1,4,8,8,512]{4,3,2,1,0:T(8,128)(2,1)S(1)} copy-done((bf16[1,4,8,8,512]{4,3,2,1,0:T(8,128)(2,1)S(1)}, bf16[1,4,8,8,512]{4,3,2,1,0:T(8,128)(2,1)}, u32[]{:S(2)}) %copy-start) | copy-done | bytes 262168
  1.0 0.0 copy-start.6
  1.0 0.7 %copy-done.6 = s32[1,4,512]{2,1,0:T(4,128)S(1)} copy-done((s32[1,4,512]{2,1,0:T(4,128)S(1)}, s32[1,4,512]{2,1,0:T(4,128)}, u32[]{:S(2)}) %copy-start.6) | copy-done | bytes 8216
  1.6 0.0 copy-start.7
  1.7 0.7 %copy-done.7 = s32[1,4,6]{2,1,0:T(4,128)S(1)} copy-done((s32[1,4,6]{2,1,0:T(4,128)S(1)}, s32[1,4,6]{2,1,0:T(4,128)}, u32[]{:S(2)}) %copy-start.7) | copy-done | bytes 120
  2.3 0.0 copy-start.10
  2.3 0.7 %copy-done.10 = s32[1,2]{1,0:T(1,128)S(1)} copy-done((s32[1,2]{1,0:T(1,128)S(1)}, s32[1,2]{1,0:T(1,128)}, u32[]{:S(2)}) %copy-start.10) | copy-done | bytes 32
  3.0 1.0 %pack.1 = (f32[5,8,8,512]{3,2,1,0:T(8,128)S(1)}, f32[256,512]{1,0:T(8,128)S(1)}, bf16[96,256]{1,0:T(8,128)(2,1)S(1)}, bf16[96,256]{1,0:T(8,128)(2,1)S(1)}) custom-call(s32[1,2]{1,0:T(1,128)S(1)} %copy-done.10, s32[1,4,6]{2,1,0:T(4,128)S(1)} %copy-done.7, bf16[1,4,8,8,512]{4,3,2,1,0:T(8,128)(2,1)S(1)} %copy-done, s32[1,4,512]{2,1,0:T(4,128)S(1)} %copy-done.6), custom_call_target="tpu_custom_call" | custom-call | flops 100000000 | bytes 1000000 | tf_op jit(solution)/shard_map/pack/pallas_call | solution.py:442
  4.0 0.7 %collective-permute-start = (bf16[96,256]{1,0:T(8,128)(2,1)S(1)}, bf16[96,256]{1,0:T(8,128)(2,1)S(1)}, u32[]{:S(2)}, u32[]{:S(2)}) collective-permute-start(bf16[96,256]{1,0:T(8,128)(2,1)S(1)} %get-tuple-element.14), channel_id=1, source_target_pairs={{0,4},{1,5},{2,6},{3,7},{4,0},{5,1},{6,2},{7,3},{8,12},{9,13},{10,... | collective-permute-start | bytes 147464 | tf_op jit(solution)/shard_map/ppermute | solution.py:456
  4.7 0.0 copy-start.12
  4.7 0.0 copy-start.13
  4.7 0.0 copy-start.8
  4.7 1.2 %collective-permute-start.1 = (bf16[96,256]{1,0:T(8,128)(2,1)S(1)}, bf16[96,256]{1,0:T(8,128)(2,1)S(1)}, u32[]{:S(2)}, u32[]{:S(2)}) collective-permute-start(bf16[96,256]{1,0:T(8,128)(2,1)S(1)} %get-tuple-element.15), channel_id=1, source_target_pairs={{0,1},{1,0},{2,3},{3,2},{4,8},{5,9},{6,10},{7,11},{8,4},{9,5},{10,... | collective-permute-start | bytes 147464 | tf_op jit(solution)/shard_map/ppermute | solution.py:457
  5.9 0.0 collective-permute-done.ra_ref
  5.9 3.2 %collective-permute-done.1.rb_ref = bf16[96,256]{1,0:T(8,128)(2,1)S(1)} collective-permute-done((bf16[96,256]{1,0:T(8,128)(2,1)S(1)}, bf16[96,256]{1,0:T(8,128)(2,1)S(1)}, u32[]{:S(2)}, u32[]{:S(2)}) %collective-permute-start.1) | collective-permute-done | bytes 49184 | tf_op jit(solution)/shard_map/ppermute | solution.py:457
  9.1 0.0 copy-start.9
  9.1 0.0 copy-start.11
  9.1 0.0 copy-done.12
  9.1 0.0 copy-done.13
  9.1 0.0 copy-done.8
  9.1 0.7 %copy-done.9 = f32[2,64]{1,0:T(2,128)S(1)} copy-done((f32[2,64]{1,0:T(2,128)S(1)}, f32[2,64]{1,0:T(2,128)}, u32[]{:S(2)}) %copy-start.9) | copy-done | bytes 536
  9.8 0.0 copy-done.11
  9.8 0.0 copy-start.5
  9.8 1.2 %copy-done.5 = bf16[2,27,64,64]{3,2,1,0:T(8,128)(2,1)S(1)} copy-done((bf16[2,27,64,64]{3,2,1,0:T(8,128)(2,1)S(1)}, bf16[2,27,64,64]{3,2,1,0:T(8,128)(2,1)}, u32[]{:S(2)}) %copy-start.5) | copy-done | bytes 442392
  11.0 0.0 copy-start.1
  11.0 0.0 copy-start.2
  11.0 4.3 %spatial.1 = (bf16[4,8,8,512]{3,2,1,0:T(8,128)(2,1)S(1)}, bf16[3,8,8,512]{3,2,1,0:T(8,128)(2,1)S(1)}, bf16[3,8,8,512]{3,2,1,0:T(8,128)(2,1)S(1)}) custom-call(s32[1,2]{1,0:T(1,128)S(1)} %copy-done.11, s32[1,4,6]{2,1,0:T(4,128)S(1)} %copy-done.8, s32[1,3]{1,0:T(1,128)S(1)} %copy-done.12, s32[1,3]{1,0:T(1,128)S(1)} %copy-done.13, ...), custom_call_target="tpu_custom_call" | custom-call | flops 1000000000 | bytes 4000000 | tf_op jit(solution)/shard_map/spatial/pallas_call | solution.py:459
  15.3 1.4 %collective-permute-start.2 = (bf16[3,8,8,512]{3,2,1,0:T(8,128)(2,1)S(1)}, bf16[3,8,8,512]{3,2,1,0:T(8,128)(2,1)S(1)}, u32[]{:S(2)}, u32[]{:S(2)}) collective-permute-start(bf16[3,8,8,512]{3,2,1,0:T(8,128)(2,1)S(1)} %get-tuple-element.17), channel_id=1, source_target_pairs={{0,1},{1,0},{2,3},{3,2},{4,5},{5,4},{6,7},{7,6},{8,9},{9,8},{10,11... | collective-permute-start | bytes 589832 | tf_op jit(solution)/shard_map/ppermute | solution.py:491
  16.6 0.0 copy-start.3
  16.6 0.0 copy-start.4
  16.6 0.0 collective-permute-start.3
  16.6 5.3 %collective-permute-done.2.ga_ref = bf16[3,8,8,512]{3,2,1,0:T(8,128)(2,1)S(1)} collective-permute-done((bf16[3,8,8,512]{3,2,1,0:T(8,128)(2,1)S(1)}, bf16[3,8,8,512]{3,2,1,0:T(8,128)(2,1)S(1)}, u32[]{:S(2)}, u32[]{:S(2)}) %collective-permute-start.2) | collective-permute-done | bytes 196640 | tf_op jit(solution)/shard_map/ppermute | solution.py:491
  21.9 1.5 %collective-permute-done.3.gb_ref = bf16[3,8,8,512]{3,2,1,0:T(8,128)(2,1)S(1)} collective-permute-done((bf16[3,8,8,512]{3,2,1,0:T(8,128)(2,1)S(1)}, bf16[3,8,8,512]{3,2,1,0:T(8,128)(2,1)S(1)}, u32[]{:S(2)}, u32[]{:S(2)}) %collective-permute-start.3) | collective-permute-done | bytes 196640 | tf_op jit(solution)/shard_map/ppermute | solution.py:492
  23.4 0.0 copy-done.1
  23.4 0.0 copy-done.2
  23.4 0.0 copy-done.3
  23.4 0.0 copy-done.4
  23.5 1.7 %temporal.1 = bf16[1,4,8,8,512]{4,3,2,1,0:T(8,128)(2,1)} custom-call(s32[1,4]{1,0:T(1,128)S(1)} %copy-done.3, s32[1,4]{1,0:T(1,128)S(1)} %copy-done.4, bf16[1,4,8,8,512]{4,3,2,1,0:T(8,128)(2,1)S(1)} %copy-done.1, f32[256,512]{1,0:T(8,128)S(1)} %get-tuple-element.12.mask_ref, bf16[4,8,8,512]{3,2,1,0:T(8,128)(2,1)S(1)} %get-tuple-element.16.hid_ref, ...), custom_call_target="tpu_custom_call" | custom-call | flops 100000000 | bytes 2000000 | tf_op jit(solution)/shard_map/temporal/pallas_call | solution.py:493
Async XLA Ops:
  0.0 0.9 %copy-start = (bf16[1,4,8,8,512]{4,3,2,1,0:T(8,128)(2,1)S(1)}, bf16[1,4,8,8,512]{4,3,2,1,0:T(8,128)(2,1)}, u32[]{:S(2)}) copy-start(bf16[1,4,8,8,512]{4,3,2,1,0:T(8,128)(2,1)} %feat_ref.3) | copy-start | bytes 786436
  1.0 0.7 %copy-start.6 = (s32[1,4,512]{2,1,0:T(4,128)S(1)}, s32[1,4,512]{2,1,0:T(4,128)}, u32[]{:S(2)}) copy-start(s32[1,4,512]{2,1,0:T(4,128)} %occ_ref.1) | copy-start | bytes 24580
  1.6 0.7 %copy-start.7 = (s32[1,4,6]{2,1,0:T(4,128)S(1)}, s32[1,4,6]{2,1,0:T(4,128)}, u32[]{:S(2)}) copy-start(s32[1,4,6]{2,1,0:T(4,128)} %source_ref.3) | copy-start | bytes 292
  2.3 0.7 %copy-start.10 = (s32[1,2]{1,0:T(1,128)S(1)}, s32[1,2]{1,0:T(1,128)}, u32[]{:S(2)}) copy-start(s32[1,2]{1,0:T(1,128)} %send_ref.3) | copy-start | bytes 28
  4.0 2.0 %collective-permute-start = (bf16[96,256]{1,0:T(8,128)(2,1)S(1)}, bf16[96,256]{1,0:T(8,128)(2,1)S(1)}, u32[]{:S(2)}, u32[]{:S(2)}) collective-permute-start(bf16[96,256]{1,0:T(8,128)(2,1)S(1)} %get-tuple-element.14), channel_id=1, source_target_pairs={{0,4},{1,5},{2,6},{3,7},{4,0},{5,1},{6,2},{7,3},{8,12},{9,13},{10,... | collective-permute-start | bytes 147464 | tf_op jit(solution)/shard_map/ppermute | solution.py:456
  4.7 4.4 %copy-start.12 = (s32[1,3]{1,0:T(1,128)S(1)}, s32[1,3]{1,0:T(1,128)}, u32[]{:S(2)}) copy-start(s32[1,3]{1,0:T(1,128)} %ahead_ref.1) | copy-start | bytes 40
  4.7 4.4 %copy-start.13 = (s32[1,3]{1,0:T(1,128)S(1)}, s32[1,3]{1,0:T(1,128)}, u32[]{:S(2)}) copy-start(s32[1,3]{1,0:T(1,128)} %back_ref.1) | copy-start | bytes 40
  4.7 4.4 %copy-start.8 = (s32[1,4,6]{2,1,0:T(4,128)S(1)}, s32[1,4,6]{2,1,0:T(4,128)}, u32[]{:S(2)}) copy-start(s32[1,4,6]{2,1,0:T(4,128)} %source_ref.3) | copy-start | bytes 292
  4.7 4.4 %collective-permute-start.1 = (bf16[96,256]{1,0:T(8,128)(2,1)S(1)}, bf16[96,256]{1,0:T(8,128)(2,1)S(1)}, u32[]{:S(2)}, u32[]{:S(2)}) collective-permute-start(bf16[96,256]{1,0:T(8,128)(2,1)S(1)} %get-tuple-element.15), channel_id=1, source_target_pairs={{0,1},{1,0},{2,3},{3,2},{4,8},{5,9},{6,10},{7,11},{8,4},{9,5},{10,... | collective-permute-start | bytes 147464 | tf_op jit(solution)/shard_map/ppermute | solution.py:457
  9.1 0.7 %copy-start.9 = (f32[2,64]{1,0:T(2,128)S(1)}, f32[2,64]{1,0:T(2,128)}, u32[]{:S(2)}) copy-start(f32[2,64]{1,0:T(2,128)} %bias_ref.1) | copy-start | bytes 1540
  9.1 0.7 %copy-start.11 = (s32[1,2]{1,0:T(1,128)S(1)}, s32[1,2]{1,0:T(1,128)}, u32[]{:S(2)}) copy-start(s32[1,2]{1,0:T(1,128)} %send_ref.3) | copy-start | bytes 28
  9.8 1.2 %copy-start.5 = (bf16[2,27,64,64]{3,2,1,0:T(8,128)(2,1)S(1)}, bf16[2,27,64,64]{3,2,1,0:T(8,128)(2,1)}, u32[]{:S(2)}) copy-start(bf16[2,27,64,64]{3,2,1,0:T(8,128)(2,1)} %w_ref.2) | copy-start | bytes 1327108
  11.0 12.5 %copy-start.1 = (bf16[1,4,8,8,512]{4,3,2,1,0:T(8,128)(2,1)S(1)}, bf16[1,4,8,8,512]{4,3,2,1,0:T(8,128)(2,1)}, u32[]{:S(2)}) copy-start(bf16[1,4,8,8,512]{4,3,2,1,0:T(8,128)(2,1)} %feat_ref.3) | copy-start | bytes 786436
  11.0 12.5 %copy-start.2 = (bf16[3,64,64]{2,1,0:T(8,128)(2,1)S(1)}, bf16[3,64,64]{2,1,0:T(8,128)(2,1)}, u32[]{:S(2)}) copy-start(bf16[3,64,64]{2,1,0:T(8,128)(2,1)} %w_ref.3) | copy-start | bytes 73732
  15.3 6.7 %collective-permute-start.2 = (bf16[3,8,8,512]{3,2,1,0:T(8,128)(2,1)S(1)}, bf16[3,8,8,512]{3,2,1,0:T(8,128)(2,1)S(1)}, u32[]{:S(2)}, u32[]{:S(2)}) collective-permute-start(bf16[3,8,8,512]{3,2,1,0:T(8,128)(2,1)S(1)} %get-tuple-element.17), channel_id=1, source_target_pairs={{0,1},{1,0},{2,3},{3,2},{4,5},{5,4},{6,7},{7,6},{8,9},{9,8},{10,11... | collective-permute-start | bytes 589832 | tf_op jit(solution)/shard_map/ppermute | solution.py:491
  16.6 6.8 %copy-start.3 = (s32[1,4]{1,0:T(1,128)S(1)}, s32[1,4]{1,0:T(1,128)}, u32[]{:S(2)}) copy-start(s32[1,4]{1,0:T(1,128)} %prior_ref.1) | copy-start | bytes 52
  16.6 6.8 %copy-start.4 = (s32[1,4]{1,0:T(1,128)S(1)}, s32[1,4]{1,0:T(1,128)}, u32[]{:S(2)}) copy-start(s32[1,4]{1,0:T(1,128)} %later_ref.1) | copy-start | bytes 52
  16.6 6.8 %collective-permute-start.3 = (bf16[3,8,8,512]{3,2,1,0:T(8,128)(2,1)S(1)}, bf16[3,8,8,512]{3,2,1,0:T(8,128)(2,1)S(1)}, u32[]{:S(2)}, u32[]{:S(2)}) collective-permute-start(bf16[3,8,8,512]{3,2,1,0:T(8,128)(2,1)S(1)} %get-tuple-element.18), channel_id=1, source_target_pairs={{0,4},{1,2},{2,1},{3,7},{4,0},{5,6},{6,5},{7,3},{8,12},{9,10},{10,... | collective-permute-start | bytes 589832 | tf_op jit(solution)/shard_map/ppermute | solution.py:492

commit v2 on v0

v2 whole, which is shorter than its diff:
```python
import functools

import jax
import jax.numpy as jnp
from jax import lax
from jax.experimental import pallas as pl
from jax.experimental.pallas import tpu as pltpu
from jax.sharding import PartitionSpec as P

F32 = jnp.float32
BF16 = jnp.bfloat16
LANES = 128
AXES = ("space", "frame")


def swap_pairs(peers, frames):
    def at(s, t):
        return s * frames + t

    def second(i, n):
        return ((i + 1) ^ 1) - 1 if 0 < i < n - 1 else -1

    space_first, space_second, frame_first, frame_second = [], [], [], []
    for s in range(peers):
        for t in range(frames):
            space_first.append((at(s, t), at(s ^ 1, t)))
            other = second(s, peers)
            space_second.append((at(s, t), at(other, t) if other >= 0 else at(s, t ^ 1)))
            frame_first.append((at(s, t), at(s, t ^ 1)))
            other = second(t, frames)
            frame_second.append((at(s, t), at(s, other) if other >= 0 else at(s ^ 1, t)))
    return space_first, space_second, frame_first, frame_second


def iota(shape, dim):
    return lax.broadcasted_iota(jnp.int32, shape, dim)


def low_half():
    return iota((8, LANES), 1) < LANES // 2


def zero_tile():
    return jnp.zeros((8, LANES), F32)


def half(tile):
    return pltpu.roll(tile, LANES // 2, 1)


def tile_of(k):
    return slice(k * LANES, (k + 1) * LANES)


class Tables:
    def __init__(self, ref, bricks, slabs, slots):
        self.ref, self.bricks, self.slabs, self.slots = ref, bricks, slabs, slots
        self.at_send = 0
        self.at_source = 2 * slabs
        self.at_prior = self.at_source + 6 * bricks
        self.at_later = self.at_prior + bricks
        self.at_ahead = self.at_later + bricks
        self.at_back = self.at_ahead + slots

    def gather(self, send_ref, source_ref, ahead_ref, prior_ref, back_ref, later_ref):
        for i in range(2 * self.slabs):
            self.ref[0, self.at_send + i] = send_ref[0, i]
        for b in range(self.bricks):
            for f in range(6):
                self.ref[0, self.at_source + 6 * b + f] = source_ref[0, b, f]
            self.ref[0, self.at_prior + b] = prior_ref[0, b]
            self.ref[0, self.at_later + b] = later_ref[0, b]
        for i in range(self.slots):
            self.ref[0, self.at_ahead + i] = ahead_ref[0, i]
            self.ref[0, self.at_back + i] = back_ref[0, i]

    def has(self, side):
        return self.ref[0, self.at_send + side * self.slabs] >= 0

    def sent(self, side, k):
        entry = self.ref[0, self.at_send + side * self.slabs + k]
        return jnp.where(entry < 0, self.bricks, entry // 6)

    def raw(self, brick, face):
        inside = jnp.minimum(brick, self.bricks - 1)
        return jnp.where(brick < self.bricks, self.ref[0, self.at_source + 6 * inside + face], -1)

    def local(self, brick, face):
        entry = self.raw(brick, face)
        base = 2 * self.slabs
        return jnp.where(entry >= base, (entry - base) // 6, self.bricks)

    def remote(self, brick, face):
        entry = self.raw(brick, face)
        first = face * self.slabs
        return (entry >= first) & (entry < first + self.slabs)

    def rim(self, brick, face):
        arrived = self.bricks + 1 + self.raw(brick, face) - face * self.slabs
        return jnp.where(self.remote(brick, face), arrived, self.local(brick, face))

    def receiver(self, side, k):
        found = self.bricks
        for b in range(self.bricks):
            found = jnp.where(self.raw(b, side) == side * self.slabs + k, b, found)
        return found


def paired(side, tile, outer, spare):
    low = low_half()
    if side:
        return [jnp.where(low, spare, tile), jnp.where(low, tile, outer)]
    return [jnp.where(low, outer, tile), jnp.where(low, tile, spare)]


def pack_kernel(*refs):
    sources, (table_ref, rt_ref, mask_ref, pa_ref, pb_ref) = refs[:8], refs[8:13]
    held, sems = refs[13:21], refs[21]
    copies = [pltpu.make_async_copy(s, d, sems.at[i]) for i, (s, d) in enumerate(zip(sources, held))]
    for copy in copies:
        copy.start()
    occ_ref, feat_ref = held[6:]
    _, bricks, edge, _, wide = feat_ref.shape
    channels = wide // edge
    tables = Tables(table_ref, bricks, held[0].shape[1] // 2, held[2].shape[1])
    slabs = tables.slabs
    per_tile = LANES // (edge * edge)
    rows8, lanes8 = iota((8, LANES), 0), iota((8, LANES), 1)
    low = low_half()
    spread = (iota((LANES, wide), 0) % edge == iota((LANES, wide), 1) // channels).astype(F32)
    spread = spread.astype(BF16)
    for copy in copies[:-1]:
        copy.wait()
    tables.gather(*held[:6])
    occ = occ_ref[0].astype(F32)
    picked = []
    for z in range(edge):
        keep = (lanes8 // edge) == (z % per_tile) * edge + rows8
        for b in range(bricks):
            row = jnp.broadcast_to(occ[b : b + 1, tile_of(z // per_tile)], (8, LANES))
            picked.append(jnp.where(keep, row, 0.0))
    mask = jnp.dot(jnp.concatenate(picked, axis=0).astype(BF16), spread, preferred_element_type=F32)
    mask_ref[...] = mask
    tiles = wide // LANES
    copies[-1].wait()
    for z in range(edge):
        for b in range(bricks):
            at = (z * bricks + b) * edge
            block = feat_ref[0, b, z].astype(F32) * mask[at : at + edge]
            for k in range(tiles):
                rt_ref[b, z, :, tile_of(k)] = half(block[:, tile_of(k)])
    rt_ref[bricks] = jnp.zeros_like(rt_ref[bricks])

    zero = zero_tile()
    ends = (tile_of(0), tile_of(tiles - 1))

    def window(side, k):
        brick = tables.sent(side, k)
        inside = jnp.minimum(brick, bricks - 1)
        own, other = ends[side], ends[1 - side]
        flag = jnp.where(tables.remote(brick, side), 1.0, 0.0)
        near = tables.local(brick, side)
        planes = [paired(side, rt_ref[tables.local(brick, 4), edge - 1, :, own], flag + zero, zero)]
        for z in range(edge):
            at = pl.multiple_of((z * bricks + inside) * edge, edge)
            keep = half(mask_ref[pl.ds(at, edge), own])
            planes.append(paired(side, rt_ref[brick, z, :, own], rt_ref[near, z, :, other], keep))
        planes.append(paired(side, rt_ref[tables.local(brick, 5), 0, :, own], zero, zero))
        for face, row in ((2, edge - 1), (3, 0)):
            brick_y = tables.local(brick, face)
            gathered = zero
            for z in range(edge):
                tile = rt_ref[brick_y, z, :, own]
                if (z - row) % 8:
                    tile = pltpu.roll(tile, (z - row) % 8, 0)
                gathered = jnp.where(rows8 == z, tile, gathered)
            planes.append(paired(side, gathered, zero, zero))
        return [jnp.concatenate([p[c] for p in planes], axis=0) for c in range(2)]

    odd = lax.rem(lax.axis_index("space"), 2) == 1
    size = (edge + 4) * 8
    for k in range(slabs):
        down, up = window(0, k), window(1, k)
        for c in range(2):
            at = slice(k * size, (k + 1) * size)
            pa_ref[at, tile_of(c)] = jnp.where(odd, down[c], up[c]).astype(BF16)
            pb_ref[at, tile_of(c)] = jnp.where(odd, up[c], down[c]).astype(BF16)


def fill_band(w_ref, layer, band_ref):
    blank = jnp.zeros(w_ref.shape[2:], BF16)
    depth = w_ref.shape[2]
    for dy in range(3):
        for dz in range(3):
            tap = 3 * dz + dy
            before, here, after = (w_ref[layer, 3 * tap + i] for i in range(3))
            for row, (left, right) in enumerate(
                ((before, blank), (here, before), (after, here), (blank, after))
            ):
                block = jnp.concatenate([left, right], axis=1)
                for out in range(2):
                    at = (((dz + out) * 3 + dy) * 4 + row) * depth
                    band_ref[at : at + depth, tile_of(out)] = block
        for out, dz in ((0, 3), (1, 0)):
            at = (dz * 3 + dy) * 4 * depth
            band_ref[at : at + 4 * depth, tile_of(out)] = jnp.zeros((4 * depth, LANES), BF16)


def shifted(tile, rim, down):
    if tile is None and rim is None:
        return None
    zero = zero_tile()
    tile = zero if tile is None else tile
    rim = zero if rim is None else rim
    rows8 = iota(tile.shape, 0)
    if down:
        return pltpu.roll(jnp.where(rows8 == 7, rim, tile), 1, 0)
    return pltpu.roll(jnp.where(rows8 == 0, rim, tile), 7, 0)


def three_shifts(line, before, after):
    return (
        [shifted(t, r, True) for t, r in zip(line, before)],
        line,
        [shifted(t, r, False) for t, r in zip(line, after)],
    )


def merged(line, pairs):
    low, zero = low_half(), zero_tile()
    full = [zero if t is None else t for t in line]
    return [jnp.where(low, full[i], full[j]) for i, j in pairs]


def fill_padded(pad_ref, tables, edge, own, rim, pairs):
    bricks = tables.bricks
    index = [[tables.local(b, f) for f in range(2, 6)] for b in range(bricks)]
    for z in range(-1, edge + 1):
        for first in range(0, bricks, 2):
            built = []
            for b in (first, first + 1):
                y_low, y_high, z_low, z_high = index[b]
                if 0 <= z < edge:
                    line, before, after = own(b, z), rim(y_low, z), rim(y_high, z)
                else:
                    line = rim(z_low, edge - 1) if z < 0 else rim(z_high, 0)
                    before = after = [None] * len(line)
                built.append([merged(s, pairs) for s in three_shifts(line, before, after)])
            at = ((z + 1) * bricks + first) * edge
            for dy in range(3):
                for k in range(len(pairs)):
                    block = jnp.concatenate([built[0][dy][k], built[1][dy][k]], axis=0)
                    pad_ref[dy, at : at + 2 * edge, tile_of(k)] = block.astype(BF16)


def convolve(windows, rows, edge, band_ref):
    blocks = []
    for window in windows:
        parts = []
        for dz in range(4):
            for dy in range(3):
                parts.append(
                    jnp.concatenate(
                        [window(dy, (2 * zz + dz) * rows, rows) for zz in range(edge // 2)], axis=0
                    )
                )
        blocks.append(jnp.concatenate(parts, axis=1))
    total = jnp.dot(jnp.concatenate(blocks, axis=0), band_ref[...], preferred_element_type=F32)

    def result(window, z):
        at = (window * (edge // 2) + z // 2) * rows
        return total[at : at + rows, tile_of(z % 2)]

    return result


def inner_kernel(
    slabs,
    table_ref,
    rt_ref,
    mask_ref,
    w_hbm,
    bias_hbm,
    rt2_ref,
    pad2_ref,
    band1_ref,
    band2_ref,
    bias2_ref,
    mid_ref,
    fa_ref,
    fb_ref,
    w_ref,
    bias_ref,
    pad_ref,
    sems,
):
    copies = [
        pltpu.make_async_copy(w_hbm, w_ref, sems.at[0]),
        pltpu.make_async_copy(bias_hbm, bias_ref, sems.at[1]),
    ]
    for copy in copies:
        copy.start()
    bricks, edge, _, wide = rt_ref.shape
    bricks -= 1
    tiles = wide // LANES
    slots = fa_ref.shape[0]
    tables = Tables(table_ref, bricks, slabs, slots)
    rows = bricks * edge

    def load(field_ref, brick, z):
        return [field_ref[brick, z, :, tile_of(k)] for k in range(tiles)]

    near = [(tables.local(b, 0), tables.local(b, 1)) for b in range(bricks)]

    def own(b, z):
        left = rt_ref[near[b][0], z, :, tile_of(tiles - 1)]
        right = rt_ref[near[b][1], z, :, tile_of(0)]
        return [left] + load(rt_ref, b, z) + [right]

    def rim(brick, z):
        return [None] + load(rt_ref, brick, z) + [None]

    fill_padded(pad_ref, tables, edge, own, rim, [(k, k + 1) for k in range(tiles + 1)])
    for copy in copies:
        copy.wait()
    fill_band(w_ref, 0, band1_ref)
    for layer in range(2):
        row = bias_ref[layer : layer + 1, :]
        bias2_ref[layer : layer + 1, :] = jnp.concatenate([row, row], axis=1)

    def window_of(ref, first):
        def window(dy, at, count):
            return ref[dy, at : at + count, first * LANES : (first + 2) * LANES]

        return window

    result = convolve([window_of(pad_ref, i) for i in range(tiles)], rows, edge, band1_ref)
    bias = bias2_ref[0:1, :]
    for i in range(tiles):
        for z in range(edge):
            keep = mask_ref[z * rows : (z + 1) * rows, tile_of(i)]
            value = half(jnp.maximum(result(i, z) + bias, 0.0) * keep)
            for b in range(bricks):
                rt2_ref[b, z, :, tile_of(i)] = value[b * edge : (b + 1) * edge]
    rt2_ref[bricks] = jnp.zeros_like(rt2_ref[bricks])

    def field(b, z):
        return load(rt2_ref, b, z)

    fill_padded(pad2_ref, tables, edge, field, field, [(k, k + 1) for k in range(tiles - 1)])
    fill_band(w_ref, 1, band2_ref)
    result = convolve([window_of(pad2_ref, i) for i in range(tiles - 2)], rows, edge, band2_ref)
    bias = bias2_ref[1:2, :]
    for i in range(tiles - 2):
        for z in range(edge):
            keep = mask_ref[z * rows : (z + 1) * rows, tile_of(i + 1)]
            value = jnp.maximum(result(i, z) + bias, 0.0) * keep
            for b in range(bricks):
                mid_ref[b, z, :, tile_of(i)] = value[b * edge : (b + 1) * edge].astype(BF16)
    choose_parcels(tables, mid_ref, fa_ref, fb_ref)


def choose_parcels(tables, field_ref, fa_ref, fb_ref):
    odd = lax.rem(lax.axis_index("frame"), 2) == 1
    for slot in range(tables.slots):
        ahead = tables.ref[0, tables.at_ahead + slot]
        back = tables.ref[0, tables.at_back + slot]
        fa_ref[slot] = field_ref[jnp.where(odd, back, ahead)]
        fb_ref[slot] = field_ref[jnp.where(odd, ahead, back)]


def border_kernel(
    table_ref,
    rt_ref,
    mask_ref,
    rt2_ref,
    pad2_ref,
    band1_ref,
    band2_ref,
    bias2_ref,
    ra_ref,
    rb_ref,
    out_ref,
    fa_ref,
    fb_ref,
    edge_ref,
    side_ref,
    pad_ref,
):
    bricks, edge, _, wide = rt_ref.shape
    bricks -= 1
    tiles = wide // LANES
    size = (edge + 4) * 8
    slabs = ra_ref.shape[0] // size
    tables = Tables(table_ref, bricks, slabs, fa_ref.shape[0])
    rows = bricks * edge
    low, zero = low_half(), zero_tile()
    ends = (tile_of(0), tile_of(tiles - 1))
    odd = lax.rem(lax.axis_index("space"), 2) == 1
    arrived_a, arrived_b = ra_ref[...].astype(F32), rb_ref[...].astype(F32)
    arrived = (
        jnp.where(tables.has(0), jnp.where(odd, arrived_a, arrived_b), 0.0),
        jnp.where(tables.has(1), jnp.where(odd, arrived_b, arrived_a), 0.0),
    )

    def arrived_tile(side, k, i, c):
        at = k * size + i * 8
        return arrived[side][at : at + 8, tile_of(c)]

    def own_block(side, k):
        brick = tables.receiver(side, k)
        tile = ends[side]
        y_low, y_high = tables.local(brick, 2), tables.local(brick, 3)
        planes = [paired(side, rt_ref[tables.local(brick, 4), edge - 1, :, tile], zero, zero)]
        before, after = [[None, None]], [[None, None]]
        for z in range(edge):
            face = arrived_tile(side, k, z + 1, 1 - side)
            planes.append(paired(side, rt_ref[brick, z, :, tile], face, zero))
            before.append(paired(side, rt_ref[y_low, z, :, tile], zero, zero))
            after.append(paired(side, rt_ref[y_high, z, :, tile], zero, zero))
        planes.append(paired(side, rt_ref[tables.local(brick, 5), 0, :, tile], zero, zero))
        return planes, before + [[None, None]], after + [[None, None]]

    def far_block(side, k):
        planes = [[arrived_tile(side, k, i, c) for c in range(2)] for i in range(edge + 2)]
        c = 1 - side
        flag = planes[0][c]
        planes[0][c] = jnp.where(low, flag, zero) if c else jnp.where(low, zero, flag)
        mine = tables.sent(side, k)
        before, after = [[None, None]], [[None, None]]
        for z in range(edge):
            face = rt_ref[mine, z, :, ends[side]] * flag
            face = jnp.where(low, zero, face) if c else jnp.where(low, face, zero)
            planes[z + 1][c] = planes[z + 1][c] + face
            rims = []
            for i in (edge + 2, edge + 3):
                pair = [arrived_tile(side, k, i, d)[z : z + 1] for d in range(2)]
                rims.append([jnp.broadcast_to(r, (8, LANES)) for r in pair])
            before.append(rims[0])
            after.append(rims[1])
        return planes, before + [[None, None]], after + [[None, None]]

    blocks = []
    for k in range(slabs):
        blocks += [own_block(0, k), own_block(1, k), far_block(0, k), far_block(1, k)]
    count = len(blocks) * 8
    for i in range(edge + 2):
        for q in range(0, len(blocks), 2):
            shifts = [three_shifts(p[i], r[i], s[i]) for p, r, s in blocks[q : q + 2]]
            at = i * count + q * 8
            for dy in range(3):
                for c in range(2):
                    block = jnp.concatenate([shifts[0][dy][c], shifts[1][dy][c]], axis=0)
                    side_ref[dy, at : at + 16, tile_of(c)] = block.astype(BF16)

    for b in range(bricks + 1):
        for z in range(edge):
            for side in range(2):
                edge_ref[b, z, :, tile_of(side)] = rt2_ref[b, z, :, ends[side]]

    def side_window(dy, at, n):
        return side_ref[dy, at : at + n, :]

    result = convolve([side_window], count, edge, band1_ref)
    bias = bias2_ref[0:1, :]
    for z in range(edge):
        value = jnp.maximum(result(0, z) + bias, 0.0)
        for k in range(slabs):
            for side in range(2):
                at = (4 * k + side) * 8
                brick = tables.receiver(side, k)
                inside = jnp.minimum(brick, bricks - 1)
                from_row = pl.multiple_of((z * bricks + inside) * edge, edge)
                new = half(value[at : at + 8] * mask_ref[pl.ds(from_row, edge), ends[side]])
                old = edge_ref[brick, z, :, tile_of(side)]
                new = jnp.where(low, new, old) if side else jnp.where(low, old, new)
                edge_ref[brick, z, :, tile_of(side)] = jnp.where(brick < bricks, new, old)
                at += 16
                far = half(value[at : at + 8]) * arrived_tile(side, k, z + 1, side)
                edge_ref[bricks + 1 + k, z, :, tile_of(1 - side)] = far

    outer = [(tables.rim(b, 0), tables.rim(b, 1)) for b in range(bricks)]

    def own(b, z):
        left, right = edge_ref[outer[b][0], z, :, tile_of(1)], edge_ref[outer[b][1], z, :, tile_of(0)]
        return [left, edge_ref[b, z, :, tile_of(0)], edge_ref[b, z, :, tile_of(1)], right]

    def rim(brick, z):
        return [None, edge_ref[brick, z, :, tile_of(0)], edge_ref[brick, z, :, tile_of(1)], None]

    fill_padded(pad_ref, tables, edge, own, rim, [(0, 1), (2, 3)])

    def low_window(dy, at, n):
        return jnp.concatenate(
            [pad_ref[dy, at : at + n, tile_of(0)], pad2_ref[dy, at : at + n, tile_of(0)]], axis=1
        )

    def high_window(dy, at, n):
        return jnp.concatenate(
            [pad2_ref[dy, at : at + n, tile_of(tiles - 2)], pad_ref[dy, at : at + n, tile_of(1)]],
            axis=1,
        )

    result = convolve([low_window, high_window], rows, edge, band2_ref)
    bias = bias2_ref[1:2, :]
    for side in range(2):
        for z in range(edge):
            keep = mask_ref[z * rows : (z + 1) * rows, ends[side]]
            value = jnp.maximum(result(side, z) + bias, 0.0) * keep
            for b in range(bricks):
                out_ref[b, z, :, tile_of(side)] = value[b * edge : (b + 1) * edge].astype(BF16)
    choose_parcels(tables, out_ref, fa_ref, fb_ref)


def temporal_part(
    tables, tiles, rt_ref, mask_ref, hid_ref, ga_ref, gb_ref, band, out_hbm, held_ref, sems
):
    bricks, edge, _, part = hid_ref.shape
    odd = lax.rem(lax.axis_index("frame"), 2) == 1

    def flat(block):
        return block.astype(F32).reshape(edge * edge, part)

    copies = []
    for b in range(bricks):
        prior = tables.ref[0, tables.at_prior + b]
        later = tables.ref[0, tables.at_later + b]
        at_prior = jnp.clip(prior, 0, tables.slots - 1)
        at_later = jnp.clip(later, 0, tables.slots - 1)
        before = flat(jnp.where(odd, ga_ref[at_prior], gb_ref[at_prior]))
        after = flat(jnp.where(odd, gb_ref[at_later], ga_ref[at_later]))
        before = jnp.where(prior >= 0, before, 0.0).astype(BF16)
        after = jnp.where(later >= 0, after, 0.0).astype(BF16)
        here = flat(hid_ref[b]).astype(BF16)
        lhs = [
            jnp.concatenate([f[:, tile_of(k)] for f in (before, here, after)], axis=1)
            for k in range(len(tiles))
        ]
        total = jnp.dot(jnp.concatenate(lhs, axis=0), band, preferred_element_type=F32)
        for k, tile in enumerate(tiles):
            for z in range(edge):
                at = (z * bricks + b) * edge
                keep = mask_ref[at : at + edge, tile_of(tile)]
                row = k * edge * edge + z * edge
                sums = half(rt_ref[b, z, :, tile_of(tile)]) + total[row : row + edge]
                held_ref[b, z, :, tile_of(k)] = (keep * sums).astype(BF16)
        done = 0
        while done < len(tiles):
            run = 1
            while done + run < len(tiles) and tiles[done + run] == tiles[done] + run:
                run += 1
            first = tiles[done]
            copies.append(
                pltpu.make_async_copy(
                    held_ref.at[b, :, :, done * LANES : (done + run) * LANES],
                    out_hbm.at[0, b, :, :, first * LANES : (first + run) * LANES],
                    sems.at[len(copies)],
                )
            )
            copies[-1].start()
            done += run
    for copy in copies:
        copy.wait()


def middle_out_kernel(
    slabs,
    table_ref,
    rt_ref,
    mask_ref,
    hid_ref,
    ga_ref,
    gb_ref,
    w_hbm,
    order_ref,
    out_hbm,
    band_ref,
    w_ref,
    held_ref,
    sem,
    sems,
):
    copy = pltpu.make_async_copy(w_hbm, w_ref, sem)
    copy.start()
    copy.wait()
    depth = w_ref.shape[1]
    blank = jnp.zeros((depth, depth), BF16)
    for i in range(3):
        at = 2 * i * depth
        band_ref[at : at + depth, :] = jnp.concatenate([w_ref[i], blank], axis=1)
        band_ref[at + depth : at + 2 * depth, :] = jnp.concatenate([blank, w_ref[i]], axis=1)
    tables = Tables(table_ref, rt_ref.shape[0] - 1, slabs, ga_ref.shape[0])
    tiles = rt_ref.shape[-1] // LANES
    temporal_part(
        tables,
        list(range(1, tiles - 1)),
        rt_ref,
        mask_ref,
        hid_ref,
        ga_ref,
        gb_ref,
        band_ref[...],
        out_hbm,
        held_ref,
        sems,
    )


def edge_out_kernel(
    slabs,
    table_ref,
    rt_ref,
    mask_ref,
    hid_ref,
    ga_ref,
    gb_ref,
    band_ref,
    before_hbm,
    out_hbm,
    held_ref,
    sems,
):
    tables = Tables(table_ref, rt_ref.shape[0] - 1, slabs, ga_ref.shape[0])
    tiles = rt_ref.shape[-1] // LANES
    temporal_part(
        tables,
        [0, tiles - 1],
        rt_ref,
        mask_ref,
        hid_ref,
        ga_ref,
        gb_ref,
        band_ref[...],
        out_hbm,
        held_ref,
        sems,
    )


VMEM = pl.BlockSpec(memory_space=pltpu.VMEM)
SMEM = pl.BlockSpec(memory_space=pltpu.SMEM)
HBM = pl.BlockSpec(memory_space=pltpu.HBM)


def in_hbm(*arrays):
    return [pltpu.with_memory_space_constraint(a, pltpu.HBM) for a in arrays]


def cost(flops, moved):
    return pl.CostEstimate(flops=flops, bytes_accessed=moved, transcendentals=0)


def per_device(
    swaps,
    features,
    occupancy,
    w_spatial,
    b_spatial,
    w_temporal,
    face_send,
    face_source,
    send_ahead,
    from_prior,
    send_back,
    from_later,
):
    _, bricks, edge, _, wide = features.shape
    slabs = face_send.shape[1] // 2
    slots = send_ahead.shape[1]
    rows = bricks * edge * edge
    depth = w_spatial.shape[2]
    shape = jax.ShapeDtypeStruct
    space_first, space_second, frame_first, frame_second = swaps
    parcel = shape((slabs * (edge + 4) * 8, 2 * LANES), BF16)
    field = shape((bricks + 1, edge, edge, wide), F32)
    arguments = (
        face_send,
        face_source,
        send_ahead,
        from_prior,
        send_back,
        from_later,
        occupancy,
        features,
    )
    table, rolled, mask, parcel_a, parcel_b = pl.pallas_call(
        pack_kernel,
        name="pack",
        out_shape=(shape((1, LANES), jnp.int32), field, shape((rows, wide), F32), parcel, parcel),
        in_specs=[HBM] * 8,
        out_specs=(SMEM, VMEM, VMEM, VMEM, VMEM),
        scratch_shapes=[pltpu.SMEM(a.shape, a.dtype) for a in arguments[:6]]
        + [pltpu.VMEM(a.shape, a.dtype) for a in arguments[6:]]
        + [pltpu.SemaphoreType.DMA((8,))],
        compiler_params=pltpu.CompilerParams(vmem_limit_bytes=8 << 20),
        cost_estimate=cost(10**8, 10**6),
    )(*in_hbm(*arguments))
    space_a = lax.ppermute(parcel_a, AXES, space_first)
    space_b = lax.ppermute(parcel_b, AXES, space_second)

    half_wide = wide // 2
    band = shape((48 * depth, 2 * LANES), BF16)
    pad_rows = (edge + 2) * bricks * edge
    hidden = shape((bricks, edge, edge, half_wide), BF16)
    sent = shape((slots, edge, edge, half_wide), BF16)
    rolled2, pad2, band1, band2, bias2, middle, parcel_a, parcel_b = pl.pallas_call(
        functools.partial(inner_kernel, slabs),
        name="inner",
        out_shape=(
            field,
            shape((3, pad_rows, wide - LANES), BF16),
            band,
            band,
            shape((2, LANES), F32),
            hidden,
            sent,
            sent,
        ),
        in_specs=[SMEM, VMEM, VMEM, HBM, HBM],
        out_specs=(VMEM,) * 8,
        scratch_shapes=[
            pltpu.VMEM(w_spatial.shape, BF16),
            pltpu.VMEM(b_spatial.shape, F32),
            pltpu.VMEM((3, pad_rows, wide + LANES), BF16),
            pltpu.SemaphoreType.DMA((2,)),
        ],
        compiler_params=pltpu.CompilerParams(vmem_limit_bytes=24 << 20),
        cost_estimate=cost(10**9, 4 * 10**6),
    )(table, rolled, mask, *in_hbm(w_spatial, b_spatial))
    middle_a = lax.ppermute(parcel_a, AXES, frame_first)
    middle_b = lax.ppermute(parcel_b, AXES, frame_second)

    edges, parcel_a, parcel_b = pl.pallas_call(
        border_kernel,
        name="border",
        out_shape=(hidden, sent, sent),
        in_specs=[SMEM] + [VMEM] * 9,
        out_specs=(VMEM,) * 3,
        scratch_shapes=[
            pltpu.VMEM((bricks + 1 + slabs, edge, edge, 2 * LANES), F32),
            pltpu.VMEM((3, (edge + 2) * 32 * slabs, 2 * LANES), BF16),
            pltpu.VMEM((3, pad_rows, 2 * LANES), BF16),
        ],
        compiler_params=pltpu.CompilerParams(vmem_limit_bytes=16 << 20),
        cost_estimate=cost(5 * 10**8, 2 * 10**6),
    )(table, rolled, mask, rolled2, pad2, band1, band2, bias2, space_a, space_b)
    edge_a = lax.ppermute(parcel_a, AXES, frame_first)
    edge_b = lax.ppermute(parcel_b, AXES, frame_second)

    out_shape = shape(features.shape, BF16)
    out, band = pl.pallas_call(
        functools.partial(middle_out_kernel, slabs),
        name="middle_out",
        out_shape=(out_shape, shape((6 * depth, LANES), BF16)),
        in_specs=[SMEM] + [VMEM] * 5 + [HBM, pl.BlockSpec(memory_space=pl.ANY)],
        out_specs=(HBM, VMEM),
        scratch_shapes=[
            pltpu.VMEM(w_temporal.shape, BF16),
            pltpu.VMEM(hidden.shape, BF16),
            pltpu.SemaphoreType.DMA,
            pltpu.SemaphoreType.DMA((bricks,)),
        ],
        compiler_params=pltpu.CompilerParams(vmem_limit_bytes=8 << 20),
        cost_estimate=cost(10**8, 10**6),
    )(table, rolled, mask, middle, middle_a, middle_b, *in_hbm(w_temporal), edges)
    return pl.pallas_call(
        functools.partial(edge_out_kernel, slabs),
        name="edge_out",
        out_shape=out_shape,
        in_specs=[SMEM] + [VMEM] * 6 + [HBM],
        out_specs=HBM,
        scratch_shapes=[
            pltpu.VMEM(hidden.shape, BF16),
            pltpu.SemaphoreType.DMA((2 * bricks,)),
        ],
        input_output_aliases={7: 0},
        compiler_params=pltpu.CompilerParams(vmem_limit_bytes=8 << 20),
        cost_estimate=cost(10**8, 10**6),
    )(table, rolled, mask, edges, edge_a, edge_b, band, out)


def solution(mesh):
    swaps = swap_pairs(mesh.shape["space"], mesh.shape["frame"])
    in_specs = (
        P("frame", "space", None, None, None),
        P("frame", "space", None),
        P(),
        P(),
        P(),
        P("frame", "space"),
        P("frame", "space", None),
        P("frame", "space"),
        P("frame", "space"),
        P("frame", "space"),
        P("frame", "space"),
    )
    out_specs = P("frame", "space", None, None, None)
    return jax.shard_map(
        functools.partial(per_device, swaps),
        mesh=mesh,
        in_specs=in_specs,
        out_specs=out_specs,
        check_vma=False,
    )
```

time: 299 us -> 20.5 us (0.07); the launches traced: 296 us -> 20.3 us
  local copies, waits for them, and re-layouts: 243 us -> 0 us
  matrix products: 20.3 us -> 0 us
  Pallas kernels: 0 us -> 12.1 us
  other arithmetic: 11 us -> 0 us
  starting transfers between devices: 16.6 us -> 7.24 us
    while x132 -> x0, local copies, waits for them, and re-layouts: 83.6 us -> none
    another operation x145 -> x0, local copies, waits for them, and re-layouts: 67.7 us -> none  [the longest x112 61.4 us: one_group(): jnp.stack(shifted, axis=1)]
    scatter x14 -> x0, local copies, waits for them, and re-layouts: 67.1 us -> none  [the longest x2 20.2 us: padded_block(): padded.at[:, inner, inner, (edge_len + 1) * channels:wide_cols]]
    dot_general x7 -> x0, matrix products: 20.3 us -> none  [the longest x4 19.3 us: one_group(): jnp.einsum('btzyxc,tcd->bzyxd', columns, weights, preferred_element_type=...]
    pallas_call x0 -> x5, Pallas kernels: none -> 12.1 us  [the longest x1 4.43 us: per_device(): pl.pallas_call(functools.partial(inner_kernel, slabs), name='inner', out_...]
    slice x21 -> x0, local copies, waits for them, and re-layouts: 9.6 us -> none  [the longest x8 8.27 us: one_group(): piece_block[:, depth_off:depth_off + edge_len, row_off:row_off + edge_len...]
    ppermute x6, starting transfers between devices: 16.6 us -> 7.24 us  [the longest x1 2.64 us: per_device(): space_b = lax.ppermute(parcel_b, AXES, space_second)]
    gather x8 -> x0, local copies, waits for them, and re-layouts: 6.36 us -> none  [the longest x1 1.51 us: per_device(): back_rows = hidden[send_back[0]]]
  transfers between devices with their start and end apart: 6 -> 6, of which waited for: 2 -> 1; matrix products, arithmetic and copies ran while one was open for 5% -> 0% of each run, Pallas kernels for 0% -> 44%
where the time goes in v2:
time: 20.5 us; the launch traced here: 20.3 us
  Pallas kernels  12.1 us (59%)
  starting transfers between devices  7.24 us (35%)
  waiting for transfers between devices  0.9 us (4%)
    pallas_call x1, Pallas kernels, per_device(): pl.pallas_call(functools.partial(inner_kernel, slabs), name='inner', out_...  4.43 us
    ppermute x1, starting transfers between devices, per_device(): space_b = lax.ppermute(parcel_b, AXES, space_second)  2.64 us
    ppermute x1, starting transfers between devices, per_device(): edge_a = lax.ppermute(parcel_a, AXES, frame_first)  2.34 us
    pallas_call x1, Pallas kernels, per_device(): pl.pallas_call(functools.partial(middle_out_kernel, slabs), name='middle_...  2.33 us
    pallas_call x1, Pallas kernels, per_device(): pl.pallas_call(border_kernel, name='border', out_shape=(hidden, sent, sen...  2.1 us
    pallas_call x1, Pallas kernels, per_device(): pl.pallas_call(pack_kernel, name='pack', out_shape=(shape((1, LANES), jnp...  1.77 us
    pallas_call x1, Pallas kernels, per_device(): pl.pallas_call(functools.partial(edge_out_kernel, slabs), name='edge_out'...  1.49 us
    ppermute x1, starting transfers between devices, per_device(): middle_b = lax.ppermute(parcel_b, AXES, frame_second)  1.3 us
  transfers between devices with their start and end apart: 6, of which 1 were waited for; matrix products, arithmetic and copies ran while one was open for 0% of the time, Pallas kernels for 44%

profile of v2, /device:TPU:0, one launch (start us, length us, event | category | flops | bytes accessed | tf_op | source)
XLA Modules:
  0.0 20.3 jit_solution(18287470008363347066)
XLA Ops:
  0.0 1.8 %pack.1 = (s32[1,128]{1,0:T(1,128)S(1)}, f32[5,8,8,512]{3,2,1,0:T(8,128)S(1)}, f32[256,512]{1,0:T(8,128)S(1)}, bf16[96,256]{1,0:T(8,128)(2,1)S(1)}, bf16[96,256]{1,0:T(8,128)(2,1)S(1)}) custom-call(s32[1,2]{1,0:T(1,128)} %refs_0_.1, s32[1,4,6]{2,1,0:T(4,128)} %refs_1_.1, s32[1,3]{1,0:T(1,128)} %refs_2_.1, s32[1,4]{1,0:T(1,128)} %refs_3_.1, s32[1,3]{1,0:T(1,128)} %refs_4_.1, ...), custom_call_target="tpu_custom_call" | custom-call | flops 100000000 | bytes 1000000 | tf_op jit(solution)/shard_map/pack/pallas_call | solution.py:686
  1.8 0.6 %collective-permute-start = (bf16[96,256]{1,0:T(8,128)(2,1)S(1)}, bf16[96,256]{1,0:T(8,128)(2,1)S(1)}, u32[]{:S(2)}, u32[]{:S(2)}) collective-permute-start(bf16[96,256]{1,0:T(8,128)(2,1)S(1)} %get-tuple-element.31), channel_id=1, source_target_pairs={{0,4},{1,5},{2,6},{3,7},{4,0},{5,1},{6,2},{7,3},{8,12},{9,13},{10,... | collective-permute-start | bytes 147464 | tf_op jit(solution)/shard_map/ppermute | solution.py:698
  2.3 2.6 %collective-permute-start.1 = (bf16[96,256]{1,0:T(8,128)(2,1)S(1)}, bf16[96,256]{1,0:T(8,128)(2,1)S(1)}, u32[]{:S(2)}, u32[]{:S(2)}) collective-permute-start(bf16[96,256]{1,0:T(8,128)(2,1)S(1)} %get-tuple-element.32), channel_id=1, source_target_pairs={{0,1},{1,0},{2,3},{3,2},{4,8},{5,9},{6,10},{7,11},{8,4},{9,5},{10,... | collective-permute-start | bytes 147464 | tf_op jit(solution)/shard_map/ppermute | solution.py:699
  5.0 4.4 %inner.1 = (f32[5,8,8,512]{3,2,1,0:T(8,128)S(1)}, bf16[3,320,384]{2,1,0:T(8,128)(2,1)S(1)}, bf16[3072,256]{1,0:T(8,128)(2,1)S(1)}, bf16[3072,256]{1,0:T(8,128)(2...) custom-call(s32[1,128]{1,0:T(1,128)S(1)} %get-tuple-element.23.table, ...), custom_call_target="tpu_custom_call" | custom-call | flops 1000000000 | bytes 4000000 | tf_op jit(solution)/shard_map/inner/pallas_call | solution.py:706
  9.4 0.1 collective-permute-start.4
  9.5 1.3 %collective-permute-start.5 = (bf16[3,8,8,256]{3,2,1,0:T(8,128)(2,1)S(1)}, bf16[3,8,8,256]{3,2,1,0:T(8,128)(2,1)S(1)}, u32[]{:S(2)}, u32[]{:S(2)}) collective-permute-start(bf16[3,8,8,256]{3,2,1,0:T(8,128)(2,1)S(1)} %get-tuple-element.38), channel_id=1, source_target_pairs={{0,4},{1,2},{2,1},{3,7},{4,0},{5,6},{6,5},{7,3},{8,12},{9,10},{10,... | collective-permute-start | bytes 294920 | tf_op jit(solution)/shard_map/ppermute | solution.py:731
  10.8 0.0 collective-permute-done.ra_ref
  10.8 0.0 collective-permute-done.1.rb_ref
  10.8 2.1 %border.1 = (bf16[4,8,8,256]{3,2,1,0:T(8,128)(2,1)S(1)}, bf16[3,8,8,256]{3,2,1,0:T(8,128)(2,1)S(1)}, bf16[3,8,8,256]{3,2,1,0:T(8,128)(2,1)S(1)}) custom-call(s32[1,128]{1,0:T(1,128)S(1)} %get-tuple-element.23.table_ref, f32[5,8,8,512]{3,2,1,0:T(8,128)S(1)} %get-tuple-element.24.rt_ref, f32[256,512]{1,0:T(8,128)S(1)} %get-tuple-element.25.mask_ref, ...), custom_call_target="tpu_custom_call" | custom-call | flops 500000000 | bytes 2000000 | tf_op jit(solution)/shard_map/border/pallas_call | solution.py:733
  12.9 2.3 %collective-permute-start.2 = (bf16[3,8,8,256]{3,2,1,0:T(8,128)(2,1)S(1)}, bf16[3,8,8,256]{3,2,1,0:T(8,128)(2,1)S(1)}, u32[]{:S(2)}, u32[]{:S(2)}) collective-permute-start(bf16[3,8,8,256]{3,2,1,0:T(8,128)(2,1)S(1)} %get-tuple-element.34), channel_id=1, source_target_pairs={{0,1},{1,0},{2,3},{3,2},{4,5},{5,4},{6,7},{7,6},{8,9},{9,8},{10,11... | collective-permute-start | bytes 294920 | tf_op jit(solution)/shard_map/ppermute | solution.py:747
  15.3 0.3 %collective-permute-start.3 = (bf16[3,8,8,256]{3,2,1,0:T(8,128)(2,1)S(1)}, bf16[3,8,8,256]{3,2,1,0:T(8,128)(2,1)S(1)}, u32[]{:S(2)}, u32[]{:S(2)}) collective-permute-start(bf16[3,8,8,256]{3,2,1,0:T(8,128)(2,1)S(1)} %get-tuple-element.35), channel_id=1, source_target_pairs={{0,4},{1,2},{2,1},{3,7},{4,0},{5,6},{6,5},{7,3},{8,12},{9,10},{10,... | collective-permute-start | bytes 294920 | tf_op jit(solution)/shard_map/ppermute | solution.py:748
  15.6 0.0 collective-permute-done.4.ga_ref
  15.6 0.0 collective-permute-done.5.gb_ref
  15.6 2.3 %middle_out.1 = (bf16[1,4,8,8,512]{4,3,2,1,0:T(8,128)(2,1)}, bf16[384,128]{1,0:T(8,128)(2,1)S(1)}) custom-call(s32[1,128]{1,0:T(1,128)S(1)} %get-tuple-element.23.table_ref, f32[5,8,8,512]{3,2,1,0:T(8,128)S(1)} %get-tuple-element.24.rt_ref, f32[256,512]{1,0:T(8,128)S(1)} %get-tuple-element.25.mask_ref, bf16[4,8,8,256]{3,2,1,0:T(8,128)(2,1)S(1)} %get-tuple-element.36.hid_ref, ...), custom_call_target="tpu_custom_call" | custom-call | flops 100000000 | bytes 1000000 | tf_op jit(solution)/shard_map/middle_out/pallas_call | solution.py:751
  17.9 0.9 %collective-permute-done.2.ga_ref = bf16[3,8,8,256]{3,2,1,0:T(8,128)(2,1)S(1)} collective-permute-done((bf16[3,8,8,256]{3,2,1,0:T(8,128)(2,1)S(1)}, bf16[3,8,8,256]{3,2,1,0:T(8,128)(2,1)S(1)}, u32[]{:S(2)}, u32[]{:S(2)}) %collective-permute-start.2) | collective-permute-done | bytes 98336 | tf_op jit(solution)/shard_map/ppermute | solution.py:747
  18.8 0.0 collective-permute-done.3.gb_ref
  18.8 1.5 %edge_out.1 = bf16[1,4,8,8,512]{4,3,2,1,0:T(8,128)(2,1)} custom-call(s32[1,128]{1,0:T(1,128)S(1)} %get-tuple-element.23.table_ref, f32[5,8,8,512]{3,2,1,0:T(8,128)S(1)} %get-tuple-element.24.rt_ref, f32[256,512]{1,0:T(8,128)S(1)} %get-tuple-element.25.mask_ref, ...), custom_call_target="tpu_custom_call", output_to_operand_aliasing={{}: (7, {})} | custom-call | flops 100000000 | bytes 1000000 | tf_op jit(solution)/shard_map/edge_out/pallas_call | solution.py:766
Async XLA Ops:
  1.8 9.0 %collective-permute-start = (bf16[96,256]{1,0:T(8,128)(2,1)S(1)}, bf16[96,256]{1,0:T(8,128)(2,1)S(1)}, u32[]{:S(2)}, u32[]{:S(2)}) collective-permute-start(bf16[96,256]{1,0:T(8,128)(2,1)S(1)} %get-tuple-element.31), channel_id=1, source_target_pairs={{0,4},{1,5},{2,6},{3,7},{4,0},{5,1},{6,2},{7,3},{8,12},{9,13},{10,... | collective-permute-start | bytes 147464 | tf_op jit(solution)/shard_map/ppermute | solution.py:698
  2.3 8.5 %collective-permute-start.1 = (bf16[96,256]{1,0:T(8,128)(2,1)S(1)}, bf16[96,256]{1,0:T(8,128)(2,1)S(1)}, u32[]{:S(2)}, u32[]{:S(2)}) collective-permute-start(bf16[96,256]{1,0:T(8,128)(2,1)S(1)} %get-tuple-element.32), channel_id=1, source_target_pairs={{0,1},{1,0},{2,3},{3,2},{4,8},{5,9},{6,10},{7,11},{8,4},{9,5},{10,... | collective-permute-start | bytes 147464 | tf_op jit(solution)/shard_map/ppermute | solution.py:699
  9.4 6.2 %collective-permute-start.4 = (bf16[3,8,8,256]{3,2,1,0:T(8,128)(2,1)S(1)}, bf16[3,8,8,256]{3,2,1,0:T(8,128)(2,1)S(1)}, u32[]{:S(2)}, u32[]{:S(2)}) collective-permute-start(bf16[3,8,8,256]{3,2,1,0:T(8,128)(2,1)S(1)} %get-tuple-element.37), channel_id=1, source_target_pairs={{0,1},{1,0},{2,3},{3,2},{4,5},{5,4},{6,7},{7,6},{8,9},{9,8},{10,11... | collective-permute-start | bytes 294920 | tf_op jit(solution)/shard_map/ppermute | solution.py:730
  9.5 6.1 %collective-permute-start.5 = (bf16[3,8,8,256]{3,2,1,0:T(8,128)(2,1)S(1)}, bf16[3,8,8,256]{3,2,1,0:T(8,128)(2,1)S(1)}, u32[]{:S(2)}, u32[]{:S(2)}) collective-permute-start(bf16[3,8,8,256]{3,2,1,0:T(8,128)(2,1)S(1)} %get-tuple-element.38), channel_id=1, source_target_pairs={{0,4},{1,2},{2,1},{3,7},{4,0},{5,6},{6,5},{7,3},{8,12},{9,10},{10,... | collective-permute-start | bytes 294920 | tf_op jit(solution)/shard_map/ppermute | solution.py:731
  12.9 5.9 %collective-permute-start.2 = (bf16[3,8,8,256]{3,2,1,0:T(8,128)(2,1)S(1)}, bf16[3,8,8,256]{3,2,1,0:T(8,128)(2,1)S(1)}, u32[]{:S(2)}, u32[]{:S(2)}) collective-permute-start(bf16[3,8,8,256]{3,2,1,0:T(8,128)(2,1)S(1)} %get-tuple-element.34), channel_id=1, source_target_pairs={{0,1},{1,0},{2,3},{3,2},{4,5},{5,4},{6,7},{7,6},{8,9},{9,8},{10,11... | collective-permute-start | bytes 294920 | tf_op jit(solution)/shard_map/ppermute | solution.py:747
  15.3 3.6 %collective-permute-start.3 = (bf16[3,8,8,256]{3,2,1,0:T(8,128)(2,1)S(1)}, bf16[3,8,8,256]{3,2,1,0:T(8,128)(2,1)S(1)}, u32[]{:S(2)}, u32[]{:S(2)}) collective-permute-start(bf16[3,8,8,256]{3,2,1,0:T(8,128)(2,1)S(1)} %get-tuple-element.35), channel_id=1, source_target_pairs={{0,4},{1,2},{2,1},{3,7},{4,0},{5,6},{6,5},{7,3},{8,12},{9,10},{10,... | collective-permute-start | bytes 294920 | tf_op jit(solution)/shard_map/ppermute | solution.py:748

commit v3 on v2

--- a/solution.py
+++ b/solution.py
@@ -74,6 +74,9 @@
             self.ref[0, self.at_ahead + i] = ahead_ref[0, i]
             self.ref[0, self.at_back + i] = back_ref[0, i]
 
+    def live(self):
+        return self.ref[0, self.at_ahead] >= 0
+
     def has(self, side):
         return self.ref[0, self.at_send + side * self.slabs] >= 0
 
@@ -114,11 +117,12 @@
 
 
 def pack_kernel(*refs):
-    sources, (table_ref, rt_ref, mask_ref, pa_ref, pb_ref) = refs[:8], refs[8:13]
-    held, sems = refs[13:21], refs[21]
+    sources, (table_ref, rt_ref, mask_ref, pa_ref, pb_ref) = refs[:11], refs[11:16]
+    held, sems = refs[19:27] + refs[16:19], refs[27]
     copies = [pltpu.make_async_copy(s, d, sems.at[i]) for i, (s, d) in enumerate(zip(sources, held))]
     for copy in copies:
         copy.start()
+    copies, late_copies, held = copies[:8], copies[8:], held[:8]
     occ_ref, feat_ref = held[6:]
     _, bricks, edge, _, wide = feat_ref.shape
     channels = wide // edge
@@ -185,6 +189,8 @@
             at = slice(k * size, (k + 1) * size)
             pa_ref[at, tile_of(c)] = jnp.where(odd, down[c], up[c]).astype(BF16)
             pb_ref[at, tile_of(c)] = jnp.where(odd, up[c], down[c]).astype(BF16)
+    for copy in late_copies:
+        copy.wait()
 
 
 def fill_band(w_ref, layer, band_ref):
@@ -264,8 +270,12 @@
                         [window(dy, (2 * zz + dz) * rows, rows) for zz in range(edge // 2)], axis=0
                     )
                 )
-        blocks.append(jnp.concatenate(parts, axis=1))
-    total = jnp.dot(jnp.concatenate(blocks, axis=0), band_ref[...], preferred_element_type=F32)
+        blocks.append(parts)
+    total = 0.0
+    for first in (0, 6):
+        lhs = [jnp.concatenate(parts[first : first + 6], axis=1) for parts in blocks]
+        band = band_ref[first * 2 * LANES : (first + 6) * 2 * LANES, :]
+        total = total + jnp.dot(jnp.concatenate(lhs, axis=0), band, preferred_element_type=F32)
 
     def result(window, z):
         at = (window * (edge // 2) + z // 2) * rows
@@ -279,8 +289,8 @@
     table_ref,
     rt_ref,
     mask_ref,
-    w_hbm,
-    bias_hbm,
+    w_ref,
+    bias_ref,
     rt2_ref,
     pad2_ref,
     band1_ref,
@@ -289,17 +299,8 @@
     mid_ref,
     fa_ref,
     fb_ref,
-    w_ref,
-    bias_ref,
     pad_ref,
-    sems,
 ):
-    copies = [
-        pltpu.make_async_copy(w_hbm, w_ref, sems.at[0]),
-        pltpu.make_async_copy(bias_hbm, bias_ref, sems.at[1]),
-    ]
-    for copy in copies:
-        copy.start()
     bricks, edge, _, wide = rt_ref.shape
     bricks -= 1
     tiles = wide // LANES
@@ -321,8 +322,6 @@
         return [None] + load(rt_ref, brick, z) + [None]
 
     fill_padded(pad_ref, tables, edge, own, rim, [(k, k + 1) for k in range(tiles + 1)])
-    for copy in copies:
-        copy.wait()
     fill_band(w_ref, 0, band1_ref)
     for layer in range(2):
         row = bias_ref[layer : layer + 1, :]
@@ -334,6 +333,7 @@
 
         return window
 
+    fill_band(w_ref, 1, band2_ref)
     result = convolve([window_of(pad_ref, i) for i in range(tiles)], rows, edge, band1_ref)
     bias = bias2_ref[0:1, :]
     for i in range(tiles):
@@ -344,20 +344,21 @@
                 rt2_ref[b, z, :, tile_of(i)] = value[b * edge : (b + 1) * edge]
     rt2_ref[bricks] = jnp.zeros_like(rt2_ref[bricks])
 
-    def field(b, z):
-        return load(rt2_ref, b, z)
-
-    fill_padded(pad2_ref, tables, edge, field, field, [(k, k + 1) for k in range(tiles - 1)])
-    fill_band(w_ref, 1, band2_ref)
-    result = convolve([window_of(pad2_ref, i) for i in range(tiles - 2)], rows, edge, band2_ref)
-    bias = bias2_ref[1:2, :]
-    for i in range(tiles - 2):
-        for z in range(edge):
-            keep = mask_ref[z * rows : (z + 1) * rows, tile_of(i + 1)]
-            value = jnp.maximum(result(i, z) + bias, 0.0) * keep
-            for b in range(bricks):
-                mid_ref[b, z, :, tile_of(i)] = value[b * edge : (b + 1) * edge].astype(BF16)
-    choose_parcels(tables, mid_ref, fa_ref, fb_ref)
+    @pl.when(tables.live())
+    def _():
+        def field(b, z):
+            return load(rt2_ref, b, z)
+
+        fill_padded(pad2_ref, tables, edge, field, field, [(k, k + 1) for k in range(tiles - 1)])
+        result = convolve([window_of(pad2_ref, i) for i in range(tiles - 2)], rows, edge, band2_ref)
+        bias = bias2_ref[1:2, :]
+        for i in range(tiles - 2):
+            for z in range(edge):
+                keep = mask_ref[z * rows : (z + 1) * rows, tile_of(i + 1)]
+                value = jnp.maximum(result(i, z) + bias, 0.0) * keep
+                for b in range(bricks):
+                    mid_ref[b, z, :, tile_of(i)] = value[b * edge : (b + 1) * edge].astype(BF16)
+        choose_parcels(tables, mid_ref, fa_ref, fb_ref)
 
 
 def choose_parcels(tables, field_ref, fa_ref, fb_ref):
@@ -481,86 +482,67 @@
 
     outer = [(tables.rim(b, 0), tables.rim(b, 1)) for b in range(bricks)]
 
-    def own(b, z):
-        left, right = edge_ref[outer[b][0], z, :, tile_of(1)], edge_ref[outer[b][1], z, :, tile_of(0)]
-        return [left, edge_ref[b, z, :, tile_of(0)], edge_ref[b, z, :, tile_of(1)], right]
-
-    def rim(brick, z):
-        return [None, edge_ref[brick, z, :, tile_of(0)], edge_ref[brick, z, :, tile_of(1)], None]
-
-    fill_padded(pad_ref, tables, edge, own, rim, [(0, 1), (2, 3)])
-
-    def low_window(dy, at, n):
-        return jnp.concatenate(
-            [pad_ref[dy, at : at + n, tile_of(0)], pad2_ref[dy, at : at + n, tile_of(0)]], axis=1
-        )
-
-    def high_window(dy, at, n):
-        return jnp.concatenate(
-            [pad2_ref[dy, at : at + n, tile_of(tiles - 2)], pad_ref[dy, at : at + n, tile_of(1)]],
-            axis=1,
-        )
-
-    result = convolve([low_window, high_window], rows, edge, band2_ref)
-    bias = bias2_ref[1:2, :]
-    for side in range(2):
-        for z in range(edge):
-            keep = mask_ref[z * rows : (z + 1) * rows, ends[side]]
-            value = jnp.maximum(result(side, z) + bias, 0.0) * keep
-            for b in range(bricks):
-                out_ref[b, z, :, tile_of(side)] = value[b * edge : (b + 1) * edge].astype(BF16)
-    choose_parcels(tables, out_ref, fa_ref, fb_ref)
-
-
-def temporal_part(
-    tables, tiles, rt_ref, mask_ref, hid_ref, ga_ref, gb_ref, band, out_hbm, held_ref, sems
-):
+    @pl.when(tables.live())
+    def _():
+        def own(b, z):
+            left, right = edge_ref[outer[b][0], z, :, tile_of(1)], edge_ref[outer[b][1], z, :, tile_of(0)]
+            return [left, edge_ref[b, z, :, tile_of(0)], edge_ref[b, z, :, tile_of(1)], right]
+
+        def rim(brick, z):
+            return [None, edge_ref[brick, z, :, tile_of(0)], edge_ref[brick, z, :, tile_of(1)], None]
+
+        fill_padded(pad_ref, tables, edge, own, rim, [(0, 1), (2, 3)])
+
+        def low_window(dy, at, n):
+            return jnp.concatenate(
+                [pad_ref[dy, at : at + n, tile_of(0)], pad2_ref[dy, at : at + n, tile_of(0)]], axis=1
+            )
+
+        def high_window(dy, at, n):
+            return jnp.concatenate(
+                [pad2_ref[dy, at : at + n, tile_of(tiles - 2)], pad_ref[dy, at : at + n, tile_of(1)]],
+                axis=1,
+            )
+
+        result = convolve([low_window, high_window], rows, edge, band2_ref)
+        bias = bias2_ref[1:2, :]
+        for side in range(2):
+            for z in range(edge):
+                keep = mask_ref[z * rows : (z + 1) * rows, ends[side]]
+                value = jnp.maximum(result(side, z) + bias, 0.0) * keep
+                for b in range(bricks):
+                    out_ref[b, z, :, tile_of(side)] = value[b * edge : (b + 1) * edge].astype(BF16)
+        choose_parcels(tables, out_ref, fa_ref, fb_ref)
+
+
+def temporal_part(tables, tiles, rt_ref, mask_ref, hid_ref, ga_ref, gb_ref, band, b, put):
     bricks, edge, _, part = hid_ref.shape
     odd = lax.rem(lax.axis_index("frame"), 2) == 1
 
     def flat(block):
         return block.astype(F32).reshape(edge * edge, part)
 
-    copies = []
-    for b in range(bricks):
-        prior = tables.ref[0, tables.at_prior + b]
-        later = tables.ref[0, tables.at_later + b]
-        at_prior = jnp.clip(prior, 0, tables.slots - 1)
-        at_later = jnp.clip(later, 0, tables.slots - 1)
-        before = flat(jnp.where(odd, ga_ref[at_prior], gb_ref[at_prior]))
-        after = flat(jnp.where(odd, gb_ref[at_later], ga_ref[at_later]))
-        before = jnp.where(prior >= 0, before, 0.0).astype(BF16)
-        after = jnp.where(later >= 0, after, 0.0).astype(BF16)
-        here = flat(hid_ref[b]).astype(BF16)
-        lhs = [
-            jnp.concatenate([f[:, tile_of(k)] for f in (before, here, after)], axis=1)
-            for k in range(len(tiles))
-        ]
-        total = jnp.dot(jnp.concatenate(lhs, axis=0), band, preferred_element_type=F32)
-        for k, tile in enumerate(tiles):
-            for z in range(edge):
-                at = (z * bricks + b) * edge
-                keep = mask_ref[at : at + edge, tile_of(tile)]
-                row = k * edge * edge + z * edge
-                sums = half(rt_ref[b, z, :, tile_of(tile)]) + total[row : row + edge]
-                held_ref[b, z, :, tile_of(k)] = (keep * sums).astype(BF16)
-        done = 0
-        while done < len(tiles):
-            run = 1
-            while done + run < len(tiles) and tiles[done + run] == tiles[done] + run:
-                run += 1
-            first = tiles[done]
-            copies.append(
-                pltpu.make_async_copy(
-                    held_ref.at[b, :, :, done * LANES : (done + run) * LANES],
-                    out_hbm.at[0, b, :, :, first * LANES : (first + run) * LANES],
-                    sems.at[len(copies)],
-                )
-            )
-            copies[-1].start()
-            done += run
-    for copy in copies:
-        copy.wait()
+    prior = tables.ref[0, tables.at_prior + b]
+    later = tables.ref[0, tables.at_later + b]
+    at_prior = jnp.clip(prior, 0, tables.slots - 1)
+    at_later = jnp.clip(later, 0, tables.slots - 1)
+    before = flat(jnp.where(odd, ga_ref[at_prior], gb_ref[at_prior]))
+    after = flat(jnp.where(odd, gb_ref[at_later], ga_ref[at_later]))
+    before = jnp.where(prior >= 0, before, 0.0).astype(BF16)
+    after = jnp.where(later >= 0, after, 0.0).astype(BF16)
+    here = flat(hid_ref[b]).astype(BF16)
+    lhs = [
+        jnp.concatenate([f[:, tile_of(k)] for f in (before, here, after)], axis=1)
+        for k in range(len(tiles))
+    ]
+    total = jnp.dot(jnp.concatenate(lhs, axis=0), band, preferred_element_type=F32)
+    for k, tile in enumerate(tiles):
+        for z in range(edge):
+            at = (z * bricks + b) * edge
+            keep = mask_ref[at : at + edge, tile_of(tile)]
+            row = k * edge * edge + z * edge
+            sums = half(rt_ref[b, z, :, tile_of(tile)]) + total[row : row + edge]
+            put(b, z, k, (keep * sums).astype(BF16))
 
 
 def middle_out_kernel(
@@ -571,18 +553,11 @@
     hid_ref,
     ga_ref,
     gb_ref,
-    w_hbm,
+    w_ref,
     order_ref,
-    out_hbm,
+    out_ref,
     band_ref,
-    w_ref,
-    held_ref,
-    sem,
-    sems,
 ):
-    copy = pltpu.make_async_copy(w_hbm, w_ref, sem)
-    copy.start()
-    copy.wait()
     depth = w_ref.shape[1]
     blank = jnp.zeros((depth, depth), BF16)
     for i in range(3):
@@ -591,19 +566,24 @@
         band_ref[at + depth : at + 2 * depth, :] = jnp.concatenate([blank, w_ref[i]], axis=1)
     tables = Tables(table_ref, rt_ref.shape[0] - 1, slabs, ga_ref.shape[0])
     tiles = rt_ref.shape[-1] // LANES
-    temporal_part(
-        tables,
-        list(range(1, tiles - 1)),
-        rt_ref,
-        mask_ref,
-        hid_ref,
-        ga_ref,
-        gb_ref,
-        band_ref[...],
-        out_hbm,
-        held_ref,
-        sems,
-    )
+
+    def put(b, z, k, value):
+        out_ref[b, z, :, tile_of(k)] = value
+
+    band = band_ref[...]
+    for b in range(tables.bricks):
+        temporal_part(
+            tables,
+            list(range(1, tiles - 1)),
+            rt_ref,
+            mask_ref,
+            hid_ref,
+            ga_ref,
+            gb_ref,
+            band,
+            b,
+            put,
+        )
 
 
 def edge_out_kernel(
@@ -615,26 +595,38 @@
     ga_ref,
     gb_ref,
     band_ref,
-    before_hbm,
+    middle_ref,
     out_hbm,
     held_ref,
     sems,
 ):
     tables = Tables(table_ref, rt_ref.shape[0] - 1, slabs, ga_ref.shape[0])
     tiles = rt_ref.shape[-1] // LANES
-    temporal_part(
-        tables,
-        [0, tiles - 1],
-        rt_ref,
-        mask_ref,
-        hid_ref,
-        ga_ref,
-        gb_ref,
-        band_ref[...],
-        out_hbm,
-        held_ref,
-        sems,
-    )
+    wide = tiles * LANES
+    copies = [
+        pltpu.make_async_copy(
+            middle_ref, out_hbm.at[0, :, :, :, LANES : wide - LANES], sems.at[2 * tables.bricks]
+        )
+    ]
+    copies[0].start()
+
+    def put(b, z, k, value):
+        held_ref[k, b, z] = value
+
+    band = band_ref[...]
+    for b in range(tables.bricks):
+        temporal_part(
+            tables, [0, tiles - 1], rt_ref, mask_ref, hid_ref, ga_ref, gb_ref, band, b, put
+        )
+        for k, tile in enumerate((0, tiles - 1)):
+            copies.append(
+                pltpu.make_async_copy(
+                    held_ref.at[k, b], out_hbm.at[0, b, :, :, tile_of(tile)], sems.at[2 * b + k]
+                )
+            )
+            copies[-1].start()
+    for copy in copies:
+        copy.wait()
 
 
 VMEM = pl.BlockSpec(memory_space=pltpu.VMEM)
@@ -682,16 +674,20 @@
         from_later,
         occupancy,
         features,
+        w_spatial,
+        b_spatial,
+        w_temporal,
     )
-    table, rolled, mask, parcel_a, parcel_b = pl.pallas_call(
+    table, rolled, mask, parcel_a, parcel_b, w_held, b_held, wt_held = pl.pallas_call(
         pack_kernel,
         name="pack",
-        out_shape=(shape((1, LANES), jnp.int32), field, shape((rows, wide), F32), parcel, parcel),
-        in_specs=[HBM] * 8,
-        out_specs=(SMEM, VMEM, VMEM, VMEM, VMEM),
+        out_shape=(shape((1, LANES), jnp.int32), field, shape((rows, wide), F32), parcel, parcel)
+        + tuple(shape(a.shape, a.dtype) for a in arguments[8:]),
+        in_specs=[HBM] * 11,
+        out_specs=(SMEM,) + (VMEM,) * 7,
         scratch_shapes=[pltpu.SMEM(a.shape, a.dtype) for a in arguments[:6]]
-        + [pltpu.VMEM(a.shape, a.dtype) for a in arguments[6:]]
-        + [pltpu.SemaphoreType.DMA((8,))],
+        + [pltpu.VMEM(a.shape, a.dtype) for a in arguments[6:8]]
+        + [pltpu.SemaphoreType.DMA((11,))],
         compiler_params=pltpu.CompilerParams(vmem_limit_bytes=8 << 20),
         cost_estimate=cost(10**8, 10**6),
     )(*in_hbm(*arguments))
@@ -716,17 +712,12 @@
             sent,
             sent,
         ),
-        in_specs=[SMEM, VMEM, VMEM, HBM, HBM],
+        in_specs=[SMEM] + [VMEM] * 4,
         out_specs=(VMEM,) * 8,
-        scratch_shapes=[
-            pltpu.VMEM(w_spatial.shape, BF16),
-            pltpu.VMEM(b_spatial.shape, F32),
-            pltpu.VMEM((3, pad_rows, wide + LANES), BF16),
-            pltpu.SemaphoreType.DMA((2,)),
-        ],
+        scratch_shapes=[pltpu.VMEM((3, pad_rows, wide + LANES), BF16)],
         compiler_params=pltpu.CompilerParams(vmem_limit_bytes=24 << 20),
         cost_estimate=cost(10**9, 4 * 10**6),
-    )(table, rolled, mask, *in_hbm(w_spatial, b_spatial))
+    )(table, rolled, mask, w_held, b_held)
     middle_a = lax.ppermute(parcel_a, AXES, frame_first)
     middle_b = lax.ppermute(parcel_b, AXES, frame_second)
 
@@ -747,36 +738,28 @@
     edge_a = lax.ppermute(parcel_a, AXES, frame_first)
     edge_b = lax.ppermute(parcel_b, AXES, frame_second)
 
-    out_shape = shape(features.shape, BF16)
-    out, band = pl.pallas_call(
+    middle_out, band = pl.pallas_call(
         functools.partial(middle_out_kernel, slabs),
         name="middle_out",
-        out_shape=(out_shape, shape((6 * depth, LANES), BF16)),
-        in_specs=[SMEM] + [VMEM] * 5 + [HBM, pl.BlockSpec(memory_space=pl.ANY)],
-        out_specs=(HBM, VMEM),
+        out_shape=(hidden, shape((6 * depth, LANES), BF16)),
+        in_specs=[SMEM] + [VMEM] * 6 + [pl.BlockSpec(memory_space=pl.ANY)],
+        out_specs=(VMEM, VMEM),
+        compiler_params=pltpu.CompilerParams(vmem_limit_bytes=8 << 20),
+        cost_estimate=cost(10**8, 10**6),
+    )(table, rolled, mask, middle, middle_a, middle_b, wt_held, edges)
+    return pl.pallas_call(
+        functools.partial(edge_out_kernel, slabs),
+        name="edge_out",
+        out_shape=shape(features.shape, BF16),
+        in_specs=[SMEM] + [VMEM] * 7,
+        out_specs=HBM,
         scratch_shapes=[
-            pltpu.VMEM(w_temporal.shape, BF16),
-            pltpu.VMEM(hidden.shape, BF16),
-            pltpu.SemaphoreType.DMA,
-            pltpu.SemaphoreType.DMA((bricks,)),
+            pltpu.VMEM((2, bricks, edge, edge, LANES), BF16),
+            pltpu.SemaphoreType.DMA((2 * bricks + 1,)),
         ],
         compiler_params=pltpu.CompilerParams(vmem_limit_bytes=8 << 20),
         cost_estimate=cost(10**8, 10**6),
-    )(table, rolled, mask, middle, middle_a, middle_b, *in_hbm(w_temporal), edges)
-    return pl.pallas_call(
-        functools.partial(edge_out_kernel, slabs),
-        name="edge_out",
-        out_shape=out_shape,
-        in_specs=[SMEM] + [VMEM] * 6 + [HBM],
-        out_specs=HBM,
-        scratch_shapes=[
-            pltpu.VMEM(hidden.shape, BF16),
-            pltpu.SemaphoreType.DMA((2 * bricks,)),
-        ],
-        input_output_aliases={7: 0},
-        compiler_params=pltpu.CompilerParams(vmem_limit_bytes=8 << 20),
-        cost_estimate=cost(10**8, 10**6),
-    )(table, rolled, mask, edges, edge_a, edge_b, band, out)
+    )(table, rolled, mask, edges, edge_a, edge_b, band, middle_out)
 
 
 def solution(mesh):

time: 20.5 us -> 18.5 us (0.902)
  Pallas kernels: 12.1 us -> 8.68 us
  waiting for transfers between devices: 0.9 us -> 2.36 us
    pallas_call x1, Pallas kernels: 4.43 us -> 2.55 us  [per_device(): pl.pallas_call(functools.partial(inner_kernel, slabs), name='inner', out_...]
    pallas_call x1, Pallas kernels: 2.33 us -> 0.88 us  [per_device(): pl.pallas_call(functools.partial(middle_out_kernel, slabs), name='middle_...]
    ppermute x1, waiting for transfers between devices: 0.89 us -> 2.35 us  [per_device(): edge_a = lax.ppermute(parcel_a, AXES, frame_first)]
    pallas_call x1, Pallas kernels: 2.1 us -> 1.79 us  [per_device(): pl.pallas_call(border_kernel, name='border', out_shape=(hidden, sent, sen...]
  transfers between devices with their start and end apart: 6 -> 6, of which waited for: 1 -> 1; matrix products, arithmetic and copies ran while one was open for 0% -> 0% of each run, Pallas kernels for 44% -> 29%
where the time goes in v3:
time: 18.5 us; the launch traced here: 18.3 us
  Pallas kernels  8.68 us (47%)
  starting transfers between devices  7.24 us (39%)
  waiting for transfers between devices  2.36 us (13%)
    ppermute x1, starting transfers between devices, per_device(): space_b = lax.ppermute(parcel_b, AXES, space_second)  2.64 us
    pallas_call x1, Pallas kernels, per_device(): pl.pallas_call(functools.partial(inner_kernel, slabs), name='inner', out_...  2.55 us
    ppermute x1, waiting for transfers between devices, per_device(): edge_a = lax.ppermute(parcel_a, AXES, frame_first)  2.35 us
    ppermute x1, starting transfers between devices, per_device(): edge_a = lax.ppermute(parcel_a, AXES, frame_first)  2.34 us
    pallas_call x1, Pallas kernels, per_device(): pl.pallas_call(pack_kernel, name='pack', out_shape=(shape((1, LANES), jnp...  1.97 us
    pallas_call x1, Pallas kernels, per_device(): pl.pallas_call(border_kernel, name='border', out_shape=(hidden, sent, sen...  1.79 us
    pallas_call x1, Pallas kernels, per_device(): pl.pallas_call(functools.partial(edge_out_kernel, slabs), name='edge_out'...  1.5 us
    ppermute x1, starting transfers between devices, per_device(): middle_b = lax.ppermute(parcel_b, AXES, frame_second)  1.31 us
  transfers between devices with their start and end apart: 6, of which 1 were waited for; matrix products, arithmetic and copies ran while one was open for 0% of the time, Pallas kernels for 29%

profile of v3, /device:TPU:0, one launch (start us, length us, event | category | flops | bytes accessed | tf_op | source)
XLA Modules:
  0.0 18.3 jit_solution(8748964448002225791)
XLA Ops:
  0.0 2.0 %pack.1 = (s32[1,128]{1,0:T(1,128)S(1)}, f32[5,8,8,512]{3,2,1,0:T(8,128)S(1)}, f32[256,512]{1,0:T(8,128)S(1)}, bf16[96,256]{1,0:T(8,128)(2,1)S(1)}, bf16[96,256]...) custom-call(s32[1,2]{1,0:T(1,128)} %refs_0_.1, ...), custom_call_target="tpu_custom_call" | custom-call | flops 100000000 | bytes 1000000 | tf_op jit(solution)/shard_map/pack/pallas_call | solution.py:681
  2.0 0.6 %collective-permute-start = (bf16[96,256]{1,0:T(8,128)(2,1)S(1)}, bf16[96,256]{1,0:T(8,128)(2,1)S(1)}, u32[]{:S(2)}, u32[]{:S(2)}) collective-permute-start(bf16[96,256]{1,0:T(8,128)(2,1)S(1)} %get-tuple-element.36), channel_id=1, source_target_pairs={{0,4},{1,5},{2,6},{3,7},{4,0},{5,1},{6,2},{7,3},{8,12},{9,13},{10,... | collective-permute-start | bytes 147464 | tf_op jit(solution)/shard_map/ppermute | solution.py:694
  2.5 2.6 %collective-permute-start.1 = (bf16[96,256]{1,0:T(8,128)(2,1)S(1)}, bf16[96,256]{1,0:T(8,128)(2,1)S(1)}, u32[]{:S(2)}, u32[]{:S(2)}) collective-permute-start(bf16[96,256]{1,0:T(8,128)(2,1)S(1)} %get-tuple-element.37), channel_id=1, source_target_pairs={{0,1},{1,0},{2,3},{3,2},{4,8},{5,9},{6,10},{7,11},{8,4},{9,5},{10,... | collective-permute-start | bytes 147464 | tf_op jit(solution)/shard_map/ppermute | solution.py:695
  5.2 2.6 %inner.1 = (f32[5,8,8,512]{3,2,1,0:T(8,128)S(1)}, bf16[3,320,384]{2,1,0:T(8,128)(2,1)S(1)}, bf16[3072,256]{1,0:T(8,128)(2,1)S(1)}, bf16[3072,256]{1,0:T(8,128)(2...) custom-call(s32[1,128]{1,0:T(1,128)S(1)} %get-tuple-element.26.table, ...), custom_call_target="tpu_custom_call" | custom-call | flops 1000000000 | bytes 4000000 | tf_op jit(solution)/shard_map/inner/pallas_call | solution.py:702
  7.7 0.1 collective-permute-start.4
  7.8 1.3 %collective-permute-start.5 = (bf16[3,8,8,256]{3,2,1,0:T(8,128)(2,1)S(1)}, bf16[3,8,8,256]{3,2,1,0:T(8,128)(2,1)S(1)}, u32[]{:S(2)}, u32[]{:S(2)}) collective-permute-start(bf16[3,8,8,256]{3,2,1,0:T(8,128)(2,1)S(1)} %get-tuple-element.43), channel_id=1, source_target_pairs={{0,4},{1,2},{2,1},{3,7},{4,0},{5,6},{6,5},{7,3},{8,12},{9,10},{10,... | collective-permute-start | bytes 294920 | tf_op jit(solution)/shard_map/ppermute | solution.py:722
  9.1 0.0 collective-permute-done.ra_ref
  9.1 0.0 collective-permute-done.1.rb_ref
  9.1 1.8 %border.1 = (bf16[4,8,8,256]{3,2,1,0:T(8,128)(2,1)S(1)}, bf16[3,8,8,256]{3,2,1,0:T(8,128)(2,1)S(1)}, bf16[3,8,8,256]{3,2,1,0:T(8,128)(2,1)S(1)}) custom-call(s32[1,128]{1,0:T(1,128)S(1)} %get-tuple-element.26.table_ref, f32[5,8,8,512]{3,2,1,0:T(8,128)S(1)} %get-tuple-element.27.rt_ref, f32[256,512]{1,0:T(8,128)S(1)} %get-tuple-element.28.mask_ref, ...), custom_call_target="tpu_custom_call" | custom-call | flops 500000000 | bytes 2000000 | tf_op jit(solution)/shard_map/border/pallas_call | solution.py:724
  10.9 2.3 %collective-permute-start.2 = (bf16[3,8,8,256]{3,2,1,0:T(8,128)(2,1)S(1)}, bf16[3,8,8,256]{3,2,1,0:T(8,128)(2,1)S(1)}, u32[]{:S(2)}, u32[]{:S(2)}) collective-permute-start(bf16[3,8,8,256]{3,2,1,0:T(8,128)(2,1)S(1)} %get-tuple-element.39), channel_id=1, source_target_pairs={{0,1},{1,0},{2,3},{3,2},{4,5},{5,4},{6,7},{7,6},{8,9},{9,8},{10,11... | collective-permute-start | bytes 294920 | tf_op jit(solution)/shard_map/ppermute | solution.py:738
  13.3 0.3 %collective-permute-start.3 = (bf16[3,8,8,256]{3,2,1,0:T(8,128)(2,1)S(1)}, bf16[3,8,8,256]{3,2,1,0:T(8,128)(2,1)S(1)}, u32[]{:S(2)}, u32[]{:S(2)}) collective-permute-start(bf16[3,8,8,256]{3,2,1,0:T(8,128)(2,1)S(1)} %get-tuple-element.40), channel_id=1, source_target_pairs={{0,4},{1,2},{2,1},{3,7},{4,0},{5,6},{6,5},{7,3},{8,12},{9,10},{10,... | collective-permute-start | bytes 294920 | tf_op jit(solution)/shard_map/ppermute | solution.py:739
  13.6 0.0 collective-permute-done.4.ga_ref
  13.6 0.0 collective-permute-done.5.gb_ref
  13.6 0.9 %middle_out.1 = (bf16[4,8,8,256]{3,2,1,0:T(8,128)(2,1)S(1)}, bf16[384,128]{1,0:T(8,128)(2,1)S(1)}) custom-call(s32[1,128]{1,0:T(1,128)S(1)} %get-tuple-element.26.table_ref, f32[5,8,8,512]{3,2,1,0:T(8,128)S(1)} %get-tuple-element.27.rt_ref, f32[256,512]{1,0:T(8,128)S(1)} %get-tuple-element.28.mask_ref, bf16[4,8,8,256]{3,2,1,0:T(8,128)(2,1)S(1)} %get-tuple-element.41.hid_ref, ...), custom_call_target="tpu_custom_call" | custom-call | flops 100000000 | bytes 1000000 | tf_op jit(solution)/shard_map/middle_out/pallas_call | solution.py:741
  14.5 2.3 %collective-permute-done.2.ga_ref = bf16[3,8,8,256]{3,2,1,0:T(8,128)(2,1)S(1)} collective-permute-done((bf16[3,8,8,256]{3,2,1,0:T(8,128)(2,1)S(1)}, bf16[3,8,8,256]{3,2,1,0:T(8,128)(2,1)S(1)}, u32[]{:S(2)}, u32[]{:S(2)}) %collective-permute-start.2) | collective-permute-done | bytes 98336 | tf_op jit(solution)/shard_map/ppermute | solution.py:738
  16.8 0.0 collective-permute-done.3.gb_ref
  16.8 1.5 %edge_out.1 = bf16[1,4,8,8,512]{4,3,2,1,0:T(8,128)(2,1)} custom-call(s32[1,128]{1,0:T(1,128)S(1)} %get-tuple-element.26.table_ref, f32[5,8,8,512]{3,2,1,0:T(8,128)S(1)} %get-tuple-element.27.rt_ref, f32[256,512]{1,0:T(8,128)S(1)} %get-tuple-element.28.mask_ref, bf16[4,8,8,256]{3,2,1,0:T(8,128)(2,1)S(1)} %get-tuple-element.38.order_ref.hid_ref, ...), custom_call_target="tpu_custom_call" | custom-call | flops 100000000 | bytes 1000000 | tf_op jit(solution)/shard_map/edge_out/pallas_call | solution.py:750
Async XLA Ops:
  2.0 7.2 %collective-permute-start = (bf16[96,256]{1,0:T(8,128)(2,1)S(1)}, bf16[96,256]{1,0:T(8,128)(2,1)S(1)}, u32[]{:S(2)}, u32[]{:S(2)}) collective-permute-start(bf16[96,256]{1,0:T(8,128)(2,1)S(1)} %get-tuple-element.36), channel_id=1, source_target_pairs={{0,4},{1,5},{2,6},{3,7},{4,0},{5,1},{6,2},{7,3},{8,12},{9,13},{10,... | collective-permute-start | bytes 147464 | tf_op jit(solution)/shard_map/ppermute | solution.py:694
  2.5 6.6 %collective-permute-start.1 = (bf16[96,256]{1,0:T(8,128)(2,1)S(1)}, bf16[96,256]{1,0:T(8,128)(2,1)S(1)}, u32[]{:S(2)}, u32[]{:S(2)}) collective-permute-start(bf16[96,256]{1,0:T(8,128)(2,1)S(1)} %get-tuple-element.37), channel_id=1, source_target_pairs={{0,1},{1,0},{2,3},{3,2},{4,8},{5,9},{6,10},{7,11},{8,4},{9,5},{10,... | collective-permute-start | bytes 147464 | tf_op jit(solution)/shard_map/ppermute | solution.py:695
  7.7 5.9 %collective-permute-start.4 = (bf16[3,8,8,256]{3,2,1,0:T(8,128)(2,1)S(1)}, bf16[3,8,8,256]{3,2,1,0:T(8,128)(2,1)S(1)}, u32[]{:S(2)}, u32[]{:S(2)}) collective-permute-start(bf16[3,8,8,256]{3,2,1,0:T(8,128)(2,1)S(1)} %get-tuple-element.42), channel_id=1, source_target_pairs={{0,1},{1,0},{2,3},{3,2},{4,5},{5,4},{6,7},{7,6},{8,9},{9,8},{10,11... | collective-permute-start | bytes 294920 | tf_op jit(solution)/shard_map/ppermute | solution.py:721
  7.8 5.8 %collective-permute-start.5 = (bf16[3,8,8,256]{3,2,1,0:T(8,128)(2,1)S(1)}, bf16[3,8,8,256]{3,2,1,0:T(8,128)(2,1)S(1)}, u32[]{:S(2)}, u32[]{:S(2)}) collective-permute-start(bf16[3,8,8,256]{3,2,1,0:T(8,128)(2,1)S(1)} %get-tuple-element.43), channel_id=1, source_target_pairs={{0,4},{1,2},{2,1},{3,7},{4,0},{5,6},{6,5},{7,3},{8,12},{9,10},{10,... | collective-permute-start | bytes 294920 | tf_op jit(solution)/shard_map/ppermute | solution.py:722
  10.9 5.9 %collective-permute-start.2 = (bf16[3,8,8,256]{3,2,1,0:T(8,128)(2,1)S(1)}, bf16[3,8,8,256]{3,2,1,0:T(8,128)(2,1)S(1)}, u32[]{:S(2)}, u32[]{:S(2)}) collective-permute-start(bf16[3,8,8,256]{3,2,1,0:T(8,128)(2,1)S(1)} %get-tuple-element.39), channel_id=1, source_target_pairs={{0,1},{1,0},{2,3},{3,2},{4,5},{5,4},{6,7},{7,6},{8,9},{9,8},{10,11... | collective-permute-start | bytes 294920 | tf_op jit(solution)/shard_map/ppermute | solution.py:738
  13.3 3.6 %collective-permute-start.3 = (bf16[3,8,8,256]{3,2,1,0:T(8,128)(2,1)S(1)}, bf16[3,8,8,256]{3,2,1,0:T(8,128)(2,1)S(1)}, u32[]{:S(2)}, u32[]{:S(2)}) collective-permute-start(bf16[3,8,8,256]{3,2,1,0:T(8,128)(2,1)S(1)} %get-tuple-element.40), channel_id=1, source_target_pairs={{0,4},{1,2},{2,1},{3,7},{4,0},{5,6},{6,5},{7,3},{8,12},{9,10},{10,... | collective-permute-start | bytes 294920 | tf_op jit(solution)/shard_map/ppermute | solution.py:739

commit v4 on v3

--- a/solution.py
+++ b/solution.py
@@ -53,45 +53,37 @@
 
 
 class Tables:
-    def __init__(self, ref, bricks, slabs, slots):
-        self.ref, self.bricks, self.slabs, self.slots = ref, bricks, slabs, slots
-        self.at_send = 0
-        self.at_source = 2 * slabs
-        self.at_prior = self.at_source + 6 * bricks
-        self.at_later = self.at_prior + bricks
-        self.at_ahead = self.at_later + bricks
-        self.at_back = self.at_ahead + slots
-
-    def gather(self, send_ref, source_ref, ahead_ref, prior_ref, back_ref, later_ref):
-        for i in range(2 * self.slabs):
-            self.ref[0, self.at_send + i] = send_ref[0, i]
+    def __init__(self, refs):
+        self.send_ref, source_ref, self.ahead_ref, self.prior_ref, self.back_ref, self.later_ref = refs
+        self.bricks = source_ref.shape[1]
+        self.slabs = self.send_ref.shape[1] // 2
+        self.slots = self.ahead_ref.shape[1]
+        self.source = [[source_ref[0, b, f] for f in range(6)] for b in range(self.bricks)]
+
+    def live(self):
+        return self.ahead_ref[0, 0] >= 0
+
+    def has(self, side):
+        return self.send_ref[0, side * self.slabs] >= 0
+
+    def brick_of(self, entry):
+        return (entry * 10923) >> 16
+
+    def sent(self, side, k):
+        entry = self.send_ref[0, side * self.slabs + k]
+        return jnp.where(entry < 0, self.bricks, self.brick_of(entry))
+
+    def raw(self, brick, face):
+        if isinstance(brick, int):
+            return self.source[brick][face]
+        entry = -1
         for b in range(self.bricks):
-            for f in range(6):
-                self.ref[0, self.at_source + 6 * b + f] = source_ref[0, b, f]
-            self.ref[0, self.at_prior + b] = prior_ref[0, b]
-            self.ref[0, self.at_later + b] = later_ref[0, b]
-        for i in range(self.slots):
-            self.ref[0, self.at_ahead + i] = ahead_ref[0, i]
-            self.ref[0, self.at_back + i] = back_ref[0, i]
-
-    def live(self):
-        return self.ref[0, self.at_ahead] >= 0
-
-    def has(self, side):
-        return self.ref[0, self.at_send + side * self.slabs] >= 0
-
-    def sent(self, side, k):
-        entry = self.ref[0, self.at_send + side * self.slabs + k]
-        return jnp.where(entry < 0, self.bricks, entry // 6)
-
-    def raw(self, brick, face):
-        inside = jnp.minimum(brick, self.bricks - 1)
-        return jnp.where(brick < self.bricks, self.ref[0, self.at_source + 6 * inside + face], -1)
+            entry = jnp.where(brick == b, self.source[b][face], entry)
+        return entry
 
     def local(self, brick, face):
-        entry = self.raw(brick, face)
-        base = 2 * self.slabs
-        return jnp.where(entry >= base, (entry - base) // 6, self.bricks)
+        entry = self.raw(brick, face) - 2 * self.slabs
+        return jnp.where(entry >= 0, self.brick_of(entry), self.bricks)
 
     def remote(self, brick, face):
         entry = self.raw(brick, face)
@@ -117,8 +109,8 @@
 
 
 def pack_kernel(*refs):
-    sources, (table_ref, rt_ref, mask_ref, pa_ref, pb_ref) = refs[:11], refs[11:16]
-    held, sems = refs[19:27] + refs[16:19], refs[27]
+    sources, table_refs, (rt_ref, mask_ref, pa_ref, pb_ref) = refs[:11], refs[11:17], refs[17:21]
+    held, sems = table_refs + refs[24:26] + refs[21:24], refs[26]
     copies = [pltpu.make_async_copy(s, d, sems.at[i]) for i, (s, d) in enumerate(zip(sources, held))]
     for copy in copies:
         copy.start()
@@ -126,8 +118,6 @@
     occ_ref, feat_ref = held[6:]
     _, bricks, edge, _, wide = feat_ref.shape
     channels = wide // edge
-    tables = Tables(table_ref, bricks, held[0].shape[1] // 2, held[2].shape[1])
-    slabs = tables.slabs
     per_tile = LANES // (edge * edge)
     rows8, lanes8 = iota((8, LANES), 0), iota((8, LANES), 1)
     low = low_half()
@@ -135,7 +125,8 @@
     spread = spread.astype(BF16)
     for copy in copies[:-1]:
         copy.wait()
-    tables.gather(*held[:6])
+    tables = Tables(table_refs)
+    slabs = tables.slabs
     occ = occ_ref[0].astype(F32)
     picked = []
     for z in range(edge):
@@ -285,8 +276,14 @@
 
 
 def inner_kernel(
-    slabs,
-    table_ref,
+    *refs,
+):
+    tables, refs = Tables(refs[:6]), refs[6:]
+    inner_body(tables, *refs)
+
+
+def inner_body(
+    tables,
     rt_ref,
     mask_ref,
     w_ref,
@@ -304,8 +301,6 @@
     bricks, edge, _, wide = rt_ref.shape
     bricks -= 1
     tiles = wide // LANES
-    slots = fa_ref.shape[0]
-    tables = Tables(table_ref, bricks, slabs, slots)
     rows = bricks * edge
 
     def load(field_ref, brick, z):
@@ -364,14 +359,18 @@
 def choose_parcels(tables, field_ref, fa_ref, fb_ref):
     odd = lax.rem(lax.axis_index("frame"), 2) == 1
     for slot in range(tables.slots):
-        ahead = tables.ref[0, tables.at_ahead + slot]
-        back = tables.ref[0, tables.at_back + slot]
+        ahead, back = tables.ahead_ref[0, slot], tables.back_ref[0, slot]
         fa_ref[slot] = field_ref[jnp.where(odd, back, ahead)]
         fb_ref[slot] = field_ref[jnp.where(odd, ahead, back)]
 
 
-def border_kernel(
-    table_ref,
+def border_kernel(*refs):
+    tables, refs = Tables(refs[:6]), refs[6:]
+    border_body(tables, *refs)
+
+
+def border_body(
+    tables,
     rt_ref,
     mask_ref,
     rt2_ref,
@@ -392,8 +391,7 @@
     bricks -= 1
     tiles = wide // LANES
     size = (edge + 4) * 8
-    slabs = ra_ref.shape[0] // size
-    tables = Tables(table_ref, bricks, slabs, fa_ref.shape[0])
+    slabs = tables.slabs
     rows = bricks * edge
     low, zero = low_half(), zero_tile()
     ends = (tile_of(0), tile_of(tiles - 1))
@@ -522,8 +520,7 @@
     def flat(block):
         return block.astype(F32).reshape(edge * edge, part)
 
-    prior = tables.ref[0, tables.at_prior + b]
-    later = tables.ref[0, tables.at_later + b]
+    prior, later = tables.prior_ref[0, b], tables.later_ref[0, b]
     at_prior = jnp.clip(prior, 0, tables.slots - 1)
     at_later = jnp.clip(later, 0, tables.slots - 1)
     before = flat(jnp.where(odd, ga_ref[at_prior], gb_ref[at_prior]))
@@ -545,9 +542,13 @@
             put(b, z, k, (keep * sums).astype(BF16))
 
 
-def middle_out_kernel(
-    slabs,
-    table_ref,
+def middle_out_kernel(*refs):
+    tables, refs = Tables(refs[:6]), refs[6:]
+    middle_out_body(tables, *refs)
+
+
+def middle_out_body(
+    tables,
     rt_ref,
     mask_ref,
     hid_ref,
@@ -564,7 +565,6 @@
         at = 2 * i * depth
         band_ref[at : at + depth, :] = jnp.concatenate([w_ref[i], blank], axis=1)
         band_ref[at + depth : at + 2 * depth, :] = jnp.concatenate([blank, w_ref[i]], axis=1)
-    tables = Tables(table_ref, rt_ref.shape[0] - 1, slabs, ga_ref.shape[0])
     tiles = rt_ref.shape[-1] // LANES
 
     def put(b, z, k, value):
@@ -586,9 +586,13 @@
         )
 
 
-def edge_out_kernel(
-    slabs,
-    table_ref,
+def edge_out_kernel(*refs):
+    tables, refs = Tables(refs[:6]), refs[6:]
+    edge_out_body(tables, *refs)
+
+
+def edge_out_body(
+    tables,
     rt_ref,
     mask_ref,
     hid_ref,
@@ -600,7 +604,6 @@
     held_ref,
     sems,
 ):
-    tables = Tables(table_ref, rt_ref.shape[0] - 1, slabs, ga_ref.shape[0])
     tiles = rt_ref.shape[-1] // LANES
     wide = tiles * LANES
     copies = [
@@ -630,7 +633,6 @@
 
 
 VMEM = pl.BlockSpec(memory_space=pltpu.VMEM)
-SMEM = pl.BlockSpec(memory_space=pltpu.SMEM)
 HBM = pl.BlockSpec(memory_space=pltpu.HBM)
 
 
@@ -678,15 +680,15 @@
         b_spatial,
         w_temporal,
     )
-    table, rolled, mask, parcel_a, parcel_b, w_held, b_held, wt_held = pl.pallas_call(
+    *table, rolled, mask, parcel_a, parcel_b, w_held, b_held, wt_held = pl.pallas_call(
         pack_kernel,
         name="pack",
-        out_shape=(shape((1, LANES), jnp.int32), field, shape((rows, wide), F32), parcel, parcel)
+        out_shape=tuple(shape(a.shape, a.dtype) for a in arguments[:6])
+        + (field, shape((rows, wide), F32), parcel, parcel)
         + tuple(shape(a.shape, a.dtype) for a in arguments[8:]),
         in_specs=[HBM] * 11,
-        out_specs=(SMEM,) + (VMEM,) * 7,
-        scratch_shapes=[pltpu.SMEM(a.shape, a.dtype) for a in arguments[:6]]
-        + [pltpu.VMEM(a.shape, a.dtype) for a in arguments[6:8]]
+        out_specs=(VMEM,) * 13,
+        scratch_shapes=[pltpu.VMEM(a.shape, a.dtype) for a in arguments[6:8]]
         + [pltpu.SemaphoreType.DMA((11,))],
         compiler_params=pltpu.CompilerParams(vmem_limit_bytes=8 << 20),
         cost_estimate=cost(10**8, 10**6),
@@ -700,7 +702,7 @@
     hidden = shape((bricks, edge, edge, half_wide), BF16)
     sent = shape((slots, edge, edge, half_wide), BF16)
     rolled2, pad2, band1, band2, bias2, middle, parcel_a, parcel_b = pl.pallas_call(
-        functools.partial(inner_kernel, slabs),
+        inner_kernel,
         name="inner",
         out_shape=(
             field,
@@ -712,12 +714,12 @@
             sent,
             sent,
         ),
-        in_specs=[SMEM] + [VMEM] * 4,
+        in_specs=[VMEM] * 10,
         out_specs=(VMEM,) * 8,
         scratch_shapes=[pltpu.VMEM((3, pad_rows, wide + LANES), BF16)],
         compiler_params=pltpu.CompilerParams(vmem_limit_bytes=24 << 20),
         cost_estimate=cost(10**9, 4 * 10**6),
-    )(table, rolled, mask, w_held, b_held)
+    )(*table, rolled, mask, w_held, b_held)
     middle_a = lax.ppermute(parcel_a, AXES, frame_first)
     middle_b = lax.ppermute(parcel_b, AXES, frame_second)
 
@@ -725,7 +727,7 @@
         border_kernel,
         name="border",
         out_shape=(hidden, sent, sent),
-        in_specs=[SMEM] + [VMEM] * 9,
+        in_specs=[VMEM] * 15,
         out_specs=(VMEM,) * 3,
         scratch_shapes=[
             pltpu.VMEM((bricks + 1 + slabs, edge, edge, 2 * LANES), F32),
@@ -734,24 +736,24 @@
         ],
         compiler_params=pltpu.CompilerParams(vmem_limit_bytes=16 << 20),
         cost_estimate=cost(5 * 10**8, 2 * 10**6),
-    )(table, rolled, mask, rolled2, pad2, band1, band2, bias2, space_a, space_b)
+    )(*table, rolled, mask, rolled2, pad2, band1, band2, bias2, space_a, space_b)
     edge_a = lax.ppermute(parcel_a, AXES, frame_first)
     edge_b = lax.ppermute(parcel_b, AXES, frame_second)
 
     middle_out, band = pl.pallas_call(
-        functools.partial(middle_out_kernel, slabs),
+        middle_out_kernel,
         name="middle_out",
         out_shape=(hidden, shape((6 * depth, LANES), BF16)),
-        in_specs=[SMEM] + [VMEM] * 6 + [pl.BlockSpec(memory_space=pl.ANY)],
+        in_specs=[VMEM] * 12 + [pl.BlockSpec(memory_space=pl.ANY)],
         out_specs=(VMEM, VMEM),
         compiler_params=pltpu.CompilerParams(vmem_limit_bytes=8 << 20),
         cost_estimate=cost(10**8, 10**6),
-    )(table, rolled, mask, middle, middle_a, middle_b, wt_held, edges)
+    )(*table, rolled, mask, middle, middle_a, middle_b, wt_held, edges)
     return pl.pallas_call(
-        functools.partial(edge_out_kernel, slabs),
+        edge_out_kernel,
         name="edge_out",
         out_shape=shape(features.shape, BF16),
-        in_specs=[SMEM] + [VMEM] * 7,
+        in_specs=[VMEM] * 13,
         out_specs=HBM,
         scratch_shapes=[
             pltpu.VMEM((2, bricks, edge, edge, LANES), BF16),
@@ -759,7 +761,7 @@
         ],
         compiler_params=pltpu.CompilerParams(vmem_limit_bytes=8 << 20),
         cost_estimate=cost(10**8, 10**6),
-    )(table, rolled, mask, edges, edge_a, edge_b, band, middle_out)
+    )(*table, rolled, mask, edges, edge_a, edge_b, band, middle_out)
 
 
 def solution(mesh):

time: 18.5 us -> 16.6 us (0.90)
  Pallas kernels: 8.68 us -> 6.31 us
  waiting for transfers between devices: 2.36 us -> 2.9 us
    pallas_call x4, Pallas kernels: 6.89 us -> 5.02 us  [the longest x1 2.17 us: per_device(): pl.pallas_call(inner_kernel, name='inner', out_shape=(field, shape((3, pa...]
    ppermute x1, waiting for transfers between devices: 2.35 us -> 2.88 us  [per_device(): edge_a = lax.ppermute(parcel_a, AXES, frame_first)]
    pallas_call x1, Pallas kernels: 1.79 us -> 1.29 us  [per_device(): pl.pallas_call(border_kernel, name='border', out_shape=(hidden, sent, sen...]
  transfers between devices with their start and end apart: 6 -> 6, of which waited for: 1 -> 1; matrix products, arithmetic and copies ran while one was open for 0% -> 0% of each run, Pallas kernels for 29% -> 23%
where the time goes in v4:
time: 16.6 us; the launch traced here: 16.5 us
  starting transfers between devices  7.24 us (44%)
  Pallas kernels  6.31 us (38%)
  waiting for transfers between devices  2.9 us (17%)
    ppermute x1, waiting for transfers between devices, per_device(): edge_a = lax.ppermute(parcel_a, AXES, frame_first)  2.88 us
    ppermute x1, starting transfers between devices, per_device(): space_b = lax.ppermute(parcel_b, AXES, space_second)  2.64 us
    ppermute x1, starting transfers between devices, per_device(): edge_a = lax.ppermute(parcel_a, AXES, frame_first)  2.34 us
    pallas_call x1, Pallas kernels, per_device(): pl.pallas_call(inner_kernel, name='inner', out_shape=(field, shape((3, pa...  2.17 us
    pallas_call x1, Pallas kernels, per_device(): pl.pallas_call(pack_kernel, name='pack', out_shape=tuple((shape(a.shape,...  1.46 us
    ppermute x1, starting transfers between devices, per_device(): middle_b = lax.ppermute(parcel_b, AXES, frame_second)  1.31 us
    pallas_call x1, Pallas kernels, per_device(): pl.pallas_call(border_kernel, name='border', out_shape=(hidden, sent, sen...  1.29 us
    pallas_call x1, Pallas kernels, per_device(): pl.pallas_call(edge_out_kernel, name='edge_out', out_shape=shape(features...  1.05 us
  transfers between devices with their start and end apart: 6, of which 1 were waited for; matrix products, arithmetic and copies ran while one was open for 0% of the time, Pallas kernels for 23%

profile of v4, /device:TPU:0, one launch (start us, length us, event | category | flops | bytes accessed | tf_op | source)
XLA Modules:
  0.0 16.5 jit_solution(8720108449071886879)
XLA Ops:
  0.0 1.5 %pack.1 = (s32[1,2]{1,0:T(1,128)S(1)}, s32[1,4,6]{2,1,0:T(4,128)S(1)}, s32[1,3]{1,0:T(1,128)S(1)}, s32[1,4]{1,0:T(1,128)S(1)}, s32[1,3]{1,0:T(1,128)S(1)}, /*ind...) custom-call(s32[1,2]{1,0:T(1,128)} %refs_0_.1, ...), custom_call_target="tpu_custom_call" | custom-call | flops 100000000 | bytes 1000000 | tf_op jit(solution)/shard_map/pack/pallas_call | solution.py:683
  1.5 0.6 %collective-permute-start = (bf16[96,256]{1,0:T(8,128)(2,1)S(1)}, bf16[96,256]{1,0:T(8,128)(2,1)S(1)}, u32[]{:S(2)}, u32[]{:S(2)}) collective-permute-start(bf16[96,256]{1,0:T(8,128)(2,1)S(1)} %get-tuple-element.46), channel_id=1, source_target_pairs={{0,4},{1,5},{2,6},{3,7},{4,0},{5,1},{6,2},{7,3},{8,12},{9,13},{10,... | collective-permute-start | bytes 147464 | tf_op jit(solution)/shard_map/ppermute | solution.py:696
  2.0 2.6 %collective-permute-start.1 = (bf16[96,256]{1,0:T(8,128)(2,1)S(1)}, bf16[96,256]{1,0:T(8,128)(2,1)S(1)}, u32[]{:S(2)}, u32[]{:S(2)}) collective-permute-start(bf16[96,256]{1,0:T(8,128)(2,1)S(1)} %get-tuple-element.47), channel_id=1, source_target_pairs={{0,1},{1,0},{2,3},{3,2},{4,8},{5,9},{6,10},{7,11},{8,4},{9,5},{10,... | collective-permute-start | bytes 147464 | tf_op jit(solution)/shard_map/ppermute | solution.py:697
  4.7 2.2 %inner.1 = (f32[5,8,8,512]{3,2,1,0:T(8,128)S(1)}, bf16[3,320,384]{2,1,0:T(8,128)(2,1)S(1)}, bf16[3072,256]{1,0:T(8,128)(2,1)S(1)}, bf16[3072,256]{1,0:T(8,128)(2...) custom-call(s32[1,2]{1,0:T(1,128)S(1)} %get-tuple-element.31.refs_0_, ...), custom_call_target="tpu_custom_call" | custom-call | flops 1000000000 | bytes 4000000 | tf_op jit(solution)/shard_map/inner/pallas_call | solution.py:704
  6.8 0.1 collective-permute-start.4
  6.9 1.3 %collective-permute-start.5 = (bf16[3,8,8,256]{3,2,1,0:T(8,128)(2,1)S(1)}, bf16[3,8,8,256]{3,2,1,0:T(8,128)(2,1)S(1)}, u32[]{:S(2)}, u32[]{:S(2)}) collective-permute-start(bf16[3,8,8,256]{3,2,1,0:T(8,128)(2,1)S(1)} %get-tuple-element.53), channel_id=1, source_target_pairs={{0,4},{1,2},{2,1},{3,7},{4,0},{5,6},{6,5},{7,3},{8,12},{9,10},{10,... | collective-permute-start | bytes 294920 | tf_op jit(solution)/shard_map/ppermute | solution.py:724
  8.2 0.0 collective-permute-done.refs_13_
  8.2 0.0 collective-permute-done.1.refs_14_
  8.2 1.3 %border.1 = (bf16[4,8,8,256]{3,2,1,0:T(8,128)(2,1)S(1)}, bf16[3,8,8,256]{3,2,1,0:T(8,128)(2,1)S(1)}, bf16[3,8,8,256]{3,2,1,0:T(8,128)(2,1)S(1)}) custom-call(s32[1,2]{1,0:T(1,128)S(1)} %get-tuple-element.31.refs_0_, s32[1,4,6]{2,1,0:T(4,128)S(1)} %get-tuple-element.32.refs_1_, s32[1,3]{1,0:T(1,128)S(1)} %get-tuple-element.33.refs_2_, ...), custom_call_target="tpu_custom_call" | custom-call | flops 500000000 | bytes 2000000 | tf_op jit(solution)/shard_map/border/pallas_call | solution.py:726
  9.5 2.3 %collective-permute-start.2 = (bf16[3,8,8,256]{3,2,1,0:T(8,128)(2,1)S(1)}, bf16[3,8,8,256]{3,2,1,0:T(8,128)(2,1)S(1)}, u32[]{:S(2)}, u32[]{:S(2)}) collective-permute-start(bf16[3,8,8,256]{3,2,1,0:T(8,128)(2,1)S(1)} %get-tuple-element.49), channel_id=1, source_target_pairs={{0,1},{1,0},{2,3},{3,2},{4,5},{5,4},{6,7},{7,6},{8,9},{9,8},{10,11... | collective-permute-start | bytes 294920 | tf_op jit(solution)/shard_map/ppermute | solution.py:740
  11.9 0.3 %collective-permute-start.3 = (bf16[3,8,8,256]{3,2,1,0:T(8,128)(2,1)S(1)}, bf16[3,8,8,256]{3,2,1,0:T(8,128)(2,1)S(1)}, u32[]{:S(2)}, u32[]{:S(2)}) collective-permute-start(bf16[3,8,8,256]{3,2,1,0:T(8,128)(2,1)S(1)} %get-tuple-element.50), channel_id=1, source_target_pairs={{0,4},{1,2},{2,1},{3,7},{4,0},{5,6},{6,5},{7,3},{8,12},{9,10},{10,... | collective-permute-start | bytes 294920 | tf_op jit(solution)/shard_map/ppermute | solution.py:741
  12.2 0.0 collective-permute-done.4.refs_9_
  12.2 0.0 collective-permute-done.5.refs_10_
  12.2 0.3 %middle_out.1 = (bf16[4,8,8,256]{3,2,1,0:T(8,128)(2,1)S(1)}, bf16[384,128]{1,0:T(8,128)(2,1)S(1)}) custom-call(s32[1,2]{1,0:T(1,128)S(1)} %get-tuple-element.31.refs_0_, s32[1,4,6]{2,1,0:T(4,128)S(1)} %get-tuple-element.32.refs_1_, s32[1,3]{1,0:T(1,128)S(1)} %get-tuple-element.33.refs_2_, s32[1,4]{1,0:T(1,128)S(1)} %get-tuple-element.34.refs_3_, ...), custom_call_target="tpu_custom_call" | custom-call | flops 100000000 | bytes 1000000 | tf_op jit(solution)/shard_map/middle_out/pallas_call | solution.py:743
  12.6 2.9 %collective-permute-done.2.refs_9_ = bf16[3,8,8,256]{3,2,1,0:T(8,128)(2,1)S(1)} collective-permute-done((bf16[3,8,8,256]{3,2,1,0:T(8,128)(2,1)S(1)}, bf16[3,8,8,256]{3,2,1,0:T(8,128)(2,1)S(1)}, u32[]{:S(2)}, u32[]{:S(2)}) %collective-permute-start.2) | collective-permute-done | bytes 98336 | tf_op jit(solution)/shard_map/ppermute | solution.py:740
  15.4 0.0 collective-permute-done.3.refs_10_
  15.4 1.0 %edge_out.1 = bf16[1,4,8,8,512]{4,3,2,1,0:T(8,128)(2,1)} custom-call(s32[1,2]{1,0:T(1,128)S(1)} %get-tuple-element.31.refs_0_, s32[1,4,6]{2,1,0:T(4,128)S(1)} %get-tuple-element.32.refs_1_, s32[1,3]{1,0:T(1,128)S(1)} %get-tuple-element.33.refs_2_, s32[1,4]{1,0:T(1,128)S(1)} %get-tuple-element.34.refs_3_, s32[1,3]{1,0:T(1,128)S(1)} %get-tuple-element.35.refs_4_, ...), custom_call_target="tpu_custom_call" | custom-call | flops 100000000 | bytes 1000000 | tf_op jit(solution)/shard_map/edge_out/pallas_call | solution.py:752
Async XLA Ops:
  1.5 6.8 %collective-permute-start = (bf16[96,256]{1,0:T(8,128)(2,1)S(1)}, bf16[96,256]{1,0:T(8,128)(2,1)S(1)}, u32[]{:S(2)}, u32[]{:S(2)}) collective-permute-start(bf16[96,256]{1,0:T(8,128)(2,1)S(1)} %get-tuple-element.46), channel_id=1, source_target_pairs={{0,4},{1,5},{2,6},{3,7},{4,0},{5,1},{6,2},{7,3},{8,12},{9,13},{10,... | collective-permute-start | bytes 147464 | tf_op jit(solution)/shard_map/ppermute | solution.py:696
  2.0 6.2 %collective-permute-start.1 = (bf16[96,256]{1,0:T(8,128)(2,1)S(1)}, bf16[96,256]{1,0:T(8,128)(2,1)S(1)}, u32[]{:S(2)}, u32[]{:S(2)}) collective-permute-start(bf16[96,256]{1,0:T(8,128)(2,1)S(1)} %get-tuple-element.47), channel_id=1, source_target_pairs={{0,1},{1,0},{2,3},{3,2},{4,8},{5,9},{6,10},{7,11},{8,4},{9,5},{10,... | collective-permute-start | bytes 147464 | tf_op jit(solution)/shard_map/ppermute | solution.py:697
  6.8 5.4 %collective-permute-start.4 = (bf16[3,8,8,256]{3,2,1,0:T(8,128)(2,1)S(1)}, bf16[3,8,8,256]{3,2,1,0:T(8,128)(2,1)S(1)}, u32[]{:S(2)}, u32[]{:S(2)}) collective-permute-start(bf16[3,8,8,256]{3,2,1,0:T(8,128)(2,1)S(1)} %get-tuple-element.52), channel_id=1, source_target_pairs={{0,1},{1,0},{2,3},{3,2},{4,5},{5,4},{6,7},{7,6},{8,9},{9,8},{10,11... | collective-permute-start | bytes 294920 | tf_op jit(solution)/shard_map/ppermute | solution.py:723
  6.9 5.3 %collective-permute-start.5 = (bf16[3,8,8,256]{3,2,1,0:T(8,128)(2,1)S(1)}, bf16[3,8,8,256]{3,2,1,0:T(8,128)(2,1)S(1)}, u32[]{:S(2)}, u32[]{:S(2)}) collective-permute-start(bf16[3,8,8,256]{3,2,1,0:T(8,128)(2,1)S(1)} %get-tuple-element.53), channel_id=1, source_target_pairs={{0,4},{1,2},{2,1},{3,7},{4,0},{5,6},{6,5},{7,3},{8,12},{9,10},{10,... | collective-permute-start | bytes 294920 | tf_op jit(solution)/shard_map/ppermute | solution.py:724
  9.5 5.9 %collective-permute-start.2 = (bf16[3,8,8,256]{3,2,1,0:T(8,128)(2,1)S(1)}, bf16[3,8,8,256]{3,2,1,0:T(8,128)(2,1)S(1)}, u32[]{:S(2)}, u32[]{:S(2)}) collective-permute-start(bf16[3,8,8,256]{3,2,1,0:T(8,128)(2,1)S(1)} %get-tuple-element.49), channel_id=1, source_target_pairs={{0,1},{1,0},{2,3},{3,2},{4,5},{5,4},{6,7},{7,6},{8,9},{9,8},{10,11... | collective-permute-start | bytes 294920 | tf_op jit(solution)/shard_map/ppermute | solution.py:740
  11.9 3.6 %collective-permute-start.3 = (bf16[3,8,8,256]{3,2,1,0:T(8,128)(2,1)S(1)}, bf16[3,8,8,256]{3,2,1,0:T(8,128)(2,1)S(1)}, u32[]{:S(2)}, u32[]{:S(2)}) collective-permute-start(bf16[3,8,8,256]{3,2,1,0:T(8,128)(2,1)S(1)} %get-tuple-element.50), channel_id=1, source_target_pairs={{0,4},{1,2},{2,1},{3,7},{4,0},{5,6},{6,5},{7,3},{8,12},{9,10},{10,... | collective-permute-start | bytes 294920 | tf_op jit(solution)/shard_map/ppermute | solution.py:741

commit v5 on v4

--- a/solution.py
+++ b/solution.py
@@ -184,10 +184,14 @@
         copy.wait()
 
 
+def tap_place(dz, dy):
+    return (dz // 2) * 6 + (1, 0, 2)[dy] * 2 + dz % 2
+
+
 def fill_band(w_ref, layer, band_ref):
     blank = jnp.zeros(w_ref.shape[2:], BF16)
     depth = w_ref.shape[2]
-    for dy in range(3):
+    for dy in (1, 0, 2):
         for dz in range(3):
             tap = 3 * dz + dy
             before, here, after = (w_ref[layer, 3 * tap + i] for i in range(3))
@@ -196,10 +200,10 @@
             ):
                 block = jnp.concatenate([left, right], axis=1)
                 for out in range(2):
-                    at = (((dz + out) * 3 + dy) * 4 + row) * depth
+                    at = (tap_place(dz + out, dy) * 4 + row) * depth
                     band_ref[at : at + depth, tile_of(out)] = block
         for out, dz in ((0, 3), (1, 0)):
-            at = (dz * 3 + dy) * 4 * depth
+            at = tap_place(dz, dy) * 4 * depth
             band_ref[at : at + 4 * depth, tile_of(out)] = jnp.zeros((4 * depth, LANES), BF16)
 
 
@@ -232,35 +236,42 @@
 def fill_padded(pad_ref, tables, edge, own, rim, pairs):
     bricks = tables.bricks
     index = [[tables.local(b, f) for f in range(2, 6)] for b in range(bricks)]
-    for z in range(-1, edge + 1):
-        for first in range(0, bricks, 2):
+
+    def lines(b, z):
+        y_low, y_high, z_low, z_high = index[b]
+        if 0 <= z < edge:
+            return own(b, z), rim(y_low, z), rim(y_high, z)
+        line = rim(z_low, edge - 1) if z < 0 else rim(z_high, 0)
+        return line, [None] * len(line), [None] * len(line)
+
+    def store(dy, z, first, built):
+        at = ((z + 1) * bricks + first) * edge
+        for k in range(len(pairs)):
+            block = jnp.concatenate([built[0][k], built[1][k]], axis=0)
+            pad_ref[dy, at : at + 2 * edge, tile_of(k)] = block.astype(BF16)
+
+    places = [(z, first) for z in range(-1, edge + 1) for first in range(0, bricks, 2)]
+    for z, first in places:
+        store(1, z, first, [merged(lines(b, z)[0], pairs) for b in (first, first + 1)])
+    for dy in (0, 2):
+        for z, first in places:
             built = []
             for b in (first, first + 1):
-                y_low, y_high, z_low, z_high = index[b]
-                if 0 <= z < edge:
-                    line, before, after = own(b, z), rim(y_low, z), rim(y_high, z)
-                else:
-                    line = rim(z_low, edge - 1) if z < 0 else rim(z_high, 0)
-                    before = after = [None] * len(line)
-                built.append([merged(s, pairs) for s in three_shifts(line, before, after)])
-            at = ((z + 1) * bricks + first) * edge
-            for dy in range(3):
-                for k in range(len(pairs)):
-                    block = jnp.concatenate([built[0][dy][k], built[1][dy][k]], axis=0)
-                    pad_ref[dy, at : at + 2 * edge, tile_of(k)] = block.astype(BF16)
+                sides = lines(b, z)
+                moved = [shifted(t, r, dy == 0) for t, r in zip(sides[0], sides[1 + dy // 2])]
+                built.append(merged(moved, pairs))
+            store(dy, z, first, built)
 
 
 def convolve(windows, rows, edge, band_ref):
     blocks = []
     for window in windows:
         parts = []
-        for dz in range(4):
-            for dy in range(3):
-                parts.append(
-                    jnp.concatenate(
-                        [window(dy, (2 * zz + dz) * rows, rows) for zz in range(edge // 2)], axis=0
-                    )
-                )
+        for first in (0, 2):
+            for dy in (1, 0, 2):
+                for dz in (first, first + 1):
+                    starts = [(2 * zz + dz) * rows for zz in range(edge // 2)]
+                    parts.append(jnp.concatenate([window(dy, at, rows) for at in starts], axis=0))
         blocks.append(parts)
     total = 0.0
     for first in (0, 6):

time: 16.6 us -> 16.4 us (0.988)
  Pallas kernels: 6.31 us -> 6.09 us
    pallas_call x1, Pallas kernels: 2.17 us -> 1.93 us  [per_device(): pl.pallas_call(inner_kernel, name='inner', out_shape=(field, shape((3, pa...]
  transfers between devices with their start and end apart: 6 -> 6, of which waited for: 1 -> 1; matrix products, arithmetic and copies ran while one was open for 0% -> 0% of each run, Pallas kernels for 23% -> 22%
where the time goes in v5:
time: 16.4 us; the launch traced here: 16.3 us
  starting transfers between devices  7.25 us (44%)
  Pallas kernels  6.09 us (37%)
  waiting for transfers between devices  2.9 us (18%)
    ppermute x1, waiting for transfers between devices, per_device(): edge_a = lax.ppermute(parcel_a, AXES, frame_first)  2.89 us
    ppermute x1, starting transfers between devices, per_device(): space_b = lax.ppermute(parcel_b, AXES, space_second)  2.64 us
    ppermute x1, starting transfers between devices, per_device(): edge_a = lax.ppermute(parcel_a, AXES, frame_first)  2.34 us
    pallas_call x1, Pallas kernels, per_device(): pl.pallas_call(inner_kernel, name='inner', out_shape=(field, shape((3, pa...  1.93 us
    pallas_call x1, Pallas kernels, per_device(): pl.pallas_call(pack_kernel, name='pack', out_shape=tuple((shape(a.shape,...  1.46 us
    ppermute x1, starting transfers between devices, per_device(): middle_b = lax.ppermute(parcel_b, AXES, frame_second)  1.31 us
    pallas_call x1, Pallas kernels, per_device(): pl.pallas_call(border_kernel, name='border', out_shape=(hidden, sent, sen...  1.31 us
    pallas_call x1, Pallas kernels, per_device(): pl.pallas_call(edge_out_kernel, name='edge_out', out_shape=shape(features...  1.05 us
  transfers between devices with their start and end apart: 6, of which 1 were waited for; matrix products, arithmetic and copies ran while one was open for 0% of the time, Pallas kernels for 22%

profile of v5, /device:TPU:0, one launch (start us, length us, event | category | flops | bytes accessed | tf_op | source)
XLA Modules:
  0.0 16.3 jit_solution(4322231039917020138)
XLA Ops:
  0.0 1.5 %pack.1 = (s32[1,2]{1,0:T(1,128)S(1)}, s32[1,4,6]{2,1,0:T(4,128)S(1)}, s32[1,3]{1,0:T(1,128)S(1)}, s32[1,4]{1,0:T(1,128)S(1)}, s32[1,3]{1,0:T(1,128)S(1)}, /*ind...) custom-call(s32[1,2]{1,0:T(1,128)} %refs_0_.1, ...), custom_call_target="tpu_custom_call" | custom-call | flops 100000000 | bytes 1000000 | tf_op jit(solution)/shard_map/pack/pallas_call | solution.py:694
  1.5 0.6 %collective-permute-start = (bf16[96,256]{1,0:T(8,128)(2,1)S(1)}, bf16[96,256]{1,0:T(8,128)(2,1)S(1)}, u32[]{:S(2)}, u32[]{:S(2)}) collective-permute-start(bf16[96,256]{1,0:T(8,128)(2,1)S(1)} %get-tuple-element.46), channel_id=1, source_target_pairs={{0,4},{1,5},{2,6},{3,7},{4,0},{5,1},{6,2},{7,3},{8,12},{9,13},{10,... | collective-permute-start | bytes 147464 | tf_op jit(solution)/shard_map/ppermute | solution.py:707
  2.0 2.6 %collective-permute-start.1 = (bf16[96,256]{1,0:T(8,128)(2,1)S(1)}, bf16[96,256]{1,0:T(8,128)(2,1)S(1)}, u32[]{:S(2)}, u32[]{:S(2)}) collective-permute-start(bf16[96,256]{1,0:T(8,128)(2,1)S(1)} %get-tuple-element.47), channel_id=1, source_target_pairs={{0,1},{1,0},{2,3},{3,2},{4,8},{5,9},{6,10},{7,11},{8,4},{9,5},{10,... | collective-permute-start | bytes 147464 | tf_op jit(solution)/shard_map/ppermute | solution.py:708
  4.7 1.9 %inner.1 = (f32[5,8,8,512]{3,2,1,0:T(8,128)S(1)}, bf16[3,320,384]{2,1,0:T(8,128)(2,1)S(1)}, bf16[3072,256]{1,0:T(8,128)(2,1)S(1)}, bf16[3072,256]{1,0:T(8,128)(2...) custom-call(s32[1,2]{1,0:T(1,128)S(1)} %get-tuple-element.31.refs_0_, ...), custom_call_target="tpu_custom_call" | custom-call | flops 1000000000 | bytes 4000000 | tf_op jit(solution)/shard_map/inner/pallas_call | solution.py:715
  6.6 0.1 collective-permute-start.4
  6.7 1.3 %collective-permute-start.5 = (bf16[3,8,8,256]{3,2,1,0:T(8,128)(2,1)S(1)}, bf16[3,8,8,256]{3,2,1,0:T(8,128)(2,1)S(1)}, u32[]{:S(2)}, u32[]{:S(2)}) collective-permute-start(bf16[3,8,8,256]{3,2,1,0:T(8,128)(2,1)S(1)} %get-tuple-element.53), channel_id=1, source_target_pairs={{0,4},{1,2},{2,1},{3,7},{4,0},{5,6},{6,5},{7,3},{8,12},{9,10},{10,... | collective-permute-start | bytes 294920 | tf_op jit(solution)/shard_map/ppermute | solution.py:735
  8.0 0.0 collective-permute-done.refs_13_
  8.0 0.0 collective-permute-done.1.refs_14_
  8.0 1.3 %border.1 = (bf16[4,8,8,256]{3,2,1,0:T(8,128)(2,1)S(1)}, bf16[3,8,8,256]{3,2,1,0:T(8,128)(2,1)S(1)}, bf16[3,8,8,256]{3,2,1,0:T(8,128)(2,1)S(1)}) custom-call(s32[1,2]{1,0:T(1,128)S(1)} %get-tuple-element.31.refs_0_, s32[1,4,6]{2,1,0:T(4,128)S(1)} %get-tuple-element.32.refs_1_, s32[1,3]{1,0:T(1,128)S(1)} %get-tuple-element.33.refs_2_, ...), custom_call_target="tpu_custom_call" | custom-call | flops 500000000 | bytes 2000000 | tf_op jit(solution)/shard_map/border/pallas_call | solution.py:737
  9.3 2.3 %collective-permute-start.2 = (bf16[3,8,8,256]{3,2,1,0:T(8,128)(2,1)S(1)}, bf16[3,8,8,256]{3,2,1,0:T(8,128)(2,1)S(1)}, u32[]{:S(2)}, u32[]{:S(2)}) collective-permute-start(bf16[3,8,8,256]{3,2,1,0:T(8,128)(2,1)S(1)} %get-tuple-element.49), channel_id=1, source_target_pairs={{0,1},{1,0},{2,3},{3,2},{4,5},{5,4},{6,7},{7,6},{8,9},{9,8},{10,11... | collective-permute-start | bytes 294920 | tf_op jit(solution)/shard_map/ppermute | solution.py:751
  11.7 0.3 %collective-permute-start.3 = (bf16[3,8,8,256]{3,2,1,0:T(8,128)(2,1)S(1)}, bf16[3,8,8,256]{3,2,1,0:T(8,128)(2,1)S(1)}, u32[]{:S(2)}, u32[]{:S(2)}) collective-permute-start(bf16[3,8,8,256]{3,2,1,0:T(8,128)(2,1)S(1)} %get-tuple-element.50), channel_id=1, source_target_pairs={{0,4},{1,2},{2,1},{3,7},{4,0},{5,6},{6,5},{7,3},{8,12},{9,10},{10,... | collective-permute-start | bytes 294920 | tf_op jit(solution)/shard_map/ppermute | solution.py:752
  12.0 0.0 collective-permute-done.4.refs_9_
  12.0 0.0 collective-permute-done.5.refs_10_
  12.0 0.3 %middle_out.1 = (bf16[4,8,8,256]{3,2,1,0:T(8,128)(2,1)S(1)}, bf16[384,128]{1,0:T(8,128)(2,1)S(1)}) custom-call(s32[1,2]{1,0:T(1,128)S(1)} %get-tuple-element.31.refs_0_, s32[1,4,6]{2,1,0:T(4,128)S(1)} %get-tuple-element.32.refs_1_, s32[1,3]{1,0:T(1,128)S(1)} %get-tuple-element.33.refs_2_, s32[1,4]{1,0:T(1,128)S(1)} %get-tuple-element.34.refs_3_, ...), custom_call_target="tpu_custom_call" | custom-call | flops 100000000 | bytes 1000000 | tf_op jit(solution)/shard_map/middle_out/pallas_call | solution.py:754
  12.3 2.9 %collective-permute-done.2.refs_9_ = bf16[3,8,8,256]{3,2,1,0:T(8,128)(2,1)S(1)} collective-permute-done((bf16[3,8,8,256]{3,2,1,0:T(8,128)(2,1)S(1)}, bf16[3,8,8,256]{3,2,1,0:T(8,128)(2,1)S(1)}, u32[]{:S(2)}, u32[]{:S(2)}) %collective-permute-start.2) | collective-permute-done | bytes 98336 | tf_op jit(solution)/shard_map/ppermute | solution.py:751
  15.2 0.0 collective-permute-done.3.refs_10_
  15.2 1.0 %edge_out.1 = bf16[1,4,8,8,512]{4,3,2,1,0:T(8,128)(2,1)} custom-call(s32[1,2]{1,0:T(1,128)S(1)} %get-tuple-element.31.refs_0_, s32[1,4,6]{2,1,0:T(4,128)S(1)} %get-tuple-element.32.refs_1_, s32[1,3]{1,0:T(1,128)S(1)} %get-tuple-element.33.refs_2_, s32[1,4]{1,0:T(1,128)S(1)} %get-tuple-element.34.refs_3_, s32[1,3]{1,0:T(1,128)S(1)} %get-tuple-element.35.refs_4_, ...), custom_call_target="tpu_custom_call" | custom-call | flops 100000000 | bytes 1000000 | tf_op jit(solution)/shard_map/edge_out/pallas_call | solution.py:763
Async XLA Ops:
  1.5 6.5 %collective-permute-start = (bf16[96,256]{1,0:T(8,128)(2,1)S(1)}, bf16[96,256]{1,0:T(8,128)(2,1)S(1)}, u32[]{:S(2)}, u32[]{:S(2)}) collective-permute-start(bf16[96,256]{1,0:T(8,128)(2,1)S(1)} %get-tuple-element.46), channel_id=1, source_target_pairs={{0,4},{1,5},{2,6},{3,7},{4,0},{5,1},{6,2},{7,3},{8,12},{9,13},{10,... | collective-permute-start | bytes 147464 | tf_op jit(solution)/shard_map/ppermute | solution.py:707
  2.0 6.0 %collective-permute-start.1 = (bf16[96,256]{1,0:T(8,128)(2,1)S(1)}, bf16[96,256]{1,0:T(8,128)(2,1)S(1)}, u32[]{:S(2)}, u32[]{:S(2)}) collective-permute-start(bf16[96,256]{1,0:T(8,128)(2,1)S(1)} %get-tuple-element.47), channel_id=1, source_target_pairs={{0,1},{1,0},{2,3},{3,2},{4,8},{5,9},{6,10},{7,11},{8,4},{9,5},{10,... | collective-permute-start | bytes 147464 | tf_op jit(solution)/shard_map/ppermute | solution.py:708
  6.6 5.4 %collective-permute-start.4 = (bf16[3,8,8,256]{3,2,1,0:T(8,128)(2,1)S(1)}, bf16[3,8,8,256]{3,2,1,0:T(8,128)(2,1)S(1)}, u32[]{:S(2)}, u32[]{:S(2)}) collective-permute-start(bf16[3,8,8,256]{3,2,1,0:T(8,128)(2,1)S(1)} %get-tuple-element.52), channel_id=1, source_target_pairs={{0,1},{1,0},{2,3},{3,2},{4,5},{5,4},{6,7},{7,6},{8,9},{9,8},{10,11... | collective-permute-start | bytes 294920 | tf_op jit(solution)/shard_map/ppermute | solution.py:734
  6.7 5.3 %collective-permute-start.5 = (bf16[3,8,8,256]{3,2,1,0:T(8,128)(2,1)S(1)}, bf16[3,8,8,256]{3,2,1,0:T(8,128)(2,1)S(1)}, u32[]{:S(2)}, u32[]{:S(2)}) collective-permute-start(bf16[3,8,8,256]{3,2,1,0:T(8,128)(2,1)S(1)} %get-tuple-element.53), channel_id=1, source_target_pairs={{0,4},{1,2},{2,1},{3,7},{4,0},{5,6},{6,5},{7,3},{8,12},{9,10},{10,... | collective-permute-start | bytes 294920 | tf_op jit(solution)/shard_map/ppermute | solution.py:735
  9.3 5.9 %collective-permute-start.2 = (bf16[3,8,8,256]{3,2,1,0:T(8,128)(2,1)S(1)}, bf16[3,8,8,256]{3,2,1,0:T(8,128)(2,1)S(1)}, u32[]{:S(2)}, u32[]{:S(2)}) collective-permute-start(bf16[3,8,8,256]{3,2,1,0:T(8,128)(2,1)S(1)} %get-tuple-element.49), channel_id=1, source_target_pairs={{0,1},{1,0},{2,3},{3,2},{4,5},{5,4},{6,7},{7,6},{8,9},{9,8},{10,11... | collective-permute-start | bytes 294920 | tf_op jit(solution)/shard_map/ppermute | solution.py:751
  11.7 3.6 %collective-permute-start.3 = (bf16[3,8,8,256]{3,2,1,0:T(8,128)(2,1)S(1)}, bf16[3,8,8,256]{3,2,1,0:T(8,128)(2,1)S(1)}, u32[]{:S(2)}, u32[]{:S(2)}) collective-permute-start(bf16[3,8,8,256]{3,2,1,0:T(8,128)(2,1)S(1)} %get-tuple-element.50), channel_id=1, source_target_pairs={{0,4},{1,2},{2,1},{3,7},{4,0},{5,6},{6,5},{7,3},{8,12},{9,10},{10,... | collective-permute-start | bytes 294920 | tf_op jit(solution)/shard_map/ppermute | solution.py:752

commit v6 on v5

--- a/solution.py
+++ b/solution.py
@@ -7,12 +7,17 @@
 from jax.experimental.pallas import tpu as pltpu
 from jax.sharding import PartitionSpec as P
 
+
 F32 = jnp.float32
 BF16 = jnp.bfloat16
 LANES = 128
 AXES = ("space", "frame")
 
 
+def swap(parcel, pairs):
+    return lax.ppermute(parcel, AXES, pairs)
+
+
 def swap_pairs(peers, frames):
     def at(s, t):
         return s * frames + t
@@ -20,16 +25,26 @@
     def second(i, n):
         return ((i + 1) ^ 1) - 1 if 0 < i < n - 1 else -1
 
+    idle = {at(s, t): at(s, t ^ 1) for s in (0, peers - 1) for t in range(frames)}
     space_first, space_second, frame_first, frame_second = [], [], [], []
+    thirds = [[], [], []]
     for s in range(peers):
         for t in range(frames):
             space_first.append((at(s, t), at(s ^ 1, t)))
             other = second(s, peers)
-            space_second.append((at(s, t), at(other, t) if other >= 0 else at(s, t ^ 1)))
+            space_second.append((at(s, t), at(other, t) if other >= 0 else idle[at(s, t)]))
             frame_first.append((at(s, t), at(s, t ^ 1)))
             other = second(t, frames)
             frame_second.append((at(s, t), at(s, other) if other >= 0 else at(s ^ 1, t)))
-    return space_first, space_second, frame_first, frame_second
+            for turn in range(3):
+                if t % 3 == turn and t + 1 < frames:
+                    target = at(s, t + 1)
+                elif (t + 2) % 3 == turn and t > 0:
+                    target = at(s, t - 1)
+                else:
+                    target = at(s ^ 1, t)
+                thirds[turn].append((at(s, t), target))
+    return space_first, space_second, frame_first, frame_second, thirds
 
 
 def iota(shape, dim):
@@ -307,6 +322,7 @@
     mid_ref,
     fa_ref,
     fb_ref,
+    fc_ref,
     pad_ref,
 ):
     bricks, edge, _, wide = rt_ref.shape
@@ -364,7 +380,11 @@
                 value = jnp.maximum(result(i, z) + bias, 0.0) * keep
                 for b in range(bricks):
                     mid_ref[b, z, :, tile_of(i)] = value[b * edge : (b + 1) * edge].astype(BF16)
-        choose_parcels(tables, mid_ref, fa_ref, fb_ref)
+        frame = lax.rem(lax.axis_index("frame"), 3)
+        for slot in range(tables.slots):
+            ahead, back = tables.ahead_ref[0, slot], tables.back_ref[0, slot]
+            for turn, parcel_ref in enumerate((fa_ref, fb_ref, fc_ref)):
+                parcel_ref[slot] = mid_ref[jnp.where(frame == turn, ahead, back)]
 
 
 def choose_parcels(tables, field_ref, fa_ref, fb_ref):
@@ -524,9 +544,28 @@
         choose_parcels(tables, out_ref, fa_ref, fb_ref)
 
 
-def temporal_part(tables, tiles, rt_ref, mask_ref, hid_ref, ga_ref, gb_ref, band, b, put):
+def pick_second(frame_refs):
+    ga_ref, gb_ref = frame_refs
+    odd = lax.rem(lax.axis_index("frame"), 2) == 1
+    return (
+        lambda slot: jnp.where(odd, ga_ref[slot], gb_ref[slot]),
+        lambda slot: jnp.where(odd, gb_ref[slot], ga_ref[slot]),
+    )
+
+
+def pick_third(frame_refs):
+    frame = lax.rem(lax.axis_index("frame"), 3)
+
+    def choose(slot, turn):
+        first, second, third = (ref[slot] for ref in frame_refs)
+        return jnp.where(turn == 0, first, jnp.where(turn == 1, second, third))
+
+    return (lambda slot: choose(slot, lax.rem(frame + 2, 3)), lambda slot: choose(slot, frame))
+
+
+def temporal_part(tables, tiles, rt_ref, mask_ref, hid_ref, picks, band, b, put):
     bricks, edge, _, part = hid_ref.shape
-    odd = lax.rem(lax.axis_index("frame"), 2) == 1
+    from_prior, from_later = picks
 
     def flat(block):
         return block.astype(F32).reshape(edge * edge, part)
@@ -534,8 +573,8 @@
     prior, later = tables.prior_ref[0, b], tables.later_ref[0, b]
     at_prior = jnp.clip(prior, 0, tables.slots - 1)
     at_later = jnp.clip(later, 0, tables.slots - 1)
-    before = flat(jnp.where(odd, ga_ref[at_prior], gb_ref[at_prior]))
-    after = flat(jnp.where(odd, gb_ref[at_later], ga_ref[at_later]))
+    before = flat(from_prior(at_prior))
+    after = flat(from_later(at_later))
     before = jnp.where(prior >= 0, before, 0.0).astype(BF16)
     after = jnp.where(later >= 0, after, 0.0).astype(BF16)
     here = flat(hid_ref[b]).astype(BF16)
@@ -565,6 +604,7 @@
     hid_ref,
     ga_ref,
     gb_ref,
+    gc_ref,
     w_ref,
     order_ref,
     out_ref,
@@ -589,8 +629,7 @@
             rt_ref,
             mask_ref,
             hid_ref,
-            ga_ref,
-            gb_ref,
+            pick_third((ga_ref, gb_ref, gc_ref)),
             band,
             b,
             put,
@@ -630,7 +669,15 @@
     band = band_ref[...]
     for b in range(tables.bricks):
         temporal_part(
-            tables, [0, tiles - 1], rt_ref, mask_ref, hid_ref, ga_ref, gb_ref, band, b, put
+            tables,
+            [0, tiles - 1],
+            rt_ref,
+            mask_ref,
+            hid_ref,
+            pick_second((ga_ref, gb_ref)),
+            band,
+            b,
+            put,
         )
         for k, tile in enumerate((0, tiles - 1)):
             copies.append(
@@ -675,7 +722,7 @@
     rows = bricks * edge * edge
     depth = w_spatial.shape[2]
     shape = jax.ShapeDtypeStruct
-    space_first, space_second, frame_first, frame_second = swaps
+    space_first, space_second, frame_first, frame_second, thirds = swaps
     parcel = shape((slabs * (edge + 4) * 8, 2 * LANES), BF16)
     field = shape((bricks + 1, edge, edge, wide), F32)
     arguments = (
@@ -712,7 +759,7 @@
     pad_rows = (edge + 2) * bricks * edge
     hidden = shape((bricks, edge, edge, half_wide), BF16)
     sent = shape((slots, edge, edge, half_wide), BF16)
-    rolled2, pad2, band1, band2, bias2, middle, parcel_a, parcel_b = pl.pallas_call(
+    rolled2, pad2, band1, band2, bias2, middle, *parcels = pl.pallas_call(
         inner_kernel,
         name="inner",
         out_shape=(
@@ -724,15 +771,15 @@
             hidden,
             sent,
             sent,
+            sent,
         ),
         in_specs=[VMEM] * 10,
-        out_specs=(VMEM,) * 8,
+        out_specs=(VMEM,) * 9,
         scratch_shapes=[pltpu.VMEM((3, pad_rows, wide + LANES), BF16)],
         compiler_params=pltpu.CompilerParams(vmem_limit_bytes=24 << 20),
         cost_estimate=cost(10**9, 4 * 10**6),
     )(*table, rolled, mask, w_held, b_held)
-    middle_a = lax.ppermute(parcel_a, AXES, frame_first)
-    middle_b = lax.ppermute(parcel_b, AXES, frame_second)
+    middles = [swap(parcel, turn) for parcel, turn in zip(parcels, thirds)]
 
     edges, parcel_a, parcel_b = pl.pallas_call(
         border_kernel,
@@ -748,18 +795,18 @@
         compiler_params=pltpu.CompilerParams(vmem_limit_bytes=16 << 20),
         cost_estimate=cost(5 * 10**8, 2 * 10**6),
     )(*table, rolled, mask, rolled2, pad2, band1, band2, bias2, space_a, space_b)
-    edge_a = lax.ppermute(parcel_a, AXES, frame_first)
-    edge_b = lax.ppermute(parcel_b, AXES, frame_second)
+    edge_a = swap(parcel_a, frame_first)
+    edge_b = swap(parcel_b, frame_second)
 
     middle_out, band = pl.pallas_call(
         middle_out_kernel,
         name="middle_out",
         out_shape=(hidden, shape((6 * depth, LANES), BF16)),
-        in_specs=[VMEM] * 12 + [pl.BlockSpec(memory_space=pl.ANY)],
+        in_specs=[VMEM] * 13 + [pl.BlockSpec(memory_space=pl.ANY)],
         out_specs=(VMEM, VMEM),
         compiler_params=pltpu.CompilerParams(vmem_limit_bytes=8 << 20),
         cost_estimate=cost(10**8, 10**6),
-    )(*table, rolled, mask, middle, middle_a, middle_b, wt_held, edges)
+    )(*table, rolled, mask, middle, *middles, wt_held, edges)
     return pl.pallas_call(
         edge_out_kernel,
         name="edge_out",

time: 16.4 us -> 16 us (0.976)
  starting transfers between devices: 7.25 us -> 6.78 us
    ppermute x4 -> x5, starting transfers between devices: 4.05 us -> 3.58 us  [swap(): return lax.ppermute(parcel, AXES, pairs)]
    ppermute x4 -> x5, waiting for transfers between devices: 2.89 us -> 2.88 us  [swap(): return lax.ppermute(parcel, AXES, pairs)]
  transfers between devices with their start and end apart: 6 -> 7, of which waited for: 1 -> 1; matrix products, arithmetic and copies ran while one was open for 0% -> 0% of each run, Pallas kernels for 22% -> 23%
where the time goes in v6:
time: 16 us; the launch traced here: 15.8 us
  starting transfers between devices  6.78 us (42%)
  Pallas kernels  6.11 us (38%)
  waiting for transfers between devices  2.89 us (18%)
    ppermute x5, starting transfers between devices, swap(): return lax.ppermute(parcel, AXES, pairs)  3.58 us
    ppermute x5, waiting for transfers between devices, swap(): return lax.ppermute(parcel, AXES, pairs)  2.88 us
    ppermute x1, starting transfers between devices, per_device(): space_b = lax.ppermute(parcel_b, AXES, space_second)  2.64 us
    pallas_call x1, Pallas kernels, per_device(): pl.pallas_call(inner_kernel, name='inner', out_shape=(field, shape((3, pa...  1.94 us
    pallas_call x1, Pallas kernels, per_device(): pl.pallas_call(pack_kernel, name='pack', out_shape=tuple((shape(a.shape,...  1.46 us
    pallas_call x1, Pallas kernels, per_device(): pl.pallas_call(border_kernel, name='border', out_shape=(hidden, sent, sen...  1.31 us
    pallas_call x1, Pallas kernels, per_device(): pl.pallas_call(edge_out_kernel, name='edge_out', out_shape=shape(features...  1.05 us
    ppermute x1, starting transfers between devices, per_device(): space_a = lax.ppermute(parcel_a, AXES, space_first)  0.56 us
  transfers between devices with their start and end apart: 7, of which 1 were waited for; matrix products, arithmetic and copies ran while one was open for 0% of the time, Pallas kernels for 23%

profile of v6, /device:TPU:0, one launch (start us, length us, event | category | flops | bytes accessed | tf_op | source)
XLA Modules:
  0.0 15.8 jit_solution(10873470408149958548)
XLA Ops:
  0.0 1.5 %pack.1 = (s32[1,2]{1,0:T(1,128)S(1)}, s32[1,4,6]{2,1,0:T(4,128)S(1)}, s32[1,3]{1,0:T(1,128)S(1)}, s32[1,4]{1,0:T(1,128)S(1)}, s32[1,3]{1,0:T(1,128)S(1)}, /*ind...) custom-call(s32[1,2]{1,0:T(1,128)} %refs_0_.1, ...), custom_call_target="tpu_custom_call" | custom-call | flops 100000000 | bytes 1000000 | tf_op jit(solution)/shard_map/pack/pallas_call | solution.py:741
  1.5 0.6 %collective-permute-start = (bf16[96,256]{1,0:T(8,128)(2,1)S(1)}, bf16[96,256]{1,0:T(8,128)(2,1)S(1)}, u32[]{:S(2)}, u32[]{:S(2)}) collective-permute-start(bf16[96,256]{1,0:T(8,128)(2,1)S(1)} %get-tuple-element.47), channel_id=1, source_target_pairs={{0,4},{1,5},{2,6},{3,7},{4,0},{5,1},{6,2},{7,3},{8,12},{9,13},{10,... | collective-permute-start | bytes 147464 | tf_op jit(solution)/shard_map/ppermute | solution.py:754
  2.0 2.6 %collective-permute-start.1 = (bf16[96,256]{1,0:T(8,128)(2,1)S(1)}, bf16[96,256]{1,0:T(8,128)(2,1)S(1)}, u32[]{:S(2)}, u32[]{:S(2)}) collective-permute-start(bf16[96,256]{1,0:T(8,128)(2,1)S(1)} %get-tuple-element.48), channel_id=1, source_target_pairs={{0,1},{1,0},{2,3},{3,2},{4,8},{5,9},{6,10},{7,11},{8,4},{9,5},{10,... | collective-permute-start | bytes 147464 | tf_op jit(solution)/shard_map/ppermute | solution.py:755
  4.7 1.9 %inner.1 = (f32[5,8,8,512]{3,2,1,0:T(8,128)S(1)}, bf16[3,320,384]{2,1,0:T(8,128)(2,1)S(1)}, bf16[3072,256]{1,0:T(8,128)(2,1)S(1)}, bf16[3072,256]{1,0:T(8,128)(2...) custom-call(s32[1,2]{1,0:T(1,128)S(1)} %get-tuple-element.32.refs_0_, ...), custom_call_target="tpu_custom_call" | custom-call | flops 1000000000 | bytes 4000000 | tf_op jit(solution)/shard_map/inner/pallas_call | solution.py:762
  6.6 0.1 collective-permute-start.4
  6.7 1.3 %collective-permute-start.5 = (bf16[3,8,8,256]{3,2,1,0:T(8,128)(2,1)S(1)}, bf16[3,8,8,256]{3,2,1,0:T(8,128)(2,1)S(1)}, u32[]{:S(2)}, u32[]{:S(2)}) collective-permute-start(bf16[3,8,8,256]{3,2,1,0:T(8,128)(2,1)S(1)} %get-tuple-element.54), channel_id=1, source_target_pairs={{0,4},{1,2},{2,1},{3,7},{4,0},{5,6},{6,5},{7,3},{8,12},{9,10},{10,... | collective-permute-start | bytes 294920 | tf_op jit(solution)/shard_map/ppermute | solution.py:18
  8.0 0.0 collective-permute-start.6
  8.0 0.0 collective-permute-done.refs_13_
  8.0 0.0 collective-permute-done.1.refs_14_
  8.0 1.3 %border.1 = (bf16[4,8,8,256]{3,2,1,0:T(8,128)(2,1)S(1)}, bf16[3,8,8,256]{3,2,1,0:T(8,128)(2,1)S(1)}, bf16[3,8,8,256]{3,2,1,0:T(8,128)(2,1)S(1)}) custom-call(s32[1,2]{1,0:T(1,128)S(1)} %get-tuple-element.32.refs_0_, s32[1,4,6]{2,1,0:T(4,128)S(1)} %get-tuple-element.33.refs_1_, s32[1,3]{1,0:T(1,128)S(1)} %get-tuple-element.34.refs_2_, ...), custom_call_target="tpu_custom_call" | custom-call | flops 500000000 | bytes 2000000 | tf_op jit(solution)/shard_map/border/pallas_call | solution.py:784
  9.3 2.1 %collective-permute-start.2 = (bf16[3,8,8,256]{3,2,1,0:T(8,128)(2,1)S(1)}, bf16[3,8,8,256]{3,2,1,0:T(8,128)(2,1)S(1)}, u32[]{:S(2)}, u32[]{:S(2)}) collective-permute-start(bf16[3,8,8,256]{3,2,1,0:T(8,128)(2,1)S(1)} %get-tuple-element.50), channel_id=1, source_target_pairs={{0,1},{1,0},{2,3},{3,2},{4,5},{5,4},{6,7},{7,6},{8,9},{9,8},{10,11... | collective-permute-start | bytes 294920 | tf_op jit(solution)/shard_map/ppermute | solution.py:18
  11.4 0.1 collective-permute-start.3
  11.5 0.0 collective-permute-done.4.refs_9_
  11.5 0.0 collective-permute-done.5.refs_10_
  11.5 0.0 collective-permute-done.6.refs_11_
  11.5 0.3 %middle_out.1 = (bf16[4,8,8,256]{3,2,1,0:T(8,128)(2,1)S(1)}, bf16[384,128]{1,0:T(8,128)(2,1)S(1)}) custom-call(s32[1,2]{1,0:T(1,128)S(1)} %get-tuple-element.32.refs_0_, s32[1,4,6]{2,1,0:T(4,128)S(1)} %get-tuple-element.33.refs_1_, s32[1,3]{1,0:T(1,128)S(1)} %get-tuple-element.34.refs_2_, s32[1,4]{1,0:T(1,128)S(1)} %get-tuple-element.35.refs_3_, ...), custom_call_target="tpu_custom_call" | custom-call | flops 100000000 | bytes 1000000 | tf_op jit(solution)/shard_map/middle_out/pallas_call | solution.py:801
  11.9 2.9 %collective-permute-done.2.refs_9_ = bf16[3,8,8,256]{3,2,1,0:T(8,128)(2,1)S(1)} collective-permute-done((bf16[3,8,8,256]{3,2,1,0:T(8,128)(2,1)S(1)}, bf16[3,8,8,256]{3,2,1,0:T(8,128)(2,1)S(1)}, u32[]{:S(2)}, u32[]{:S(2)}) %collective-permute-start.2) | collective-permute-done | bytes 98336 | tf_op jit(solution)/shard_map/ppermute | solution.py:18
  14.8 0.0 collective-permute-done.3.refs_10_
  14.8 1.0 %edge_out.1 = bf16[1,4,8,8,512]{4,3,2,1,0:T(8,128)(2,1)} custom-call(s32[1,2]{1,0:T(1,128)S(1)} %get-tuple-element.32.refs_0_, s32[1,4,6]{2,1,0:T(4,128)S(1)} %get-tuple-element.33.refs_1_, s32[1,3]{1,0:T(1,128)S(1)} %get-tuple-element.34.refs_2_, s32[1,4]{1,0:T(1,128)S(1)} %get-tuple-element.35.refs_3_, s32[1,3]{1,0:T(1,128)S(1)} %get-tuple-element.36.refs_4_, ...), custom_call_target="tpu_custom_call" | custom-call | flops 100000000 | bytes 1000000 | tf_op jit(solution)/shard_map/edge_out/pallas_call | solution.py:810
Async XLA Ops:
  1.5 6.5 %collective-permute-start = (bf16[96,256]{1,0:T(8,128)(2,1)S(1)}, bf16[96,256]{1,0:T(8,128)(2,1)S(1)}, u32[]{:S(2)}, u32[]{:S(2)}) collective-permute-start(bf16[96,256]{1,0:T(8,128)(2,1)S(1)} %get-tuple-element.47), channel_id=1, source_target_pairs={{0,4},{1,5},{2,6},{3,7},{4,0},{5,1},{6,2},{7,3},{8,12},{9,13},{10,... | collective-permute-start | bytes 147464 | tf_op jit(solution)/shard_map/ppermute | solution.py:754
  2.0 6.0 %collective-permute-start.1 = (bf16[96,256]{1,0:T(8,128)(2,1)S(1)}, bf16[96,256]{1,0:T(8,128)(2,1)S(1)}, u32[]{:S(2)}, u32[]{:S(2)}) collective-permute-start(bf16[96,256]{1,0:T(8,128)(2,1)S(1)} %get-tuple-element.48), channel_id=1, source_target_pairs={{0,1},{1,0},{2,3},{3,2},{4,8},{5,9},{6,10},{7,11},{8,4},{9,5},{10,... | collective-permute-start | bytes 147464 | tf_op jit(solution)/shard_map/ppermute | solution.py:755
  6.6 4.9 %collective-permute-start.4 = (bf16[3,8,8,256]{3,2,1,0:T(8,128)(2,1)S(1)}, bf16[3,8,8,256]{3,2,1,0:T(8,128)(2,1)S(1)}, u32[]{:S(2)}, u32[]{:S(2)}) collective-permute-start(bf16[3,8,8,256]{3,2,1,0:T(8,128)(2,1)S(1)} %get-tuple-element.53), channel_id=1, source_target_pairs={{0,1},{1,0},{2,6},{3,7},{4,5},{5,4},{6,2},{7,3},{8,9},{9,8},{10,14... | collective-permute-start | bytes 294920 | tf_op jit(solution)/shard_map/ppermute | solution.py:18
  6.7 4.8 %collective-permute-start.5 = (bf16[3,8,8,256]{3,2,1,0:T(8,128)(2,1)S(1)}, bf16[3,8,8,256]{3,2,1,0:T(8,128)(2,1)S(1)}, u32[]{:S(2)}, u32[]{:S(2)}) collective-permute-start(bf16[3,8,8,256]{3,2,1,0:T(8,128)(2,1)S(1)} %get-tuple-element.54), channel_id=1, source_target_pairs={{0,4},{1,2},{2,1},{3,7},{4,0},{5,6},{6,5},{7,3},{8,12},{9,10},{10,... | collective-permute-start | bytes 294920 | tf_op jit(solution)/shard_map/ppermute | solution.py:18
  8.0 3.5 %collective-permute-start.6 = (bf16[3,8,8,256]{3,2,1,0:T(8,128)(2,1)S(1)}, bf16[3,8,8,256]{3,2,1,0:T(8,128)(2,1)S(1)}, u32[]{:S(2)}, u32[]{:S(2)}) collective-permute-start(bf16[3,8,8,256]{3,2,1,0:T(8,128)(2,1)S(1)} %get-tuple-element.55), channel_id=1, source_target_pairs={{0,4},{1,5},{2,3},{3,2},{4,0},{5,1},{6,7},{7,6},{8,12},{9,13},{10,... | collective-permute-start | bytes 294920 | tf_op jit(solution)/shard_map/ppermute | solution.py:18
  9.3 5.4 %collective-permute-start.2 = (bf16[3,8,8,256]{3,2,1,0:T(8,128)(2,1)S(1)}, bf16[3,8,8,256]{3,2,1,0:T(8,128)(2,1)S(1)}, u32[]{:S(2)}, u32[]{:S(2)}) collective-permute-start(bf16[3,8,8,256]{3,2,1,0:T(8,128)(2,1)S(1)} %get-tuple-element.50), channel_id=1, source_target_pairs={{0,1},{1,0},{2,3},{3,2},{4,5},{5,4},{6,7},{7,6},{8,9},{9,8},{10,11... | collective-permute-start | bytes 294920 | tf_op jit(solution)/shard_map/ppermute | solution.py:18
  11.4 3.3 %collective-permute-start.3 = (bf16[3,8,8,256]{3,2,1,0:T(8,128)(2,1)S(1)}, bf16[3,8,8,256]{3,2,1,0:T(8,128)(2,1)S(1)}, u32[]{:S(2)}, u32[]{:S(2)}) collective-permute-start(bf16[3,8,8,256]{3,2,1,0:T(8,128)(2,1)S(1)} %get-tuple-element.51), channel_id=1, source_target_pairs={{0,4},{1,2},{2,1},{3,7},{4,0},{5,6},{6,5},{7,3},{8,12},{9,10},{10,... | collective-permute-start | bytes 294920 | tf_op jit(solution)/shard_map/ppermute | solution.py:18

commit v7 on v6

--- a/solution.py
+++ b/solution.py
@@ -563,8 +563,8 @@
     return (lambda slot: choose(slot, lax.rem(frame + 2, 3)), lambda slot: choose(slot, frame))
 
 
-def temporal_part(tables, tiles, rt_ref, mask_ref, hid_ref, picks, band, b, put):
-    bricks, edge, _, part = hid_ref.shape
+def temporal_part(tables, tiles, rt_ref, mask_ref, hid_ref, picks, band, b, put, own_ref=None):
+    bricks, edge, _, part = (hid_ref if own_ref is None else own_ref).shape
     from_prior, from_later = picks
 
     def flat(block):
@@ -577,9 +577,11 @@
     after = flat(from_later(at_later))
     before = jnp.where(prior >= 0, before, 0.0).astype(BF16)
     after = jnp.where(later >= 0, after, 0.0).astype(BF16)
-    here = flat(hid_ref[b]).astype(BF16)
+    fields = (before, after)
+    if own_ref is None:
+        fields = (before, flat(hid_ref[b]).astype(BF16), after)
     lhs = [
-        jnp.concatenate([f[:, tile_of(k)] for f in (before, here, after)], axis=1)
+        jnp.concatenate([f[:, tile_of(k)] for f in fields], axis=1)
         for k in range(len(tiles))
     ]
     total = jnp.dot(jnp.concatenate(lhs, axis=0), band, preferred_element_type=F32)
@@ -588,7 +590,11 @@
             at = (z * bricks + b) * edge
             keep = mask_ref[at : at + edge, tile_of(tile)]
             row = k * edge * edge + z * edge
-            sums = half(rt_ref[b, z, :, tile_of(tile)]) + total[row : row + edge]
+            if own_ref is None:
+                own = half(rt_ref[b, z, :, tile_of(tile)])
+            else:
+                own = own_ref[b, z, :, tile_of(k)]
+            sums = own + total[row : row + edge]
             put(b, z, k, (keep * sums).astype(BF16))
 
 
@@ -606,9 +612,10 @@
     gb_ref,
     gc_ref,
     w_ref,
-    order_ref,
+    edges_ref,
     out_ref,
     band_ref,
+    own_ref,
 ):
     depth = w_ref.shape[1]
     blank = jnp.zeros((depth, depth), BF16)
@@ -622,7 +629,17 @@
         out_ref[b, z, :, tile_of(k)] = value
 
     band = band_ref[...]
+    edge = rt_ref.shape[1]
     for b in range(tables.bricks):
+        here = edges_ref[b].astype(F32).reshape(edge * edge, 2 * LANES).astype(BF16)
+        lhs = jnp.concatenate([here[:, tile_of(0)], here[:, tile_of(1)]], axis=0)
+        total = jnp.dot(lhs, band[2 * depth : 4 * depth, :], preferred_element_type=F32)
+        for k, tile in enumerate((0, tiles - 1)):
+            for z in range(edge):
+                row = (k * edge + z) * edge
+                own_ref[b, z, :, tile_of(k)] = (
+                    half(rt_ref[b, z, :, tile_of(tile)]) + total[row : row + edge]
+                )
         temporal_part(
             tables,
             list(range(1, tiles - 1)),
@@ -643,9 +660,8 @@
 
 def edge_out_body(
     tables,
-    rt_ref,
     mask_ref,
-    hid_ref,
+    own_ref,
     ga_ref,
     gb_ref,
     band_ref,
@@ -654,7 +670,7 @@
     held_ref,
     sems,
 ):
-    tiles = rt_ref.shape[-1] // LANES
+    tiles = mask_ref.shape[-1] // LANES
     wide = tiles * LANES
     copies = [
         pltpu.make_async_copy(
@@ -666,18 +682,20 @@
     def put(b, z, k, value):
         held_ref[k, b, z] = value
 
-    band = band_ref[...]
+    third = band_ref.shape[0] // 3
+    band = jnp.concatenate([band_ref[0:third, :], band_ref[2 * third :, :]], axis=0)
     for b in range(tables.bricks):
         temporal_part(
             tables,
             [0, tiles - 1],
-            rt_ref,
+            None,
             mask_ref,
-            hid_ref,
+            None,
             pick_second((ga_ref, gb_ref)),
             band,
             b,
             put,
+            own_ref,
         )
         for k, tile in enumerate((0, tiles - 1)):
             copies.append(
@@ -798,12 +816,12 @@
     edge_a = swap(parcel_a, frame_first)
     edge_b = swap(parcel_b, frame_second)
 
-    middle_out, band = pl.pallas_call(
+    middle_out, band, own = pl.pallas_call(
         middle_out_kernel,
         name="middle_out",
-        out_shape=(hidden, shape((6 * depth, LANES), BF16)),
-        in_specs=[VMEM] * 13 + [pl.BlockSpec(memory_space=pl.ANY)],
-        out_specs=(VMEM, VMEM),
+        out_shape=(hidden, shape((6 * depth, LANES), BF16), shape(hidden.shape, F32)),
+        in_specs=[VMEM] * 14,
+        out_specs=(VMEM,) * 3,
         compiler_params=pltpu.CompilerParams(vmem_limit_bytes=8 << 20),
         cost_estimate=cost(10**8, 10**6),
     )(*table, rolled, mask, middle, *middles, wt_held, edges)
@@ -811,7 +829,7 @@
         edge_out_kernel,
         name="edge_out",
         out_shape=shape(features.shape, BF16),
-        in_specs=[VMEM] * 13,
+        in_specs=[VMEM] * 12,
         out_specs=HBM,
         scratch_shapes=[
             pltpu.VMEM((2, bricks, edge, edge, LANES), BF16),
@@ -819,7 +837,7 @@
         ],
         compiler_params=pltpu.CompilerParams(vmem_limit_bytes=8 << 20),
         cost_estimate=cost(10**8, 10**6),
-    )(*table, rolled, mask, edges, edge_a, edge_b, band, middle_out)
+    )(*table, mask, own, edge_a, edge_b, band, middle_out)
 
 
 def solution(mesh):

time: 16 us -> 15.9 us (level)
  no operation moved by 1% of the time
where the time goes in v7:
time: 15.9 us; the launch traced here: 15.8 us
  starting transfers between devices  6.78 us (43%)
  Pallas kernels  6.11 us (38%)
  waiting for transfers between devices  2.85 us (18%)
    ppermute x5, starting transfers between devices, swap(): return lax.ppermute(parcel, AXES, pairs)  3.58 us
    ppermute x5, waiting for transfers between devices, swap(): return lax.ppermute(parcel, AXES, pairs)  2.85 us
    ppermute x1, starting transfers between devices, per_device(): space_b = lax.ppermute(parcel_b, AXES, space_second)  2.64 us
    pallas_call x1, Pallas kernels, per_device(): pl.pallas_call(inner_kernel, name='inner', out_shape=(field, shape((3, pa...  1.94 us
    pallas_call x1, Pallas kernels, per_device(): pl.pallas_call(pack_kernel, name='pack', out_shape=tuple((shape(a.shape,...  1.46 us
    pallas_call x1, Pallas kernels, per_device(): pl.pallas_call(border_kernel, name='border', out_shape=(hidden, sent, sen...  1.31 us
    pallas_call x1, Pallas kernels, per_device(): pl.pallas_call(edge_out_kernel, name='edge_out', out_shape=shape(features...  1.01 us
    ppermute x1, starting transfers between devices, per_device(): space_a = lax.ppermute(parcel_a, AXES, space_first)  0.56 us
  transfers between devices with their start and end apart: 7, of which 1 were waited for; matrix products, arithmetic and copies ran while one was open for 0% of the time, Pallas kernels for 23%

profile of v7, /device:TPU:0, one launch (start us, length us, event | category | flops | bytes accessed | tf_op | source)
XLA Modules:
  0.0 15.8 jit_solution(4998098649968002570)
XLA Ops:
  0.0 1.5 %pack.1 = (s32[1,2]{1,0:T(1,128)S(1)}, s32[1,4,6]{2,1,0:T(4,128)S(1)}, s32[1,3]{1,0:T(1,128)S(1)}, s32[1,4]{1,0:T(1,128)S(1)}, s32[1,3]{1,0:T(1,128)S(1)}, /*ind...) custom-call(s32[1,2]{1,0:T(1,128)} %refs_0_.1, ...), custom_call_target="tpu_custom_call" | custom-call | flops 100000000 | bytes 1000000 | tf_op jit(solution)/shard_map/pack/pallas_call | solution.py:759
  1.5 0.6 %collective-permute-start.3 = (bf16[96,256]{1,0:T(8,128)(2,1)S(1)}, bf16[96,256]{1,0:T(8,128)(2,1)S(1)}, u32[]{:S(2)}, u32[]{:S(2)}) collective-permute-start(bf16[96,256]{1,0:T(8,128)(2,1)S(1)} %get-tuple-element.53), channel_id=1, source_target_pairs={{0,4},{1,5},{2,6},{3,7},{4,0},{5,1},{6,2},{7,3},{8,12},{9,13},{10,... | collective-permute-start | bytes 147464 | tf_op jit(solution)/shard_map/ppermute | solution.py:772
  2.0 2.6 %collective-permute-start.4 = (bf16[96,256]{1,0:T(8,128)(2,1)S(1)}, bf16[96,256]{1,0:T(8,128)(2,1)S(1)}, u32[]{:S(2)}, u32[]{:S(2)}) collective-permute-start(bf16[96,256]{1,0:T(8,128)(2,1)S(1)} %get-tuple-element.54), channel_id=1, source_target_pairs={{0,1},{1,0},{2,3},{3,2},{4,8},{5,9},{6,10},{7,11},{8,4},{9,5},{10,... | collective-permute-start | bytes 147464 | tf_op jit(solution)/shard_map/ppermute | solution.py:773
  4.7 1.9 %inner.1 = (f32[5,8,8,512]{3,2,1,0:T(8,128)S(1)}, bf16[3,320,384]{2,1,0:T(8,128)(2,1)S(1)}, bf16[3072,256]{1,0:T(8,128)(2,1)S(1)}, bf16[3072,256]{1,0:T(8,128)(2...) custom-call(s32[1,2]{1,0:T(1,128)S(1)} %get-tuple-element.33.refs_0_, ...), custom_call_target="tpu_custom_call" | custom-call | flops 1000000000 | bytes 4000000 | tf_op jit(solution)/shard_map/inner/pallas_call | solution.py:780
  6.6 0.1 collective-permute-start
  6.7 1.3 %collective-permute-start.1 = (bf16[3,8,8,256]{3,2,1,0:T(8,128)(2,1)S(1)}, bf16[3,8,8,256]{3,2,1,0:T(8,128)(2,1)S(1)}, u32[]{:S(2)}, u32[]{:S(2)}) collective-permute-start(bf16[3,8,8,256]{3,2,1,0:T(8,128)(2,1)S(1)} %get-tuple-element.45), channel_id=1, source_target_pairs={{0,4},{1,2},{2,1},{3,7},{4,0},{5,6},{6,5},{7,3},{8,12},{9,10},{10,... | collective-permute-start | bytes 294920 | tf_op jit(solution)/shard_map/ppermute | solution.py:18
  8.0 0.0 collective-permute-start.2
  8.0 0.0 collective-permute-done.3.refs_13_
  8.0 0.0 collective-permute-done.4.refs_14_
  8.0 1.3 %border.1 = (bf16[4,8,8,256]{3,2,1,0:T(8,128)(2,1)S(1)}, bf16[3,8,8,256]{3,2,1,0:T(8,128)(2,1)S(1)}, bf16[3,8,8,256]{3,2,1,0:T(8,128)(2,1)S(1)}) custom-call(s32[1,2]{1,0:T(1,128)S(1)} %get-tuple-element.33.refs_0_, s32[1,4,6]{2,1,0:T(4,128)S(1)} %get-tuple-element.34.refs_1_, s32[1,3]{1,0:T(1,128)S(1)} %get-tuple-element.35.refs_2_, ...), custom_call_target="tpu_custom_call" | custom-call | flops 500000000 | bytes 2000000 | tf_op jit(solution)/shard_map/border/pallas_call | solution.py:802
  9.3 2.1 %collective-permute-start.5 = (bf16[3,8,8,256]{3,2,1,0:T(8,128)(2,1)S(1)}, bf16[3,8,8,256]{3,2,1,0:T(8,128)(2,1)S(1)}, u32[]{:S(2)}, u32[]{:S(2)}) collective-permute-start(bf16[3,8,8,256]{3,2,1,0:T(8,128)(2,1)S(1)} %get-tuple-element.57), channel_id=1, source_target_pairs={{0,1},{1,0},{2,3},{3,2},{4,5},{5,4},{6,7},{7,6},{8,9},{9,8},{10,11... | collective-permute-start | bytes 294920 | tf_op jit(solution)/shard_map/ppermute | solution.py:18
  11.4 0.1 collective-permute-start.6
  11.5 0.0 collective-permute-done.refs_9_
  11.5 0.0 collective-permute-done.1.refs_10_
  11.5 0.0 collective-permute-done.2.refs_11_
  11.5 0.4 %middle_out.1 = (bf16[4,8,8,256]{3,2,1,0:T(8,128)(2,1)S(1)}, bf16[384,128]{1,0:T(8,128)(2,1)S(1)}, f32[4,8,8,256]{3,2,1,0:T(8,128)S(1)}) custom-call(s32[1,2]{1,0:T(1,128)S(1)} %get-tuple-element.33.refs_0_, s32[1,4,6]{2,1,0:T(4,128)S(1)} %get-tuple-element.34.refs_1_, s32[1,3]{1,0:T(1,128)S(1)} %get-tuple-element.35.refs_2_, ...), custom_call_target="tpu_custom_call" | custom-call | flops 100000000 | bytes 1000000 | tf_op jit(solution)/shard_map/middle_out/pallas_call | solution.py:819
  11.9 2.8 %collective-permute-done.5.refs_8_ = bf16[3,8,8,256]{3,2,1,0:T(8,128)(2,1)S(1)} collective-permute-done((bf16[3,8,8,256]{3,2,1,0:T(8,128)(2,1)S(1)}, bf16[3,8,8,256]{3,2,1,0:T(8,128)(2,1)S(1)}, u32[]{:S(2)}, u32[]{:S(2)}) %collective-permute-start.5) | collective-permute-done | bytes 98336 | tf_op jit(solution)/shard_map/ppermute | solution.py:18
  14.8 0.0 collective-permute-done.6.refs_9_
  14.8 1.0 %edge_out.1 = bf16[1,4,8,8,512]{4,3,2,1,0:T(8,128)(2,1)} custom-call(s32[1,2]{1,0:T(1,128)S(1)} %get-tuple-element.33.refs_0_, s32[1,4,6]{2,1,0:T(4,128)S(1)} %get-tuple-element.34.refs_1_, s32[1,3]{1,0:T(1,128)S(1)} %get-tuple-element.35.refs_2_, s32[1,4]{1,0:T(1,128)S(1)} %get-tuple-element.36.refs_3_, s32[1,3]{1,0:T(1,128)S(1)} %get-tuple-element.37.refs_4_, ...), custom_call_target="tpu_custom_call" | custom-call | flops 100000000 | bytes 1000000 | tf_op jit(solution)/shard_map/edge_out/pallas_call | solution.py:828
Async XLA Ops:
  1.5 6.5 %collective-permute-start.3 = (bf16[96,256]{1,0:T(8,128)(2,1)S(1)}, bf16[96,256]{1,0:T(8,128)(2,1)S(1)}, u32[]{:S(2)}, u32[]{:S(2)}) collective-permute-start(bf16[96,256]{1,0:T(8,128)(2,1)S(1)} %get-tuple-element.53), channel_id=1, source_target_pairs={{0,4},{1,5},{2,6},{3,7},{4,0},{5,1},{6,2},{7,3},{8,12},{9,13},{10,... | collective-permute-start | bytes 147464 | tf_op jit(solution)/shard_map/ppermute | solution.py:772
  2.0 6.0 %collective-permute-start.4 = (bf16[96,256]{1,0:T(8,128)(2,1)S(1)}, bf16[96,256]{1,0:T(8,128)(2,1)S(1)}, u32[]{:S(2)}, u32[]{:S(2)}) collective-permute-start(bf16[96,256]{1,0:T(8,128)(2,1)S(1)} %get-tuple-element.54), channel_id=1, source_target_pairs={{0,1},{1,0},{2,3},{3,2},{4,8},{5,9},{6,10},{7,11},{8,4},{9,5},{10,... | collective-permute-start | bytes 147464 | tf_op jit(solution)/shard_map/ppermute | solution.py:773
  6.6 4.9 %collective-permute-start = (bf16[3,8,8,256]{3,2,1,0:T(8,128)(2,1)S(1)}, bf16[3,8,8,256]{3,2,1,0:T(8,128)(2,1)S(1)}, u32[]{:S(2)}, u32[]{:S(2)}) collective-permute-start(bf16[3,8,8,256]{3,2,1,0:T(8,128)(2,1)S(1)} %get-tuple-element.44), channel_id=1, source_target_pairs={{0,1},{1,0},{2,6},{3,7},{4,5},{5,4},{6,2},{7,3},{8,9},{9,8},{10,14... | collective-permute-start | bytes 294920 | tf_op jit(solution)/shard_map/ppermute | solution.py:18
  6.7 4.8 %collective-permute-start.1 = (bf16[3,8,8,256]{3,2,1,0:T(8,128)(2,1)S(1)}, bf16[3,8,8,256]{3,2,1,0:T(8,128)(2,1)S(1)}, u32[]{:S(2)}, u32[]{:S(2)}) collective-permute-start(bf16[3,8,8,256]{3,2,1,0:T(8,128)(2,1)S(1)} %get-tuple-element.45), channel_id=1, source_target_pairs={{0,4},{1,2},{2,1},{3,7},{4,0},{5,6},{6,5},{7,3},{8,12},{9,10},{10,... | collective-permute-start | bytes 294920 | tf_op jit(solution)/shard_map/ppermute | solution.py:18
  8.0 3.5 %collective-permute-start.2 = (bf16[3,8,8,256]{3,2,1,0:T(8,128)(2,1)S(1)}, bf16[3,8,8,256]{3,2,1,0:T(8,128)(2,1)S(1)}, u32[]{:S(2)}, u32[]{:S(2)}) collective-permute-start(bf16[3,8,8,256]{3,2,1,0:T(8,128)(2,1)S(1)} %get-tuple-element.46), channel_id=1, source_target_pairs={{0,4},{1,5},{2,3},{3,2},{4,0},{5,1},{6,7},{7,6},{8,12},{9,13},{10,... | collective-permute-start | bytes 294920 | tf_op jit(solution)/shard_map/ppermute | solution.py:18
  9.3 5.4 %collective-permute-start.5 = (bf16[3,8,8,256]{3,2,1,0:T(8,128)(2,1)S(1)}, bf16[3,8,8,256]{3,2,1,0:T(8,128)(2,1)S(1)}, u32[]{:S(2)}, u32[]{:S(2)}) collective-permute-start(bf16[3,8,8,256]{3,2,1,0:T(8,128)(2,1)S(1)} %get-tuple-element.57), channel_id=1, source_target_pairs={{0,1},{1,0},{2,3},{3,2},{4,5},{5,4},{6,7},{7,6},{8,9},{9,8},{10,11... | collective-permute-start | bytes 294920 | tf_op jit(solution)/shard_map/ppermute | solution.py:18
  11.4 3.3 %collective-permute-start.6 = (bf16[3,8,8,256]{3,2,1,0:T(8,128)(2,1)S(1)}, bf16[3,8,8,256]{3,2,1,0:T(8,128)(2,1)S(1)}, u32[]{:S(2)}, u32[]{:S(2)}) collective-permute-start(bf16[3,8,8,256]{3,2,1,0:T(8,128)(2,1)S(1)} %get-tuple-element.58), channel_id=1, source_target_pairs={{0,4},{1,2},{2,1},{3,7},{4,0},{5,6},{6,5},{7,3},{8,12},{9,10},{10,... | collective-permute-start | bytes 294920 | tf_op jit(solution)/shard_map/ppermute | solution.py:18
